TPU v7x, 32 devices: a whole 2x2x4 slice. The times are simulated.
32 devices in a mesh: gx: 4 (over x, core), gy: 8 (over z, y).
Axes of the slice: x: 2, y: 2, z: 4, core: 2. Of those that a mesh axis runs over, the one named last changes fastest.
Arguments:
- velocity: float32 [3, 64, 128, 128], P(None, 'gx', 'gy'), may hold values from -6 to 6
- tile_cells: int32 [4, 8, 96], P('gx', 'gy'), may hold values from 0 to 255, as said below
- owner: int32 [4, 16], P('gx'), may hold values from 0 to 7, as said below
- point_slot: int32 [4, 16, 384], P('gx'), may hold values from 0 to 767
- point_z: int32 [4, 16, 384], P('gx'), may hold values from 0 to 127
- loading: float32 [4, 16, 384], P('gx'), may hold values from 0.45 to 2
Outputs:
- velocity_out: float32 [3, 64, 128, 128], P(None, 'gx', 'gy')
Inputs may be any that keep to these rules, and one draw needn't show every extreme that they name: `tile_cells`: the 96 cells of one tile are distinct. `owner`: in every column of tiles one index of gy owns exactly 6 turbines and none owns more.
All inputs are finite; a program needn't handle non-finite values.
Results may differ from a plain program's by a relative error of at most 0.0016.
Values may be sent and summed in bfloat16 or wider, within the bound.
No kernel may reach another device: no remote copies, remote signals or barrier semaphores. Data moves between devices by JAX's collectives and lax.ppermute only.
A program may use at most 256 MiB of HBM per device.

v0:
```python
import jax
import jax.numpy as jnp
from jax import lax
from jax.sharding import PartitionSpec as P

STEPS = 2


SPREAD = 0.12
CARRY = 0.25
FREE_WIND = 1.0
LOAD = 0.6


def padded_2(cells, sides, width):
    for axis, dim in sides:
        count = lax.axis_size(axis)
        ends = count - 1
        head = lax.slice_in_dim(cells, 0, width, axis=dim)
        tail = lax.slice_in_dim(cells, cells.shape[dim] - width, cells.shape[dim], axis=dim)
        cells = jnp.concatenate(
            [
                lax.ppermute(tail, axis, [(i, (i + 1) % count) for i in range(ends)]),
                cells,
                lax.ppermute(head, axis, [((i + 1) % count, i) for i in range(ends)]),
            ],
            axis=dim,
        )
    return cells


def stencil(velocity, force_cells):
    padded = padded_2(velocity, (("gx", 1), ("gy", 2)), 1)
    vert_pad = jnp.pad(velocity, ((0, 0), (0, 0), (0, 0), (1, 1)))
    beside = padded[:, 2:, 1:-1, :] + padded[:, :-2, 1:-1, :]
    beside = beside + padded[:, 1:-1, 2:, :] + padded[:, 1:-1, :-2, :]
    beside = beside + vert_pad[:, :, :, 2:] + vert_pad[:, :, :, :-2]
    laplace = beside - 6.0 * velocity
    upwind = velocity - padded[:, :-2, 1:-1, :]
    return velocity + SPREAD * laplace - CARRY * upwind + force_cells


def body(velocity, tile_cells, owner, point_slot, point_z, loading):
    groups = lax.axis_size("gy")
    my_index = lax.axis_index("gy")
    components, cells_x, cells_y, column_len = velocity.shape
    tile_rows = tile_cells[0, 0]
    row_count = tile_rows.shape[0]
    owners = owner[0]
    slot_table = point_slot[0]
    height_table = point_z[0]
    load_table = loading[0]
    turbines, points = slot_table.shape
    per_device = turbines // groups
    sort_keys = jnp.where(owners == my_index, 0, 1) * turbines + jnp.arange(
        turbines, dtype=jnp.int32
    )
    my_turbines = jnp.argsort(sort_keys)[: 3 * per_device]
    is_mine = owners[my_turbines] == my_index
    my_loading = load_table[my_turbines]
    load_total = jnp.sum(jnp.where(is_mine[:, None], my_loading, 0.0))
    owned_count = jnp.sum(is_mine.astype(jnp.float32))
    load_scale = LOAD / (load_total / (jnp.maximum(owned_count, 1.0) * points))
    my_slots = slot_table[my_turbines].reshape(-1)
    my_heights = height_table[my_turbines].reshape(-1)
    for substep in range(STEPS):
        flat_field = velocity.reshape(components, cells_x * cells_y, column_len)
        tile_values = jnp.take(flat_field, tile_rows, axis=1).astype(jnp.bfloat16)
        block_rows = lax.all_gather(tile_values, "gy", axis=1, tiled=True)
        block_len = block_rows.shape[1]
        is_inside = (my_slots >= 0) & (my_slots < block_len)
        picked = block_rows[:, jnp.clip(my_slots, 0, block_len - 1), my_heights].astype(jnp.float32)
        sampled = jnp.where(is_inside[None, :], picked, 0.0)
        point_vel = sampled.reshape(components, -1, points)
        disk_wind = FREE_WIND + jnp.mean(point_vel[0], axis=-1)
        load_coeff = -(load_scale * disk_wind)[:, None] * my_loading
        blade_push = jnp.where(is_mine[None, :, None], load_coeff[None] * point_vel, 0.0).astype(
            jnp.bfloat16
        )
        blade_push = lax.optimization_barrier(blade_push).astype(jnp.float32)
        flat_push = blade_push.reshape(components, -1).T
        spread_is_inside = (my_slots >= 0) & (my_slots < row_count * lax.axis_size("gy"))
        target = jnp.where(spread_is_inside, my_slots, row_count * lax.axis_size("gy"))
        empty = jnp.zeros((row_count * lax.axis_size("gy"), components, column_len), jnp.float32)
        force_rows = lax.psum_scatter(
            empty.at[target, :, my_heights].add(flat_push, mode="drop"),
            "gy",
            scatter_dimension=0,
            tiled=True,
        )
        force_cells = jnp.zeros((components, cells_x * cells_y, column_len), jnp.float32)
        force_cells = force_cells.at[:, tile_rows, :].add(jnp.transpose(force_rows, (1, 0, 2)))
        velocity = stencil(velocity, force_cells.reshape(velocity.shape))
    return velocity


def solution(mesh):
    in_specs = (
        P(None, "gx", "gy", None),
        P("gx", "gy", None),
        P("gx", None),
        P("gx", None, None),
        P("gx", None, None),
        P("gx", None, None),
    )
    out_specs = P(None, "gx", "gy", None)
    return jax.shard_map(body, mesh=mesh, in_specs=in_specs, out_specs=out_specs, check_vma=False)
```

profile of v0, /device:TPU:0, one launch (start us, length us, event | category | flops | bytes accessed | tf_op | source)
XLA Modules:
  0.0 481.6 jit_solution(17093859298049288880)
XLA Ops:
  8.5 1.2 sort.17
  10.4 1.3 gather_fusion.1
  11.7 1.3 copy.29
  13.8 33.2 %all_gather.6 = bf16[3,768,128]{2,1,0:T(8,128)(2,1)S(1)} all-gather(bf16[3,96,128]{2,1,0:T(8,128)(2,1)S(1)} %bitcast_convert_fusion.1), channel_id=1, replica_groups=mesh['gx'=4,'gy'=8] {'gy'}, dimensions={1}, use_global_device_ids=true | all-gather | bytes 663552 | tf_op jit(solution)/shard_map/all_gather | solution.py:69
  47.0 16.1 %copy.31 = bf16[3,768,128]{0,2,1:T(8,128)(2,1)} copy(bf16[3,768,128]{2,1,0:T(8,128)(2,1)S(1)} %all_gather.6) | data formatting | bytes 1179648 | tf_op jit(solution)/shard_map/all_gather | solution.py:69
  63.3 20.9 %gather_fusion.4 = bf16[2304,3]{1,0:T(8,128)(2,1)S(1)} fusion(bf16[3,768,128]{0,2,1:T(8,128)(2,1)} %copy.31, s32[2304]{0:T(1024)S(1)} %get-tuple-element.22), kind=kCustom, calls=%fused_computation.6 | custom fusion | bytes 46080 | tf_op jit(solution)/shard_map/gather | solution.py:72
  84.4 1.6 fusion.5
  91.3 33.2 %scatter_custom_fusion.2 = f32[3,98304]{0,1:T(8,128)} fusion(s32[2304]{0:T(1024)S(1)} %broadcast_select_fusion, f32[]{:T(128)} %constant.23.clone.1, bf16[3,2304]{0,1:T(8,128)(2,1)S(1)} %bitcast.62), kind=kCustom, calls=%fused_computation.14 | custom fusion | flops 13824 | bytes 1769476
  124.5 26.7 %copy.32 = f32[3,768,128]{2,0,1:T(4,128)} copy(f32[3,768,128]{0,2,1:T(8,128)} %bitcast.55) | data formatting | bytes 2359296
  151.3 0.9 copy-done.3
  152.2 1.3 collective-permute-start.1
  153.5 1.3 collective-permute-start
  156.1 2.2 collective-permute-done
  158.4 1.3 collective-permute-start.2
  159.7 4.5 collective-permute-start.3
  164.2 77.8 %all-reduce.7.cloned.1.call-done = f32[768,3,128]{2,1,0:T(4,128)} async-done(((f32[768,3,128]{2,1,0:T(4,128)}), f32[768,3,128]{2,1,0:T(4,128)}) %all-reduce.7.cloned.1.call-update) | async-done | bytes 1179664
  242.0 1.0 constant_dynamic-slice_fusion.1
  243.0 3.8 scatter_fusion
  248.3 31.6 %all_gather.7 = bf16[3,768,128]{2,1,0:T(8,128)(2,1)S(1)} all-gather(bf16[3,96,128]{2,1,0:T(8,128)(2,1)S(1)} %bitcast_convert_fusion), channel_id=1, replica_groups=mesh['gx'=4,'gy'=8] {'gy'}, dimensions={1}, use_global_device_ids=true | all-gather | bytes 663552 | tf_op jit(solution)/shard_map/all_gather | solution.py:69
  279.9 16.1 %copy.36 = bf16[3,768,128]{0,2,1:T(8,128)(2,1)} copy(bf16[3,768,128]{2,1,0:T(8,128)(2,1)S(1)} %all_gather.7) | data formatting | bytes 1179648 | tf_op jit(solution)/shard_map/all_gather | solution.py:69
  296.1 20.9 %gather_fusion.5 = bf16[2304,3]{1,0:T(8,128)(2,1)S(1)} fusion(bf16[3,768,128]{0,2,1:T(8,128)(2,1)} %copy.36, s32[2304]{0:T(1024)S(1)} %get-tuple-element.22), kind=kCustom, calls=%fused_computation.7 | custom fusion | bytes 46080 | tf_op jit(solution)/shard_map/gather | solution.py:72
  317.1 1.6 fusion.4
  319.8 33.2 %scatter_custom_fusion.3 = f32[3,98304]{0,1:T(8,128)} fusion(s32[2304]{0:T(1024)S(1)} %broadcast_select_fusion, f32[]{:T(128)} %constant.23.clone.1, bf16[3,2304]{0,1:T(8,128)(2,1)S(1)} %bitcast.63), kind=kCustom, calls=%fused_computation.12 | custom fusion | flops 13824 | bytes 1769476
  353.1 26.7 %copy.37 = f32[3,768,128]{2,0,1:T(4,128)} copy(f32[3,768,128]{0,2,1:T(8,128)} %bitcast.54) | data formatting | bytes 2359296
  379.8 1.3 collective-permute-start.4
  381.1 3.0 collective-permute-start.5
  385.0 1.3 collective-permute-start.6
  386.3 4.5 collective-permute-start.7
  390.8 77.9 %all-reduce.9.cloned.1.call-done = f32[768,3,128]{2,1,0:T(4,128)} async-done(((f32[768,3,128]{2,1,0:T(4,128)}), f32[768,3,128]{2,1,0:T(4,128)}) %all-reduce.9.cloned.1.call-update) | async-done | bytes 1179664
  468.8 1.0 constant_dynamic-slice_fusion
  469.8 3.8 scatter_fusion.1
  473.7 1.1 fusion.19
  (76 shorter events, 11.9 us)
Async XLA Ops:
  6.5 3.3 copy-start
  6.5 235.4 %all-reduce.7.cloned.1.call-start = ((), (), s32[]{:S(2)}) async-start(), calls=%async_computation | async-start | bytes 3145728
  84.3 1.7 copy-start.2
  84.3 3.0 copy-start.4
  86.0 5.1 %copy-start.5 = (s32[2]{0:T(128)S(1)}, s32[2]{0:T(128)}, u32[]{:S(2)}) copy-start(s32[2]{0:T(128)} %constant.64) | copy-start | bytes 28
  86.0 5.2 %copy-start.6 = (s32[2]{0:T(128)S(1)}, s32[2]{0:T(128)}, u32[]{:S(2)}) copy-start(s32[2]{0:T(128)} %constant.67) | copy-start | bytes 28
  151.2 1.0 copy-start.3
  151.2 3.6 copy-start.7
  151.2 3.6 copy-start.8
  151.2 317.5 %all-reduce.9.cloned.1.call-start = ((), (), s32[]{:S(2)}) async-start(), calls=%async_computation.1 | async-start | bytes 3145728
  152.2 3.9 collective-permute-start.1
  153.5 4.8 %collective-permute-start = (f32[3,1,16,128]{3,2,1,0:T(8,128)S(1)}, f32[3,1,16,128]{3,2,1,0:T(8,128)S(1)}, u32[]{:S(2)}, u32[]{:S(2)}) collective-permute-start(f32[3,1,16,128]{3,2,1,0:T(8,128)S(1)} %get-tuple-element.20), channel_id=1, source_target_pairs={{8,0},{16,8},{24,16},{9,1},{17,9},{25,17},{10,2},{18,10},{26,18},{... | collective-permute-start | bytes 73736 | tf_op jit(solution)/shard_map/ppermute | solution.py:25
  158.4 88.5 %collective-permute-start.2 = (f32[3,18,1,128]{3,2,1,0:T(1,128)S(1)}, f32[3,18,1,128]{3,2,1,0:T(1,128)S(1)}, u32[]{:S(2)}, u32[]{:S(2)}) collective-permute-start(f32[3,18,1,128]{3,2,1,0:T(1,128)S(1)} %get-tuple-element.16), channel_id=1, source_target_pairs={{1,0},{2,1},{3,2},{4,3},{5,4},{6,5},{7,6},{9,8},{10,9},{11,10},{12... | collective-permute-start | bytes 82952 | tf_op jit(solution)/shard_map/ppermute | solution.py:25
  159.7 87.2 %collective-permute-start.3 = (f32[3,18,1,128]{3,2,1,0:T(1,128)S(1)}, f32[3,18,1,128]{3,2,1,0:T(1,128)S(1)}, u32[]{:S(2)}, u32[]{:S(2)}) collective-permute-start(f32[3,18,1,128]{3,2,1,0:T(1,128)S(1)} %get-tuple-element.17), channel_id=1, source_target_pairs={{0,1},{1,2},{2,3},{3,4},{4,5},{5,6},{6,7},{8,9},{9,10},{10,11},{11... | collective-permute-start | bytes 82952 | tf_op jit(solution)/shard_map/ppermute | solution.py:23
  379.8 4.3 collective-permute-start.4
  381.1 3.9 collective-permute-start.5
  385.0 88.7 %collective-permute-start.6 = (f32[3,18,1,128]{3,2,1,0:T(1,128)S(1)}, f32[3,18,1,128]{3,2,1,0:T(1,128)S(1)}, u32[]{:S(2)}, u32[]{:S(2)}) collective-permute-start(f32[3,18,1,128]{3,2,1,0:T(1,128)S(1)} %get-tuple-element.14), channel_id=1, source_target_pairs={{1,0},{2,1},{3,2},{4,3},{5,4},{6,5},{7,6},{9,8},{10,9},{11,10},{12... | collective-permute-start | bytes 82952 | tf_op jit(solution)/shard_map/ppermute | solution.py:25
  386.3 87.4 %collective-permute-start.7 = (f32[3,18,1,128]{3,2,1,0:T(1,128)S(1)}, f32[3,18,1,128]{3,2,1,0:T(1,128)S(1)}, u32[]{:S(2)}, u32[]{:S(2)}) collective-permute-start(f32[3,18,1,128]{3,2,1,0:T(1,128)S(1)} %get-tuple-element.15), channel_id=1, source_target_pairs={{0,1},{1,2},{2,3},{3,4},{4,5},{5,6},{6,7},{8,9},{9,10},{10,11},{11... | collective-permute-start | bytes 82952 | tf_op jit(solution)/shard_map/ppermute | solution.py:23
  468.8 6.0 %copy-start.1 = (s32[1,16,384]{2,1,0:T(8,128)S(1)}, s32[1,16,384]{2,1,0:T(8,128)}, u32[]{:S(2)}) copy-start(s32[1,16,384]{2,1,0:T(8,128)} %param.11) | copy-start | bytes 73732
Sparse Core Ops, SparseCore 0:
  151.3 90.5 all-reduce.6
  379.9 88.8 all-reduce.8
where the time goes:
time: 483 us; the launch traced here: 482 us
  waiting for transfers between devices  159 us (33%)
  local copies, waits for them, and re-layouts  137 us (28%)
  other arithmetic  86.4 us (18%)
  blocking collectives  64.8 us (13%)
  starting transfers between devices  18.6 us (4%)
  between operations  15.9 us (3%)
    unnamed x4, waiting for transfers between devices  156 us
    unnamed x5, other arithmetic  66.7 us
    all_gather x2, blocking collectives, body(): block_rows = lax.all_gather(tile_values, 'gy', axis=1, tiled=True)  64.8 us
    unnamed x28, local copies, waits for them, and re-layouts  58.1 us
    gather x2, local copies, waits for them, and re-layouts, body(): block_rows[:, jnp.clip(my_slots, 0, block_len - 1), my_heights]  41.8 us
    all_gather x2, local copies, waits for them, and re-layouts, body(): block_rows = lax.all_gather(tile_values, 'gy', axis=1, tiled=True)  32.3 us
    ppermute x4, starting transfers between devices, padded_2(): lax.ppermute(tail, axis, [(i, (i + 1) % count) for i in range(ends)])  13.4 us
  transfers between devices with their start and end apart: 10, of which 4 were waited for; matrix products, arithmetic and copies ran while one was open for 2% of the time, Pallas kernels for 0%

commit v1 on v0

v1 whole, which is shorter than its diff:
```python
import jax
import jax.numpy as jnp
from jax import lax
from jax.experimental import pallas as pl
from jax.experimental.pallas import tpu as pltpu
from jax.sharding import PartitionSpec as P

SPREAD = 0.12
CARRY = 0.25
FREE_WIND = 1.0
LOAD = 0.6

F32 = jnp.float32
BF16 = jnp.bfloat16
NT = (((1,), (1,)), ((), ()))
LANES = 128
OWN = 8
PLANE = 32
EDGE = 24


def iota(shape, axis):
    return lax.broadcasted_iota(jnp.int32, shape, axis)


def rounded(x):
    return x.astype(BF16).astype(F32)


def even(axis):
    return lax.rem(lax.axis_index(axis), 2) == 0


def swap_pairs(count, first):
    pairs = []
    for i in range(first, count - 1, 2):
        pairs += [(i, i + 1), (i + 1, i)]
    return pairs


def swap(x, axis, first):
    return lax.ppermute(x, axis, swap_pairs(lax.axis_size(axis), first))


def call(kernel, name, outs, args, scratch=(), flops=0, nbytes=0):
    return pl.pallas_call(
        kernel,
        out_shape=[jax.ShapeDtypeStruct(s, d) for s, d in outs],
        in_specs=[pl.BlockSpec(memory_space=pltpu.VMEM)] * len(args),
        out_specs=[pl.BlockSpec(memory_space=pltpu.VMEM)] * len(outs),
        scratch_shapes=list(scratch),
        compiler_params=pltpu.CompilerParams(vmem_limit_bytes=40 << 20),
        cost_estimate=pl.CostEstimate(flops=flops, bytes_accessed=nbytes, transcendentals=0),
        name=name,
    )(*args)


def lane_edge(center):
    lane = iota(center.shape, 2)
    last = center.shape[2] - 1
    below = jnp.where(lane == 0, 0.0, pltpu.roll(center, 1, 2))
    above = jnp.where(lane == last, 0.0, pltpu.roll(center, last, 2))
    return below + above


def stencil(ref, c, x0, nx, r0, nr):
    center = ref[c, x0 : x0 + nx, r0 : r0 + nr, :]
    before = ref[c, x0 - 1 : x0 - 1 + nx, r0 : r0 + nr, :]
    after = ref[c, x0 + 1 : x0 + 1 + nx, r0 : r0 + nr, :]
    beside = before + after
    beside = beside + ref[c, x0 : x0 + nx, r0 - 1 : r0 - 1 + nr, :]
    beside = beside + ref[c, x0 : x0 + nx, r0 + 1 : r0 + 1 + nr, :]
    beside = beside + lane_edge(center)
    return center + SPREAD * (beside - 6.0 * center) - CARRY * (center - before)


def pack_y(v, tc, to_even, to_odd):
    comps, nx, ny, _ = v.shape
    ev = even("gy")
    at = 0
    for c in range(comps):
        for k in range(2):
            high = v[c, :, ny - 2 + k, :]
            low = v[c, :, k, :]
            to_even[at : at + nx, :] = jnp.where(ev, high, low)
            to_odd[at : at + nx, :] = jnp.where(ev, low, high)
            at += nx
    cells = tc[0, :, :].astype(F32) + 1.0
    slots = cells.shape[1]
    for out in (to_even, to_odd):
        out[at : at + 8, :] = jnp.zeros((8, LANES), F32)
        out[at : at + 1, 0:slots] = cells


def histogram(v, tc, owner, slot, height, load, count_ref, load_ref, sum_ref, scale_ref, code_ref):
    turbines, points = slot.shape[1:]
    cells, levels = count_ref.shape[1:]
    slots = tc.shape[2]
    first = lax.axis_index("gy") * slots
    cell_row = jnp.broadcast_to((tc[0, :, :].astype(F32) + 1.0).astype(BF16), (8, slots))
    rows = rounded(v[0, :, :, :].reshape(cells, levels))

    def one(t, carry):
        which = slot[0, pl.ds(t, 1), :] - first
        z = height[0, pl.ds(t, 1), :]
        weight = load[0, pl.ds(t, 1), :]
        hit = jnp.where(iota((slots, points), 0) == which, 1.0, 0.0).astype(BF16)
        cell = jnp.dot(cell_row, hit, preferred_element_type=F32)[0:1, :].astype(jnp.int32) - 1
        code_ref[pl.ds(t, 1), :] = jnp.where(cell >= 0, cell * levels + z + 1, 0).astype(F32)
        a = jnp.where(iota((cells, points), 0) == cell, 1.0, 0.0).astype(BF16)
        at_z = iota((levels, points), 0) == z
        high = rounded(weight)
        b = jnp.concatenate(
            [
                jnp.where(at_z, 1.0, 0.0).astype(BF16),
                jnp.where(at_z, high, 0.0).astype(BF16),
                jnp.where(at_z, weight - high, 0.0).astype(BF16),
            ],
            axis=0,
        )
        both = lax.dot_general(a, b, NT, preferred_element_type=F32)
        count = both[:, :levels]
        count_ref[t] = count.astype(BF16)
        load_ref[t] = both[:, levels : 2 * levels] + both[:, 2 * levels :]
        sum_ref[pl.ds(t, 1), :] = jnp.sum(count * rows, axis=0, keepdims=True)
        return carry

    lax.fori_loop(0, turbines, one, 0, unroll=2)
    same = iota((turbines, turbines), 0) == iota((turbines, turbines), 1)
    owner_row = jnp.broadcast_to(owner[...].astype(F32), (turbines, turbines))
    owner_col = jnp.sum(jnp.where(same, owner_row, 0.0), axis=1, keepdims=True)
    member = owner_row == owner_col
    load_col = jnp.sum(load[0, :, :], axis=1, keepdims=True)
    load_row = jnp.sum(jnp.where(same, load_col, 0.0), axis=0, keepdims=True)
    total = jnp.sum(jnp.where(member, load_row, 0.0), axis=1, keepdims=True)
    number = jnp.sum(jnp.where(member, 1.0, 0.0), axis=1, keepdims=True)
    scale_ref[...] = jnp.broadcast_to(LOAD / (total / (number * points)), scale_ref.shape)


def pack_x(v, ye, yo, sums, scale, code, load, to_even, to_odd):
    comps, nx, ny, _ = v.shape
    turbines, points = code.shape
    ev_x, ev_y = even("gx"), even("gy")
    at = 0
    for c in range(comps):
        for k in range(2):
            low_at, high_at = (c * 2 + 1) * nx, (c * 2) * nx
            sides = []
            for x in (nx - 2 + k, k):
                below = jnp.where(ev_y, yo[low_at + x : low_at + x + 1, :], ye[low_at + x : low_at + x + 1, :])
                above = jnp.where(ev_y, ye[high_at + x : high_at + x + 1, :], yo[high_at + x : high_at + x + 1, :])
                sides.append((v[c, x, :, :], below, above))
            (own_r, below_r, above_r), (own_l, below_l, above_l) = sides
            for out, pick in ((to_even, ev_x), (to_odd, jnp.logical_not(ev_x))):
                out[at : at + EDGE, :] = jnp.zeros((EDGE, LANES), F32)
                out[at + 4 : at + 4 + ny, :] = jnp.where(pick, own_r, own_l)
                out[at + 3 : at + 4, :] = jnp.where(pick, below_r, below_l)
                out[at + 4 + ny : at + 5 + ny, :] = jnp.where(pick, above_r, above_l)
            at += EDGE
    parts = [code[:, k : k + LANES] for k in range(0, points, LANES)]
    parts += [load[0, :, k : k + LANES] for k in range(0, points, LANES)]
    parts += [sums[...], scale[...]]
    for part in parts:
        to_even[at : at + turbines, :] = part
        to_odd[at : at + turbines, :] = part
        at += turbines


def picked(flag, a, b, lo, hi):
    return jnp.where(flag, a[lo:hi, :], b[lo:hi, :])


def extend(v, ye, yo, xe, xo, field, comps):
    _, nx, ny, _ = v.shape
    ev_x, ev_y = even("gx"), even("gy")
    for c in comps:
        out = c if len(comps) > 1 else 0
        field[out, 2 : 2 + nx, 0:OWN, :] = jnp.zeros((nx, OWN, LANES), F32)
        field[out, 2 : 2 + nx, OWN + ny : PLANE, :] = jnp.zeros((nx, PLANE - OWN - ny, LANES), F32)
        field[out, 2 : 2 + nx, OWN : OWN + ny, :] = v[c, :, :, :]
        for k in range(2):
            at = (c * 2 + k) * nx
            field[out, 2 : 2 + nx, OWN - 2 + k, :] = picked(ev_y, yo, ye, at, at + nx)
            field[out, 2 : 2 + nx, OWN + ny + k, :] = picked(ev_y, ye, yo, at, at + nx)
            at = (c * 2 + k) * EDGE
            for x, a, b in ((k, xo, xe), (2 + nx + k, xe, xo)):
                field[out, x, 0:OWN, :] = jnp.zeros((OWN, LANES), F32)
                field[out, x, PLANE - OWN : PLANE, :] = jnp.zeros((OWN, LANES), F32)
                field[out, x, 4 : 4 + EDGE, :] = picked(ev_x, a, b, at, at + EDGE)


def reduce_sums(v, ye, yo, xe, xo, counts, loads, sums, out, field, products):
    comps, nx, ny, levels = v.shape
    turbines, cells, _ = counts.shape
    extend(v, ye, yo, xe, xo, field, (0,))
    update = stencil(field, 0, 2, nx, OWN, ny).reshape(cells, levels)
    rows = rounded(v[0, :, :, :].reshape(cells, levels))
    for t in range(turbines):
        products[t] = (rows * loads[t]).astype(BF16)
    products[turbines] = update.astype(BF16)
    block = 16
    wide, more = turbines * block, (turbines + 1) * block
    gram = jnp.zeros((wide, more), F32)
    for b in range(0, cells, block):
        left = counts[:, b : b + block, :].reshape(wide, levels)
        right = products[:, b : b + block, :].reshape(more, levels)
        gram = gram + lax.dot_general(left, right, NT, preferred_element_type=F32)
    keep = (iota((wide, more), 0) & (block - 1)) == (iota((wide, more), 1) & (block - 1))
    gram = jnp.sum(jnp.where(keep, gram, 0.0).reshape(turbines, block, more), axis=1)
    select = jnp.where(iota((more, LANES), 0) // block == iota((more, LANES), 1), 1.0, 0.0)
    result = jnp.dot(gram, select, precision=lax.Precision.HIGHEST, preferred_element_type=F32)
    lane = iota((turbines, LANES), 1)
    ev_x = even("gx")
    at = xe.shape[0] - 2 * turbines
    left_sums = picked(ev_x, xo, xe, at, at + turbines)
    right_sums = picked(ev_x, xe, xo, at, at + turbines)
    for k, part in enumerate((sums[...], left_sums, right_sums)):
        result = jnp.where(lane == turbines + 1 + k, jnp.sum(part, axis=1, keepdims=True), result)
    for k in range(out.shape[0]):
        out[k] = result


def edges(slots, v, slot, height, load, ye, yo, xe, xo, edge_ref, update_ref, field):
    comps, nx, ny, levels = v.shape
    turbines, points = slot.shape[1:]
    shift, level_shift = ny.bit_length() - 1, levels.bit_length() - 1
    ev_x, ev_y = even("gx"), even("gy")
    me = lax.axis_index("gy")
    extend(v, ye, yo, xe, xo, field, tuple(range(comps)))
    for c in range(comps):
        update_ref[c, :, OWN - 1 : OWN + ny + 1, :] = stencil(field, c, 1, nx + 2, OWN - 1, ny + 2)

    at = comps * 2 * nx
    columns = []
    for a, b, row in ((yo, ye, ny - 1), (ye, yo, 0)):
        cell = picked(ev_y, a, b, at, at + 1)[:, :slots].astype(jnp.int32) - 1
        valid = (cell >= 0) & ((cell & (ny - 1)) == row)
        x = jnp.where(valid, (cell >> shift) + 1, 0).astype(F32).astype(BF16)
        columns.append(jnp.broadcast_to(x, (8, slots)))

    pieces = points // LANES
    code_at = comps * 2 * EDGE
    load_at = code_at + pieces * turbines

    def row_of(flag, a, b, base, t):
        rows = [pl.ds(base + k * turbines + t, 1) for k in range(pieces)]
        return jnp.concatenate([jnp.where(flag, a[r, :], b[r, :]) for r in rows], axis=1)

    def spread(where, count, z, weight):
        high = rounded(weight)
        low = weight - high
        at_z = jnp.where(iota((levels, points), 0) == z, 1.0, 0.0).astype(BF16)
        left = []
        for place in where:
            hit = iota((count, points), 0) == place
            left += [jnp.where(hit, high, 0.0).astype(BF16), jnp.where(hit, low, 0.0).astype(BF16)]
        both = lax.dot_general(jnp.concatenate(left, axis=0), at_z, NT, preferred_element_type=F32)
        return [both[2 * k * count : (2 * k + 1) * count] + both[(2 * k + 1) * count : (2 * k + 2) * count] for k in range(len(where))]

    def one(t, carry):
        z = height[0, pl.ds(t, 1), :]
        weight = load[0, pl.ds(t, 1), :]
        where = []
        for k, x in enumerate(columns):
            which = slot[0, pl.ds(t, 1), :] - (me + 2 * k - 1) * slots
            hit = jnp.where(iota((slots, points), 0) == which, 1.0, 0.0).astype(BF16)
            where.append(jnp.dot(x, hit, preferred_element_type=F32)[0:1, :].astype(jnp.int32) - 1)
        edge_ref[2, t], edge_ref[3, t] = spread(where, nx, z, weight)
        for k, (a, b) in enumerate(((xo, xe), (xe, xo))):
            code = row_of(ev_x, a, b, code_at, t).astype(jnp.int32) - 1
            there = row_of(ev_x, a, b, load_at, t)
            place = (code >> level_shift) - (1 - k) * (nx - 1) * ny
            (edge_ref[k, t],) = spread([place], ny, code & (levels - 1), there)
        return carry

    lax.fori_loop(0, turbines, one, 0, unroll=2)


def advance(points, got, v, ye, yo, xe, xo, scale, loads, edge_ref, update_ref, out, field, weights):
    comps, nx, ny, _ = v.shape
    turbines = scale.shape[0]
    ev_x, ev_y = even("gx"), even("gy")
    total = got[0]
    for k in range(1, got.shape[0]):
        total = total + got[k]
    lane = iota((turbines, LANES), 1)

    def column(k):
        return jnp.sum(jnp.where(lane == k, total, 0.0), axis=1, keepdims=True)

    def coefs(scales, sums):
        return -(scales * (FREE_WIND + sums / points))

    scale_at = xe.shape[0] - turbines
    own = coefs(scale[...], column(turbines + 1))
    left = coefs(picked(ev_x, xo, xe, scale_at, scale_at + turbines), column(turbines + 2))
    right = coefs(picked(ev_x, xe, xo, scale_at, scale_at + turbines), column(turbines + 3))
    as_row = jnp.sum(jnp.where(iota((turbines, LANES), 0) == lane, own, 0.0), axis=0, keepdims=True)
    forced = jnp.sum(jnp.where(lane < turbines, total * as_row, 0.0), axis=1, keepdims=True)
    later = coefs(scale[...], column(turbines) + forced)

    for x in range(nx):
        first = jnp.zeros((ny, LANES), F32)
        second = first
        for t in range(turbines):
            part = loads[t, x * ny : (x + 1) * ny, :]
            first = first + own[t : t + 1, :] * part
            second = second + later[t : t + 1, :] * part
        weights[x] = second
        for c in range(comps):
            push = rounded(rounded(v[c, x, :, :]) * first)
            field[c, 1 + x, OWN : OWN + ny, :] = update_ref[c, 1 + x, OWN : OWN + ny, :] + push

    sums = []
    for k, coef in enumerate((left, right, own, own)):
        side = coef[0:1, :] * edge_ref[k, 0]
        for t in range(1, turbines):
            side = side + coef[t : t + 1, :] * edge_ref[k, t]
        sums.append(side)
    ix, iy = lax.axis_index("gx"), lax.axis_index("gy")
    for c in range(comps):
        for k, (a, b, there) in enumerate(((xo, xe, ix > 0), (xe, xo, ix < lax.axis_size("gx") - 1))):
            at = (c * 2 + 1 - k) * EDGE + 4
            x = k * (nx + 1)
            push = rounded(rounded(picked(ev_x, a, b, at, at + ny)) * sums[k])
            moved = update_ref[c, x, OWN : OWN + ny, :] + push
            field[c, x, OWN : OWN + ny, :] = jnp.where(there, moved, 0.0)
        for k, (a, b, there) in enumerate(((yo, ye, iy > 0), (ye, yo, iy < lax.axis_size("gy") - 1))):
            at = (c * 2 + 1 - k) * nx
            y = OWN - 1 + k * (ny + 1)
            push = rounded(rounded(picked(ev_y, a, b, at, at + nx)) * sums[2 + k])
            moved = update_ref[c, 1 : 1 + nx, y, :] + push
            field[c, 1 : 1 + nx, y, :] = jnp.where(there, moved, 0.0)
    for c in range(comps):
        now = field[c, 1 : 1 + nx, OWN : OWN + ny, :]
        out[c] = stencil(field, c, 1, nx, OWN, ny) + rounded(rounded(now) * weights[...])


def body(velocity, tile_cells, owner, point_slot, point_z, loading):
    comps, nx, ny, levels = velocity.shape
    turbines, points = point_slot.shape[1:]
    slots = tile_cells.shape[2]
    cells = nx * ny
    tiles_y = lax.axis_size("gy")
    rows_y = comps * 2 * nx + 8
    rows_x = comps * 2 * EDGE + 2 * (points // LANES) * turbines + 2 * turbines

    def field(n, planes):
        return pltpu.VMEM((n, planes, PLANE, levels), F32)

    y_even, y_odd = call(pack_y, "pack_y", [((rows_y, levels), F32)] * 2, (velocity, tile_cells))
    ye, yo = swap(y_even, "gy", 0), swap(y_odd, "gy", 1)
    counts, loads, sums, scale, code = call(
        histogram,
        "histogram",
        [
            ((turbines, cells, levels), BF16),
            ((turbines, cells, levels), F32),
            ((turbines, levels), F32),
            ((turbines, levels), F32),
            ((turbines, points), F32),
        ],
        (velocity, tile_cells, owner, point_slot, point_z, loading),
        flops=6 * turbines * cells * points * levels,
        nbytes=4 << 20,
    )
    x_even, x_odd = call(
        pack_x, "pack_x", [((rows_x, levels), F32)] * 2, (velocity, ye, yo, sums, scale, code, loading)
    )
    xe, xo = swap(x_even, "gx", 0), swap(x_odd, "gx", 1)
    (chunk,) = call(
        reduce_sums,
        "reduce_sums",
        [((tiles_y, turbines, LANES), F32)],
        (velocity, ye, yo, xe, xo, counts, loads, sums),
        [field(1, nx + 4), pltpu.VMEM((turbines + 1, cells, levels), BF16)],
    )
    got = lax.all_to_all(chunk, "gy", 0, 0)

    def edges_of(*args):
        return edges(slots, *args)

    edge, update = call(
        edges_of,
        "edges",
        [((4, turbines, nx, levels), F32), ((comps, nx + 2, PLANE, levels), F32)],
        (velocity, point_slot, point_z, loading, ye, yo, xe, xo),
        [field(comps, nx + 4)],
        flops=6 * turbines * cells * points * levels,
        nbytes=4 << 20,
    )

    def advance_by(*args):
        return advance(points, *args)

    (out,) = call(
        advance_by,
        "advance",
        [(velocity.shape, F32)],
        (got, velocity, ye, yo, xe, xo, scale, loads, edge, update),
        [field(comps, nx + 2), pltpu.VMEM((nx, ny, levels), F32)],
    )
    return out


def solution(mesh):
    in_specs = (
        P(None, "gx", "gy", None),
        P("gx", "gy", None),
        P("gx", None),
        P("gx", None, None),
        P("gx", None, None),
        P("gx", None, None),
    )
    out_specs = P(None, "gx", "gy", None)
    return jax.shard_map(body, mesh=mesh, in_specs=in_specs, out_specs=out_specs, check_vma=False)
```

time: 483 us -> 47 us (0.10)
  the two profiles are of different devices: /device:TPU:0 before, /device:TPU:1 now
where the time goes in v1:
time: 47 us; the launch traced here: 46 us
  Pallas kernels  14.8 us (31%)
  starting transfers between devices  14.3 us (30%)
  local copies, waits for them, and re-layouts  13.6 us (29%)
  waiting for transfers between devices  3.21 us (7%)
    pallas_call x6, Pallas kernels, call(): pl.pallas_call(kernel, out_shape=[jax.ShapeDtypeStruct(s, d) for s, d in...  14.8 us
    unnamed x42, local copies, waits for them, and re-layouts  13.6 us
    all_to_all x1, starting transfers between devices, body(): got = lax.all_to_all(chunk, 'gy', 0, 0)  7.3 us
    ppermute x4, starting transfers between devices, swap(): return lax.ppermute(x, axis, swap_pairs(lax.axis_size(axis), first))  6.95 us
    ppermute x4, waiting for transfers between devices, swap(): return lax.ppermute(x, axis, swap_pairs(lax.axis_size(axis), first))  3.2 us
  transfers between devices with their start and end apart: 5, of which 1 were waited for; matrix products, arithmetic and copies ran while one was open for 0% of the time, Pallas kernels for 22%

profile of v1, /device:TPU:1, one launch (start us, length us, event | category | flops | bytes accessed | tf_op | source)
XLA Modules:
  0.0 46.0 jit_solution(9213163201785590695)
XLA Ops:
  0.0 1.0 %copy-done = f32[3,16,16,128]{3,2,1,0:T(8,128)S(1)} copy-done((f32[3,16,16,128]{3,2,1,0:T(8,128)S(1)}, f32[3,16,16,128]{3,2,1,0:T(8,128)}, u32[]{:S(2)}) %copy-start) | copy-done | bytes 393240
  1.0 0.7 %copy-done.15 = s32[1,1,96]{2,1,0:T(1,128)S(1)} copy-done((s32[1,1,96]{2,1,0:T(1,128)S(1)}, s32[1,1,96]{2,1,0:T(1,128)}, u32[]{:S(2)}) %copy-start.15) | copy-done | bytes 408
  1.7 0.1 pack_y.1
  1.7 2.1 %collective-permute-start = (f32[104,128]{1,0:T(8,128)S(1)}, f32[104,128]{1,0:T(8,128)S(1)}, u32[]{:S(2)}, u32[]{:S(2)}) collective-permute-start(f32[104,128]{1,0:T(8,128)S(1)} %get-tuple-element.16), channel_id=1, source_target_pairs={{0,1},{1,0},{2,3},{3,2},{4,5},{5,4},{6,7},{7,6},{8,9},{9,8},{10,11... | collective-permute-start | bytes 159752 | tf_op jit(solution)/shard_map/ppermute | solution.py:42
  3.9 0.7 %collective-permute-start.1 = (f32[104,128]{1,0:T(8,128)S(1)}, f32[104,128]{1,0:T(8,128)S(1)}, u32[]{:S(2)}, u32[]{:S(2)}) collective-permute-start(f32[104,128]{1,0:T(8,128)S(1)} %get-tuple-element.17), channel_id=1, source_target_pairs={{1,2},{2,1},{3,4},{4,3},{5,6},{6,5},{9,10},{10,9},{11,12},{12,11},... | collective-permute-start | bytes 159752 | tf_op jit(solution)/shard_map/ppermute | solution.py:42
  4.5 0.7 %copy-done.13 = f32[1,16,384]{2,1,0:T(8,128)S(1)} copy-done((f32[1,16,384]{2,1,0:T(8,128)S(1)}, f32[1,16,384]{2,1,0:T(8,128)}, u32[]{:S(2)}) %copy-start.13) | copy-done | bytes 24600
  5.3 0.7 %copy-done.16 = s32[1,16,384]{2,1,0:T(8,128)S(1)} copy-done((s32[1,16,384]{2,1,0:T(8,128)S(1)}, s32[1,16,384]{2,1,0:T(8,128)}, u32[]{:S(2)}) %copy-start.16) | copy-done | bytes 24600
  6.0 0.7 %copy-done.18 = s32[1,16,384]{2,1,0:T(8,128)S(1)} copy-done((s32[1,16,384]{2,1,0:T(8,128)S(1)}, s32[1,16,384]{2,1,0:T(8,128)}, u32[]{:S(2)}) %copy-start.18) | copy-done | bytes 24600
  6.8 0.7 %copy-done.20 = s32[1,16]{1,0:T(1,128)S(1)} copy-done((s32[1,16]{1,0:T(1,128)S(1)}, s32[1,16]{1,0:T(1,128)}, u32[]{:S(2)}) %copy-start.20) | copy-done | bytes 88
  7.4 5.4 %histogram.1 = (bf16[16,256,128]{2,1,0:T(8,128)(2,1)S(1)}, f32[16,256,128]{2,1,0:T(8,128)S(1)}, f32[16,128]{1,0:T(8,128)S(1)}, f32[16,128]{1,0:T(8,128)S(1)}, f32[16,384]{1,0:T(8,128)S(1)}) custom-call(f32[3,16,16,128]{3,2,1,0:T(8,128)S(1)} %copy-done, s32[1,1,96]{2,1,0:T(1,128)S(1)} %copy-done.15, s32[1,16]{1,0:T(1,128)S(1)} %copy-done.20, ...), custom_call_target="tpu_custom_call" | custom-call | flops 1207959552 | bytes 4194304 | tf_op jit(solution)/shard_map/histogram/pallas_call | solution.py:46
  12.8 0.0 copy-start.7
  12.9 0.0 copy-start.1
  12.9 0.0 copy-start.14
  12.9 1.0 %collective-permute-start.2 = (f32[272,128]{1,0:T(8,128)S(1)}, f32[272,128]{1,0:T(8,128)S(1)}, u32[]{:S(2)}, u32[]{:S(2)}) collective-permute-start(f32[272,128]{1,0:T(8,128)S(1)} %get-tuple-element.21), channel_id=1, source_target_pairs={{0,8},{8,0},{16,24},{24,16},{1,9},{9,1},{17,25},{25,17},{2,10},{10... | collective-permute-start | bytes 417800 | tf_op jit(solution)/shard_map/ppermute | solution.py:42
  13.9 3.1 %collective-permute-start.3 = (f32[272,128]{1,0:T(8,128)S(1)}, f32[272,128]{1,0:T(8,128)S(1)}, u32[]{:S(2)}, u32[]{:S(2)}) collective-permute-start(f32[272,128]{1,0:T(8,128)S(1)} %get-tuple-element.22), channel_id=1, source_target_pairs={{8,16},{16,8},{9,17},{17,9},{10,18},{18,10},{11,19},{19,11},{12,20... | collective-permute-start | bytes 417800 | tf_op jit(solution)/shard_map/ppermute | solution.py:42
  17.1 3.2 %collective-permute-done.3.xo.args_7_.args_5_ = f32[272,128]{1,0:T(8,128)S(1)} collective-permute-done((f32[272,128]{1,0:T(8,128)S(1)}, f32[272,128]{1,0:T(8,128)S(1)}, u32[]{:S(2)}, u32[]{:S(2)}) %collective-permute-start.3) | collective-permute-done | bytes 139296 | tf_op jit(solution)/shard_map/ppermute | solution.py:42
  20.3 2.0 %reduce_sums.1 = f32[8,16,128]{2,1,0:T(8,128)} custom-call(f32[3,16,16,128]{3,2,1,0:T(8,128)S(1)} %copy-done, f32[104,128]{1,0:T(8,128)S(1)} %collective-permute-done.ye.args_4_.args_2_, f32[104,128]{1,0:T(8,128)S(1)} %collective-permute-done.1.yo.args_5_.args_3_, f32[272,128]{1,0:T(8,128)S(1)} %collective-permute-done.2.xe.args_6_.args_4_, ...), custom_call_target="tpu_custom_call" | custom-call | tf_op jit(solution)/shard_map/reduce_sums/pallas_call | solution.py:46
  22.3 0.7 %copy-done.2 = f32[272,128]{1,0:T(8,128)} copy-done((f32[272,128]{1,0:T(8,128)}, f32[272,128]{1,0:T(8,128)S(1)}, u32[]{:S(2)}) %copy-start.2) | copy-done | bytes 139288
  23.0 7.3 %all-to-all-start = ((f32[8,16,128]{2,1,0:T(8,128)}), f32[8,16,128]{2,1,0:T(8,128)}, u32[]{:S(2)}, u32[]{:S(2)}) async-start(f32[8,16,128]{2,1,0:T(8,128)} %reduce_sums.1), calls=%async_computation | async-start | bytes 131072 | tf_op jit(solution)/shard_map/all_to_all | solution.py:378
  30.3 0.0 copy-start.3
  30.3 0.9 %copy-done.3 = f32[272,128]{1,0:T(8,128)S(1)} copy-done((f32[272,128]{1,0:T(8,128)S(1)}, f32[272,128]{1,0:T(8,128)}, u32[]{:S(2)}) %copy-start.3) | copy-done | bytes 139288
  31.2 0.8 %copy-done.8 = f32[104,128]{1,0:T(8,128)S(1)} copy-done((f32[104,128]{1,0:T(8,128)S(1)}, f32[104,128]{1,0:T(8,128)}, u32[]{:S(2)}) %copy-start.8) | copy-done | bytes 53272
  32.0 0.8 %copy-done.11 = f32[104,128]{1,0:T(8,128)S(1)} copy-done((f32[104,128]{1,0:T(8,128)S(1)}, f32[104,128]{1,0:T(8,128)}, u32[]{:S(2)}) %copy-start.11) | copy-done | bytes 53272
  32.8 0.7 %copy-done.17 = s32[1,16,384]{2,1,0:T(8,128)S(1)} copy-done((s32[1,16,384]{2,1,0:T(8,128)S(1)}, s32[1,16,384]{2,1,0:T(8,128)}, u32[]{:S(2)}) %copy-start.17) | copy-done | bytes 24600
  33.6 0.7 %copy-done.19 = s32[1,16,384]{2,1,0:T(8,128)S(1)} copy-done((s32[1,16,384]{2,1,0:T(8,128)S(1)}, s32[1,16,384]{2,1,0:T(8,128)}, u32[]{:S(2)}) %copy-start.19) | copy-done | bytes 24600
  34.3 4.8 %edges.1 = (f32[4,16,16,128]{3,2,1,0:T(8,128)S(1)}, f32[3,18,32,128]{3,2,1,0:T(8,128)S(1)}) custom-call(f32[3,16,16,128]{3,2,1,0:T(8,128)S(1)} %copy-done.1, s32[1,16,384]{2,1,0:T(8,128)S(1)} %copy-done.17, s32[1,16,384]{2,1,0:T(8,128)S(1)} %copy-done.19, f32[1,16,384]{2,1,0:T(8,128)S(1)} %copy-done.14, f32[104,128]{1,0:T(8,128)S(1)} %copy-done.8, ...), custom_call_target="tpu_custom_call" | custom-call | flops 1207959552 | bytes 4194304 | tf_op jit(solution)/shard_map/edges/pallas_call | solution.py:46
  39.1 0.8 %copy-done.5 = f32[4,16,16,128]{3,2,1,0:T(8,128)} copy-done((f32[4,16,16,128]{3,2,1,0:T(8,128)}, f32[4,16,16,128]{3,2,1,0:T(8,128)S(1)}, u32[]{:S(2)}) %copy-start.5) | copy-done | bytes 524312
  40.0 0.9 %copy-done.4 = f32[272,128]{1,0:T(8,128)S(1)} copy-done((f32[272,128]{1,0:T(8,128)S(1)}, f32[272,128]{1,0:T(8,128)}, u32[]{:S(2)}) %copy-start.4) | copy-done | bytes 139288
  40.9 1.0 %copy-done.6 = f32[4,16,16,128]{3,2,1,0:T(8,128)S(1)} copy-done((f32[4,16,16,128]{3,2,1,0:T(8,128)S(1)}, f32[4,16,16,128]{3,2,1,0:T(8,128)}, u32[]{:S(2)}) %copy-start.6) | copy-done | bytes 524312
  41.9 0.8 %copy-done.9 = f32[104,128]{1,0:T(8,128)S(1)} copy-done((f32[104,128]{1,0:T(8,128)S(1)}, f32[104,128]{1,0:T(8,128)}, u32[]{:S(2)}) %copy-start.9) | copy-done | bytes 53272
  42.7 0.8 %copy-done.12 = f32[104,128]{1,0:T(8,128)S(1)} copy-done((f32[104,128]{1,0:T(8,128)S(1)}, f32[104,128]{1,0:T(8,128)}, u32[]{:S(2)}) %copy-start.12) | copy-done | bytes 53272
  43.6 2.5 %advance.1 = f32[3,16,16,128]{3,2,1,0:T(8,128)} custom-call(f32[8,16,128]{2,1,0:T(8,128)} %all-to-all-done.args_0_, f32[3,16,16,128]{3,2,1,0:T(8,128)S(1)} %copy-done.1, f32[104,128]{1,0:T(8,128)S(1)} %copy-done.9, f32[104,128]{1,0:T(8,128)S(1)} %copy-done.12, f32[272,128]{1,0:T(8,128)S(1)} %collective-permute-done.2.xe.args_6_.args_4_, ...), custom_call_target="tpu_custom_call" | custom-call | tf_op jit(solution)/shard_map/advance/pallas_call | solution.py:46
  (26 shorter events, 0.1 us)
Async XLA Ops:
  0.0 1.0 %copy-start = (f32[3,16,16,128]{3,2,1,0:T(8,128)S(1)}, f32[3,16,16,128]{3,2,1,0:T(8,128)}, u32[]{:S(2)}) copy-start(f32[3,16,16,128]{3,2,1,0:T(8,128)} %args_1_.6) | copy-start | bytes 1179652
  1.0 0.7 %copy-start.15 = (s32[1,1,96]{2,1,0:T(1,128)S(1)}, s32[1,1,96]{2,1,0:T(1,128)}, u32[]{:S(2)}) copy-start(s32[1,1,96]{2,1,0:T(1,128)} %tc.3) | copy-start | bytes 1156
  1.7 11.1 %collective-permute-start = (f32[104,128]{1,0:T(8,128)S(1)}, f32[104,128]{1,0:T(8,128)S(1)}, u32[]{:S(2)}, u32[]{:S(2)}) collective-permute-start(f32[104,128]{1,0:T(8,128)S(1)} %get-tuple-element.16), channel_id=1, source_target_pairs={{0,1},{1,0},{2,3},{3,2},{4,5},{5,4},{6,7},{7,6},{8,9},{9,8},{10,11... | collective-permute-start | bytes 159752 | tf_op jit(solution)/shard_map/ppermute | solution.py:42
  3.9 9.0 %collective-permute-start.1 = (f32[104,128]{1,0:T(8,128)S(1)}, f32[104,128]{1,0:T(8,128)S(1)}, u32[]{:S(2)}, u32[]{:S(2)}) collective-permute-start(f32[104,128]{1,0:T(8,128)S(1)} %get-tuple-element.17), channel_id=1, source_target_pairs={{1,2},{2,1},{3,4},{4,3},{5,6},{6,5},{9,10},{10,9},{11,12},{12,11},... | collective-permute-start | bytes 159752 | tf_op jit(solution)/shard_map/ppermute | solution.py:42
  4.5 0.7 %copy-start.13 = (f32[1,16,384]{2,1,0:T(8,128)S(1)}, f32[1,16,384]{2,1,0:T(8,128)}, u32[]{:S(2)}) copy-start(f32[1,16,384]{2,1,0:T(8,128)} %args_3_.4) | copy-start | bytes 73732
  5.3 0.7 %copy-start.16 = (s32[1,16,384]{2,1,0:T(8,128)S(1)}, s32[1,16,384]{2,1,0:T(8,128)}, u32[]{:S(2)}) copy-start(s32[1,16,384]{2,1,0:T(8,128)} %args_1_.5) | copy-start | bytes 73732
  6.0 0.7 %copy-start.18 = (s32[1,16,384]{2,1,0:T(8,128)S(1)}, s32[1,16,384]{2,1,0:T(8,128)}, u32[]{:S(2)}) copy-start(s32[1,16,384]{2,1,0:T(8,128)} %args_2_.4) | copy-start | bytes 73732
  6.8 0.7 %copy-start.20 = (s32[1,16]{1,0:T(1,128)S(1)}, s32[1,16]{1,0:T(1,128)}, u32[]{:S(2)}) copy-start(s32[1,16]{1,0:T(1,128)} %owner.1) | copy-start | bytes 196
  12.8 7.5 %copy-start.7 = (f32[104,128]{1,0:T(8,128)}, f32[104,128]{1,0:T(8,128)S(1)}, u32[]{:S(2)}) copy-start(f32[104,128]{1,0:T(8,128)S(1)} %collective-permute-done.ye.args_4_.args_2_) | copy-start | bytes 159748
  12.9 7.5 %copy-start.10 = (f32[104,128]{1,0:T(8,128)}, f32[104,128]{1,0:T(8,128)S(1)}, u32[]{:S(2)}) copy-start(f32[104,128]{1,0:T(8,128)S(1)} %collective-permute-done.1.yo.args_5_.args_3_) | copy-start | bytes 159748
  12.9 17.4 %copy-start.1 = (f32[3,16,16,128]{3,2,1,0:T(8,128)S(1)}, f32[3,16,16,128]{3,2,1,0:T(8,128)}, u32[]{:S(2)}) copy-start(f32[3,16,16,128]{3,2,1,0:T(8,128)} %args_1_.6) | copy-start | bytes 1179652
  12.9 17.4 %copy-start.14 = (f32[1,16,384]{2,1,0:T(8,128)S(1)}, f32[1,16,384]{2,1,0:T(8,128)}, u32[]{:S(2)}) copy-start(f32[1,16,384]{2,1,0:T(8,128)} %args_3_.4) | copy-start | bytes 73732
  12.9 4.2 %collective-permute-start.2 = (f32[272,128]{1,0:T(8,128)S(1)}, f32[272,128]{1,0:T(8,128)S(1)}, u32[]{:S(2)}, u32[]{:S(2)}) collective-permute-start(f32[272,128]{1,0:T(8,128)S(1)} %get-tuple-element.21), channel_id=1, source_target_pairs={{0,8},{8,0},{16,24},{24,16},{1,9},{9,1},{17,25},{25,17},{2,10},{10... | collective-permute-start | bytes 417800 | tf_op jit(solution)/shard_map/ppermute | solution.py:42
  13.9 6.4 %collective-permute-start.3 = (f32[272,128]{1,0:T(8,128)S(1)}, f32[272,128]{1,0:T(8,128)S(1)}, u32[]{:S(2)}, u32[]{:S(2)}) collective-permute-start(f32[272,128]{1,0:T(8,128)S(1)} %get-tuple-element.22), channel_id=1, source_target_pairs={{8,16},{16,8},{9,17},{17,9},{10,18},{18,10},{11,19},{19,11},{12,20... | collective-permute-start | bytes 417800 | tf_op jit(solution)/shard_map/ppermute | solution.py:42
  22.3 0.7 %copy-start.2 = (f32[272,128]{1,0:T(8,128)}, f32[272,128]{1,0:T(8,128)S(1)}, u32[]{:S(2)}) copy-start(f32[272,128]{1,0:T(8,128)S(1)} %collective-permute-done.3.xo.args_7_.args_5_) | copy-start | bytes 417796
  23.0 17.0 %all-to-all-start = ((f32[8,16,128]{2,1,0:T(8,128)}), f32[8,16,128]{2,1,0:T(8,128)}, u32[]{:S(2)}, u32[]{:S(2)}) async-start(f32[8,16,128]{2,1,0:T(8,128)} %reduce_sums.1), calls=%async_computation | async-start | bytes 131072 | tf_op jit(solution)/shard_map/all_to_all | solution.py:378
  30.3 0.9 %copy-start.3 = (f32[272,128]{1,0:T(8,128)S(1)}, f32[272,128]{1,0:T(8,128)}, u32[]{:S(2)}) copy-start(f32[272,128]{1,0:T(8,128)} %copy-done.2) | copy-start | bytes 417796
  31.2 0.8 %copy-start.8 = (f32[104,128]{1,0:T(8,128)S(1)}, f32[104,128]{1,0:T(8,128)}, u32[]{:S(2)}) copy-start(f32[104,128]{1,0:T(8,128)} %copy-done.7) | copy-start | bytes 159748
  32.0 0.8 %copy-start.11 = (f32[104,128]{1,0:T(8,128)S(1)}, f32[104,128]{1,0:T(8,128)}, u32[]{:S(2)}) copy-start(f32[104,128]{1,0:T(8,128)} %copy-done.10) | copy-start | bytes 159748
  32.8 0.7 %copy-start.17 = (s32[1,16,384]{2,1,0:T(8,128)S(1)}, s32[1,16,384]{2,1,0:T(8,128)}, u32[]{:S(2)}) copy-start(s32[1,16,384]{2,1,0:T(8,128)} %args_1_.5) | copy-start | bytes 73732
  33.6 0.7 %copy-start.19 = (s32[1,16,384]{2,1,0:T(8,128)S(1)}, s32[1,16,384]{2,1,0:T(8,128)}, u32[]{:S(2)}) copy-start(s32[1,16,384]{2,1,0:T(8,128)} %args_2_.4) | copy-start | bytes 73732
  39.1 0.8 %copy-start.5 = (f32[4,16,16,128]{3,2,1,0:T(8,128)}, f32[4,16,16,128]{3,2,1,0:T(8,128)S(1)}, u32[]{:S(2)}) copy-start(f32[4,16,16,128]{3,2,1,0:T(8,128)S(1)} %get-tuple-element.25.args_8_) | copy-start | bytes 1572868
  40.0 0.9 %copy-start.4 = (f32[272,128]{1,0:T(8,128)S(1)}, f32[272,128]{1,0:T(8,128)}, u32[]{:S(2)}) copy-start(f32[272,128]{1,0:T(8,128)} %copy-done.2) | copy-start | bytes 417796
  40.9 1.0 %copy-start.6 = (f32[4,16,16,128]{3,2,1,0:T(8,128)S(1)}, f32[4,16,16,128]{3,2,1,0:T(8,128)}, u32[]{:S(2)}) copy-start(f32[4,16,16,128]{3,2,1,0:T(8,128)} %copy-done.5) | copy-start | bytes 1572868
  41.9 0.8 %copy-start.9 = (f32[104,128]{1,0:T(8,128)S(1)}, f32[104,128]{1,0:T(8,128)}, u32[]{:S(2)}) copy-start(f32[104,128]{1,0:T(8,128)} %copy-done.7) | copy-start | bytes 159748
  42.7 0.8 %copy-start.12 = (f32[104,128]{1,0:T(8,128)S(1)}, f32[104,128]{1,0:T(8,128)}, u32[]{:S(2)}) copy-start(f32[104,128]{1,0:T(8,128)} %copy-done.10) | copy-start | bytes 159748

commit v2 on v1

v2 whole, which is shorter than its diff:
```python
import jax
import jax.numpy as jnp
from jax import lax
from jax.experimental import pallas as pl
from jax.experimental.pallas import tpu as pltpu
from jax.sharding import PartitionSpec as P

SPREAD = 0.12
CARRY = 0.25
FREE_WIND = 1.0
LOAD = 0.6

F32 = jnp.float32
BF16 = jnp.bfloat16
NT = (((1,), (1,)), ((), ()))
LANES = 128
OWN = 8
PLANE = 32
EDGE = 24


def iota(shape, axis):
    return lax.broadcasted_iota(jnp.int32, shape, axis)


def rounded(x):
    return x.astype(BF16).astype(F32)


def one_hot(count, row):
    places = iota((count, row.shape[1]), 0).astype(BF16)
    return places == row.astype(BF16)


def ones_at(mask):
    return jnp.where(mask, jnp.ones((), BF16), jnp.zeros((), BF16))


def pick_slots(tc, cells):
    slots = tc.shape[2]
    row = jnp.broadcast_to(tc[0, :, :].astype(F32), (slots, slots))
    same = iota((slots, slots), 0) == iota((slots, slots), 1)
    column = jnp.sum(jnp.where(same, row, 0.0), axis=1, keepdims=True).astype(jnp.int32)
    return jnp.where(iota((slots, cells), 1) == column, 1.0, 0.0).astype(BF16)


def even(axis):
    return lax.rem(lax.axis_index(axis), 2) == 0


def swap_pairs(count, first):
    pairs = []
    for i in range(first, count - 1, 2):
        pairs += [(i, i + 1), (i + 1, i)]
    return pairs


def swap(x, axis, first):
    return lax.ppermute(x, axis, swap_pairs(lax.axis_size(axis), first))


def call(kernel, name, outs, args, scratch=(), flops=0, nbytes=0, space=pltpu.VMEM):
    return pl.pallas_call(
        kernel,
        out_shape=[jax.ShapeDtypeStruct(s, d) for s, d in outs],
        in_specs=[pl.BlockSpec(memory_space=space)] * len(args),
        out_specs=[pl.BlockSpec(memory_space=pltpu.VMEM)] * len(outs),
        scratch_shapes=list(scratch),
        compiler_params=pltpu.CompilerParams(vmem_limit_bytes=16 << 20),
        cost_estimate=pl.CostEstimate(flops=flops, bytes_accessed=nbytes, transcendentals=0),
        name=name,
    )(*args)


def lane_edge(center):
    lane = iota(center.shape, 2)
    last = center.shape[2] - 1
    below = jnp.where(lane == 0, 0.0, pltpu.roll(center, 1, 2))
    above = jnp.where(lane == last, 0.0, pltpu.roll(center, last, 2))
    return below + above


def stencil(ref, c, x0, nx, r0, nr):
    center = ref[c, x0 : x0 + nx, r0 : r0 + nr, :]
    before = ref[c, x0 - 1 : x0 - 1 + nx, r0 : r0 + nr, :]
    after = ref[c, x0 + 1 : x0 + 1 + nx, r0 : r0 + nr, :]
    beside = before + after
    beside = beside + ref[c, x0 : x0 + nx, r0 - 1 : r0 - 1 + nr, :]
    beside = beside + ref[c, x0 : x0 + nx, r0 + 1 : r0 + 1 + nr, :]
    beside = beside + lane_edge(center)
    return center + SPREAD * (beside - 6.0 * center) - CARRY * (center - before)


def stage(v_hbm, tc_hbm, owner_hbm, slot_hbm, height_hbm, load_hbm, v, tc, owner, slot, height, load, to_even, to_odd, sems):
    pairs = ((v_hbm, v), (tc_hbm, tc), (slot_hbm, slot), (height_hbm, height), (load_hbm, load), (owner_hbm, owner))
    copies = [pltpu.make_async_copy(a, b, sems.at[i]) for i, (a, b) in enumerate(pairs)]
    for copy in copies:
        copy.start()
    copies[0].wait()
    comps, nx, ny, _ = v.shape
    ev = even("gy")
    at = 0
    for c in range(comps):
        for k in range(2):
            high = v[c, :, ny - 2 + k, :]
            low = v[c, :, k, :]
            to_even[at : at + nx, :] = jnp.where(ev, high, low)
            to_odd[at : at + nx, :] = jnp.where(ev, low, high)
            at += nx
    copies[1].wait()
    cells = tc[0, :, :].astype(F32) + 1.0
    slots = cells.shape[1]
    for out in (to_even, to_odd):
        out[at : at + 8, :] = jnp.zeros((8, LANES), F32)
        out[at : at + 1, 0:slots] = cells
    for copy in copies[2:]:
        copy.wait()


def histogram(v, tc, owner, slot, height, load, count_ref, load_ref, sum_ref, scale_ref, code_ref):
    _, turbines, points = slot.shape
    slots, levels = count_ref.shape[1:]
    cells = v.shape[1] * v.shape[2]
    first = lax.axis_index("gy") * slots
    values = v[0, :, :, :].reshape(cells, levels).astype(BF16)
    rows = jnp.dot(pick_slots(tc, cells), values, preferred_element_type=F32)
    local = slot[0, :, :] - first
    inside = (local >= 0) & (local < slots)
    code_ref[...] = jnp.where(inside, local * levels + height[0, :, :] + 1, 0).astype(F32)
    zero = jnp.zeros((), BF16)
    for t in range(turbines):
        a = ones_at(one_hot(slots, slot[0, t : t + 1, :] - first))
        at_z = one_hot(levels, height[0, t : t + 1, :])
        weight = load[0, t : t + 1, :]
        high = weight.astype(BF16)
        low = (weight - high.astype(F32)).astype(BF16)
        b = jnp.concatenate([ones_at(at_z), jnp.where(at_z, high, zero), jnp.where(at_z, low, zero)], axis=0)
        both = lax.dot_general(a, b, NT, preferred_element_type=F32)
        count = both[:, :levels]
        count_ref[t] = count.astype(BF16)
        load_ref[t] = both[:, levels : 2 * levels] + both[:, 2 * levels :]
        sum_ref[t : t + 1, :] = jnp.sum(count * rows, axis=0, keepdims=True)
    same = iota((turbines, turbines), 0) == iota((turbines, turbines), 1)
    owner_row = jnp.broadcast_to(owner[...].astype(F32), (turbines, turbines))
    owner_col = jnp.sum(jnp.where(same, owner_row, 0.0), axis=1, keepdims=True)
    member = owner_row == owner_col
    load_col = jnp.sum(load[0, :, :], axis=1, keepdims=True)
    load_row = jnp.sum(jnp.where(same, load_col, 0.0), axis=0, keepdims=True)
    total = jnp.sum(jnp.where(member, load_row, 0.0), axis=1, keepdims=True)
    number = jnp.sum(jnp.where(member, 1.0, 0.0), axis=1, keepdims=True)
    scale_ref[...] = jnp.broadcast_to(LOAD / (total / (number * points)), scale_ref.shape)


def pack_x(v, tc, ye, yo, sums, scale, code, load, to_even, to_odd):
    comps, nx, ny, _ = v.shape
    turbines, points = code.shape
    ev_x, ev_y = even("gx"), even("gy")
    at = 0
    for c in range(comps):
        for k in range(2):
            low_at, high_at = (c * 2 + 1) * nx, (c * 2) * nx
            sides = []
            for x in (nx - 2 + k, k):
                below = picked(ev_y, yo, ye, low_at + x, low_at + x + 1)
                above = picked(ev_y, ye, yo, high_at + x, high_at + x + 1)
                sides.append((v[c, x, :, :], below, above))
            (own_r, below_r, above_r), (own_l, below_l, above_l) = sides
            for out, pick in ((to_even, ev_x), (to_odd, jnp.logical_not(ev_x))):
                out[at : at + EDGE, :] = jnp.zeros((EDGE, LANES), F32)
                out[at + 4 : at + 4 + ny, :] = jnp.where(pick, own_r, own_l)
                out[at + 3 : at + 4, :] = jnp.where(pick, below_r, below_l)
                out[at + 4 + ny : at + 5 + ny, :] = jnp.where(pick, above_r, above_l)
            at += EDGE
    parts = [code[:, k : k + LANES] for k in range(0, points, LANES)]
    parts += [load[0, :, k : k + LANES] for k in range(0, points, LANES)]
    parts += [sums[...], scale[...]]
    cells = tc[0, :, :].astype(F32) + 1.0
    for out in (to_even, to_odd):
        end = at
        for part in parts:
            out[end : end + turbines, :] = part
            end += turbines
        out[end : end + 8, :] = jnp.zeros((8, LANES), F32)
        out[end : end + 1, 0 : cells.shape[1]] = cells


def picked(flag, a, b, lo, hi):
    return jnp.where(flag, a[lo:hi, :], b[lo:hi, :])


def extend(v, ye, yo, xe, xo, field, comps):
    _, nx, ny, _ = v.shape
    ev_x, ev_y = even("gx"), even("gy")
    for c in comps:
        out = c if len(comps) > 1 else 0
        field[out, 2 : 2 + nx, 0:OWN, :] = jnp.zeros((nx, OWN, LANES), F32)
        field[out, 2 : 2 + nx, OWN + ny : PLANE, :] = jnp.zeros((nx, PLANE - OWN - ny, LANES), F32)
        field[out, 2 : 2 + nx, OWN : OWN + ny, :] = v[c, :, :, :]
        for k in range(2):
            at = (c * 2 + k) * nx
            field[out, 2 : 2 + nx, OWN - 2 + k, :] = picked(ev_y, yo, ye, at, at + nx)
            field[out, 2 : 2 + nx, OWN + ny + k, :] = picked(ev_y, ye, yo, at, at + nx)
            at = (c * 2 + k) * EDGE
            for x, a, b in ((k, xo, xe), (2 + nx + k, xe, xo)):
                field[out, x, 0:OWN, :] = jnp.zeros((OWN, LANES), F32)
                field[out, x, PLANE - OWN : PLANE, :] = jnp.zeros((OWN, LANES), F32)
                field[out, x, 4 : 4 + EDGE, :] = picked(ev_x, a, b, at, at + EDGE)


def reduce_sums(v, tc, ye, yo, xe, xo, counts, loads, sums, out, field, products):
    _, nx, ny, levels = v.shape
    turbines, slots, _ = counts.shape
    cells = nx * ny
    extend(v, ye, yo, xe, xo, field, (0,))
    update = stencil(field, 0, 2, nx, OWN, ny).reshape(cells, levels).astype(BF16)
    values = v[0, :, :, :].reshape(cells, levels).astype(BF16)
    pair = jnp.concatenate([values, update], axis=1)
    rows = jnp.dot(pick_slots(tc, cells), pair, preferred_element_type=F32)
    products[turbines] = rows[:, levels:].astype(BF16)
    rows = rows[:, :levels]
    for t in range(turbines):
        products[t] = (rows * loads[t]).astype(BF16)
    block = 16
    wide, more = turbines * block, (turbines + 1) * block
    gram = jnp.zeros((wide, more), F32)
    for b in range(0, slots, block):
        left = counts[:, b : b + block, :].reshape(wide, levels)
        right = products[:, b : b + block, :].reshape(more, levels)
        gram = gram + lax.dot_general(left, right, NT, preferred_element_type=F32)
    keep = (iota((wide, more), 0) & (block - 1)) == (iota((wide, more), 1) & (block - 1))
    gram = jnp.sum(jnp.where(keep, gram, 0.0).reshape(turbines, block, more), axis=1)
    select = jnp.where(iota((more, LANES), 0) // block == iota((more, LANES), 1), 1.0, 0.0)
    result = jnp.dot(gram, select, precision=lax.Precision.HIGHEST, preferred_element_type=F32)
    lane = iota((turbines, LANES), 1)
    ev_x = even("gx")
    at = xe.shape[0] - 8 - 2 * turbines
    left_sums = picked(ev_x, xo, xe, at, at + turbines)
    right_sums = picked(ev_x, xe, xo, at, at + turbines)
    for k, part in enumerate((sums[...], left_sums, right_sums)):
        result = jnp.where(lane == turbines + 1 + k, jnp.sum(part, axis=1, keepdims=True), result)
    for k in range(out.shape[0]):
        out[k] = result


def spread(wheres, hits, z, weight):
    high = weight.astype(BF16)
    low = (weight - high.astype(F32)).astype(BF16)
    at_z = ones_at(one_hot(LANES, z))
    left = []
    for where, hit in zip(wheres, hits):
        place = jnp.dot(where, hit, preferred_element_type=F32).astype(BF16)
        left += [place * high, place * low]
    both = lax.dot_general(jnp.concatenate(left, axis=0), at_z, NT, preferred_element_type=F32)
    n = wheres[0].shape[0]
    return [both[2 * k * n : (2 * k + 1) * n] + both[(2 * k + 1) * n : (2 * k + 2) * n] for k in range(len(wheres))]


def edges_y(slots, nx, ny, slot, height, load, ye, yo, edge_ref):
    turbines = slot.shape[1]
    ev = even("gy")
    me = lax.axis_index("gy")
    at = ye.shape[0] - 8
    wheres = []
    for a, b, y in ((yo, ye, ny - 1), (ye, yo, 0)):
        cell = picked(ev, a, b, at, at + 1)[:, :slots].astype(jnp.int32) - 1
        wheres.append(jnp.where(iota((nx, slots), 0) * ny + y == cell, 1.0, 0.0).astype(BF16))
    for t in range(turbines):
        row = slot[0, t : t + 1, :]
        hits = [ones_at(one_hot(slots, row - (me + k) * slots)) for k in (-1, 1)]
        edge_ref[0, t], edge_ref[1, t] = spread(wheres, hits, height[0, t : t + 1, :], load[0, t : t + 1, :])


def edges_x(slots, pieces, v, ye, yo, xe, xo, edge_ref, update_ref, field):
    comps, nx, ny, levels = v.shape
    turbines = edge_ref.shape[1]
    ev = even("gx")
    extend(v, ye, yo, xe, xo, field, tuple(range(comps)))
    for c in range(comps):
        update_ref[c, :, OWN - 1 : OWN + ny + 1, :] = stencil(field, c, 1, nx + 2, OWN - 1, ny + 2)

    at = xe.shape[0] - 8
    code_at = comps * 2 * EDGE
    load_at = code_at + pieces * turbines
    shift = levels.bit_length() - 1
    for k, (a, b) in enumerate(((xo, xe), (xe, xo))):
        cell = picked(ev, a, b, at, at + 1)[:, :slots].astype(jnp.int32) - 1
        where = jnp.where(iota((ny, slots), 0) + (1 - k) * (nx - 1) * ny == cell, 1.0, 0.0).astype(BF16)
        codes = [picked(ev, a, b, code_at + i * turbines, code_at + (i + 1) * turbines) for i in range(pieces)]
        codes = jnp.concatenate(codes, axis=1).astype(jnp.int32) - 1
        there = [picked(ev, a, b, load_at + i * turbines, load_at + (i + 1) * turbines) for i in range(pieces)]
        there = jnp.concatenate(there, axis=1)
        for t in range(turbines):
            code = codes[t : t + 1, :]
            hit = ones_at(one_hot(slots, code >> shift))
            (edge_ref[k, t],) = spread([where], [hit], code & (levels - 1), there[t : t + 1, :])


def advance(points, got, v, tc, ye, yo, xe, xo, scale, loads, edge_x, edge_y, update_ref, out, field, parts):
    comps, nx, ny, levels = v.shape
    turbines, slots, _ = loads.shape
    cells = nx * ny
    ev_x, ev_y = even("gx"), even("gy")
    total = got[0]
    for k in range(1, got.shape[0]):
        total = total + got[k]
    lane = iota((turbines, LANES), 1)

    def column(k):
        return jnp.sum(jnp.where(lane == k, total, 0.0), axis=1, keepdims=True)

    def coefs(scales, sums):
        return -(scales * (FREE_WIND + sums / points))

    scale_at = xe.shape[0] - 8 - turbines
    own = coefs(scale[...], column(turbines + 1))
    left = coefs(picked(ev_x, xo, xe, scale_at, scale_at + turbines), column(turbines + 2))
    right = coefs(picked(ev_x, xe, xo, scale_at, scale_at + turbines), column(turbines + 3))
    as_row = jnp.sum(jnp.where(iota((turbines, LANES), 0) == lane, own, 0.0), axis=0, keepdims=True)
    forced = jnp.sum(jnp.where(lane < turbines, total * as_row, 0.0), axis=1, keepdims=True)
    later = coefs(scale[...], column(turbines) + forced)

    for s in range(0, slots, 16):
        first = jnp.zeros((16, levels), F32)
        second = first
        for t in range(turbines):
            part = loads[t, s : s + 16, :]
            first = first + own[t : t + 1, :] * part
            second = second + later[t : t + 1, :] * part
        for i, rest in enumerate((first, second)):
            for k in range(3):
                piece = rest.astype(BF16)
                rest = rest - piece.astype(F32)
                at = (3 * i + k) * levels
                parts[s : s + 16, at : at + levels] = piece
    row = tc[0, :, :]
    put = jnp.where(iota((cells, slots), 0) == row, 1.0, 0.0).astype(BF16)
    spread_out = jnp.dot(put, parts[...], preferred_element_type=F32)
    pieces = [spread_out[:, k * levels : (k + 1) * levels] for k in range(6)]
    first = ((pieces[0] + pieces[1]) + pieces[2]).reshape(nx, ny, levels)
    second = ((pieces[3] + pieces[4]) + pieces[5]).reshape(nx, ny, levels)
    for c in range(comps):
        push = rounded(rounded(v[c, :, :, :]) * first)
        field[c, 1 : 1 + nx, OWN : OWN + ny, :] = update_ref[c, 1 : 1 + nx, OWN : OWN + ny, :] + push

    sums = []
    for edge, coef in ((edge_x.at[0], left), (edge_x.at[1], right), (edge_y.at[0], own), (edge_y.at[1], own)):
        side = coef[0:1, :] * edge[0]
        for t in range(1, turbines):
            side = side + coef[t : t + 1, :] * edge[t]
        sums.append(side)
    ix, iy = lax.axis_index("gx"), lax.axis_index("gy")
    for c in range(comps):
        for k, (a, b, there) in enumerate(((xo, xe, ix > 0), (xe, xo, ix < lax.axis_size("gx") - 1))):
            at = (c * 2 + 1 - k) * EDGE + 4
            x = k * (nx + 1)
            push = rounded(rounded(picked(ev_x, a, b, at, at + ny)) * sums[k])
            moved = update_ref[c, x, OWN : OWN + ny, :] + push
            field[c, x, OWN : OWN + ny, :] = jnp.where(there, moved, 0.0)
        for k, (a, b, there) in enumerate(((yo, ye, iy > 0), (ye, yo, iy < lax.axis_size("gy") - 1))):
            at = (c * 2 + 1 - k) * nx
            y = OWN - 1 + k * (ny + 1)
            push = rounded(rounded(picked(ev_y, a, b, at, at + nx)) * sums[2 + k])
            moved = update_ref[c, 1 : 1 + nx, y, :] + push
            field[c, 1 : 1 + nx, y, :] = jnp.where(there, moved, 0.0)
    for c in range(comps):
        now = field[c, 1 : 1 + nx, OWN : OWN + ny, :]
        out[c] = stencil(field, c, 1, nx, OWN, ny) + rounded(rounded(now) * second)


def body(velocity, tile_cells, owner, point_slot, point_z, loading):
    comps, nx, ny, levels = velocity.shape
    _, turbines, points = point_slot.shape
    slots = tile_cells.shape[2]
    tiles_y = lax.axis_size("gy")
    pieces = points // LANES
    rows_y = comps * 2 * nx + 8
    rows_x = comps * 2 * EDGE + 2 * pieces * turbines + 2 * turbines + 8
    args = (velocity, tile_cells, owner, point_slot, point_z, loading)
    work = {"flops": 2 * turbines * slots * points * levels, "nbytes": 1 << 20}

    def field(n, planes):
        return pltpu.VMEM((n, planes, PLANE, levels), F32)

    v, tc, own, slot, height, load, y_even, y_odd = call(
        stage,
        "stage",
        [(x.shape, x.dtype) for x in args] + [((rows_y, levels), F32)] * 2,
        args,
        [pltpu.SemaphoreType.DMA((len(args),))],
        space=pltpu.HBM,
    )
    ye, yo = swap(y_even, "gy", 0), swap(y_odd, "gy", 1)
    counts, loads, sums, scale, code = call(
        histogram,
        "histogram",
        [
            ((turbines, slots, levels), BF16),
            ((turbines, slots, levels), F32),
            ((turbines, levels), F32),
            ((turbines, levels), F32),
            ((turbines, points), F32),
        ],
        (v, tc, own, slot, height, load),
        **work,
    )
    x_even, x_odd = call(
        pack_x, "pack_x", [((rows_x, levels), F32)] * 2, (v, tc, ye, yo, sums, scale, code, load)
    )
    xe, xo = swap(x_even, "gx", 0), swap(x_odd, "gx", 1)

    def edges_y_of(*refs):
        return edges_y(slots, nx, ny, *refs)

    (edge_y,) = call(
        edges_y_of, "edges_y", [((2, turbines, nx, levels), F32)], (slot, height, load, ye, yo), **work
    )
    (chunk,) = call(
        reduce_sums,
        "reduce_sums",
        [((tiles_y, turbines, LANES), F32)],
        (v, tc, ye, yo, xe, xo, counts, loads, sums),
        [field(1, nx + 4), pltpu.VMEM((turbines + 1, slots, levels), BF16)],
    )
    got = lax.all_to_all(chunk, "gy", 0, 0)

    def edges_x_of(*refs):
        return edges_x(slots, pieces, *refs)

    edge_x, update = call(
        edges_x_of,
        "edges_x",
        [((2, turbines, ny, levels), F32), ((comps, nx + 2, PLANE, levels), F32)],
        (v, ye, yo, xe, xo),
        [field(comps, nx + 4)],
        **work,
    )

    def advance_by(*refs):
        return advance(points, *refs)

    (out,) = call(
        advance_by,
        "advance",
        [(velocity.shape, F32)],
        (got, v, tc, ye, yo, xe, xo, scale, loads, edge_x, edge_y, update),
        [field(comps, nx + 2), pltpu.VMEM((slots, 6 * levels), BF16)],
    )
    return out


def solution(mesh):
    in_specs = (
        P(None, "gx", "gy", None),
        P("gx", "gy", None),
        P("gx", None),
        P("gx", None, None),
        P("gx", None, None),
        P("gx", None, None),
    )
    out_specs = P(None, "gx", "gy", None)
    return jax.shard_map(body, mesh=mesh, in_specs=in_specs, out_specs=out_specs, check_vma=False)
```

time: 47 us -> 36.5 us (0.78); the launches traced: 46 us -> 36.1 us
  local copies, waits for them, and re-layouts: 13.6 us -> 4.52 us
  Pallas kernels: 14.8 us -> 12.2 us
  starting transfers between devices: 14.3 us -> 16 us
    unnamed x42 -> x12, local copies, waits for them, and re-layouts: 13.6 us -> 4.52 us
    pallas_call x6 -> x7, Pallas kernels: 14.8 us -> 12.2 us  [call(): pl.pallas_call(kernel, out_shape=[jax.ShapeDtypeStruct(s, d) for s, d in...]
    all_to_all x1, starting transfers between devices: 7.3 us -> 9.05 us  [body(): got = lax.all_to_all(chunk, 'gy', 0, 0)]
  transfers between devices with their start and end apart: 5 -> 5, of which waited for: 1 -> 1; matrix products, arithmetic and copies ran while one was open for 0% -> 0% of each run, Pallas kernels for 22% -> 24%
where the time goes in v2:
time: 36.5 us; the launch traced here: 36.1 us
  starting transfers between devices  16 us (44%)
  Pallas kernels  12.2 us (33%)
  local copies, waits for them, and re-layouts  4.52 us (12%)
  waiting for transfers between devices  3.23 us (9%)
    pallas_call x7, Pallas kernels, call(): pl.pallas_call(kernel, out_shape=[jax.ShapeDtypeStruct(s, d) for s, d in...  12.2 us
    all_to_all x1, starting transfers between devices, body(): got = lax.all_to_all(chunk, 'gy', 0, 0)  9.05 us
    ppermute x4, starting transfers between devices, swap(): return lax.ppermute(x, axis, swap_pairs(lax.axis_size(axis), first))  6.98 us
    unnamed x12, local copies, waits for them, and re-layouts  4.52 us
    ppermute x4, waiting for transfers between devices, swap(): return lax.ppermute(x, axis, swap_pairs(lax.axis_size(axis), first))  3.23 us
  transfers between devices with their start and end apart: 5, of which 1 were waited for; matrix products, arithmetic and copies ran while one was open for 0% of the time, Pallas kernels for 24%

profile of v2, /device:TPU:1, one launch (start us, length us, event | category | flops | bytes accessed | tf_op | source)
XLA Modules:
  0.0 36.1 jit_solution(5431611654580187624)
XLA Ops:
  0.0 0.0 copy-start
  0.0 1.0 %copy-done = f32[3,16,16,128]{3,2,1,0:T(8,128)S(1)} copy-done((f32[3,16,16,128]{3,2,1,0:T(8,128)S(1)}, f32[3,16,16,128]{3,2,1,0:T(8,128)}, u32[]{:S(2)}) %copy-start) | copy-done | bytes 393240
  1.0 0.0 copy-start.1
  1.0 0.7 %copy-done.1 = s32[1,16,384]{2,1,0:T(8,128)S(1)} copy-done((s32[1,16,384]{2,1,0:T(8,128)S(1)}, s32[1,16,384]{2,1,0:T(8,128)}, u32[]{:S(2)}) %copy-start.1) | copy-done | bytes 24600
  1.7 0.0 copy-start.2
  1.7 0.7 %copy-done.2 = s32[1,16,384]{2,1,0:T(8,128)S(1)} copy-done((s32[1,16,384]{2,1,0:T(8,128)S(1)}, s32[1,16,384]{2,1,0:T(8,128)}, u32[]{:S(2)}) %copy-start.2) | copy-done | bytes 24600
  2.5 0.0 copy-start.3
  2.5 0.7 %copy-done.3 = f32[1,16,384]{2,1,0:T(8,128)S(1)} copy-done((f32[1,16,384]{2,1,0:T(8,128)S(1)}, f32[1,16,384]{2,1,0:T(8,128)}, u32[]{:S(2)}) %copy-start.3) | copy-done | bytes 24600
  3.2 0.0 copy-start.4
  3.2 0.7 %copy-done.4 = s32[1,1,96]{2,1,0:T(1,128)S(1)} copy-done((s32[1,1,96]{2,1,0:T(1,128)S(1)}, s32[1,1,96]{2,1,0:T(1,128)}, u32[]{:S(2)}) %copy-start.4) | copy-done | bytes 408
  3.9 0.0 copy-start.5
  3.9 0.7 %copy-done.5 = s32[1,16]{1,0:T(1,128)S(1)} copy-done((s32[1,16]{1,0:T(1,128)S(1)}, s32[1,16]{1,0:T(1,128)}, u32[]{:S(2)}) %copy-start.5) | copy-done | bytes 88
  4.5 0.4 %stage.1 = (f32[3,16,16,128]{3,2,1,0:T(8,128)S(1)}, s32[1,1,96]{2,1,0:T(1,128)S(1)}, s32[1,16]{1,0:T(1,128)S(1)}, s32[1,16,384]{2,1,0:T(8,128)S(1)}, s32[1,16,38...) custom-call(f32[3,16,16,128]{3,2,1,0:T(8,128)S(1)} %copy-done, ...), custom_call_target="tpu_custom_call" | custom-call | tf_op jit(solution)/shard_map/stage/pallas_call | solution.py:63
  5.0 2.1 %collective-permute-start = (f32[104,128]{1,0:T(8,128)S(1)}, f32[104,128]{1,0:T(8,128)S(1)}, u32[]{:S(2)}, u32[]{:S(2)}) collective-permute-start(f32[104,128]{1,0:T(8,128)S(1)} %get-tuple-element.24), channel_id=1, source_target_pairs={{0,1},{1,0},{2,3},{3,2},{4,5},{5,4},{6,7},{7,6},{8,9},{9,8},{10,11... | collective-permute-start | bytes 159752 | tf_op jit(solution)/shard_map/ppermute | solution.py:59
  7.1 0.7 %collective-permute-start.1 = (f32[104,128]{1,0:T(8,128)S(1)}, f32[104,128]{1,0:T(8,128)S(1)}, u32[]{:S(2)}, u32[]{:S(2)}) collective-permute-start(f32[104,128]{1,0:T(8,128)S(1)} %get-tuple-element.25), channel_id=1, source_target_pairs={{1,2},{2,1},{3,4},{4,3},{5,6},{6,5},{9,10},{10,9},{11,12},{12,11},... | collective-permute-start | bytes 159752 | tf_op jit(solution)/shard_map/ppermute | solution.py:59
  7.8 1.8 %histogram.1 = (bf16[16,96,128]{2,1,0:T(8,128)(2,1)S(1)}, f32[16,96,128]{2,1,0:T(8,128)S(1)}, f32[16,128]{1,0:T(8,128)S(1)}, f32[16,128]{1,0:T(8,128)S(1)}, f32[16,384]{1,0:T(8,128)S(1)}) custom-call(f32[3,16,16,128]{3,2,1,0:T(8,128)S(1)} %get-tuple-element.22.v.refs_0_.refs_1_, s32[1,1,96]{2,1,0:T(1,128)S(1)} %get-tuple-element.23.tc.refs_2_, ...), custom_call_target="tpu_custom_call" | custom-call | flops 150994944 | bytes 1048576 | tf_op jit(solution)/shard_map/histogram/pallas_call | solution.py:63
  9.5 0.0 collective-permute-done.ye.refs_1_.refs_3_
  9.5 0.0 collective-permute-done.1.yo.refs_2_.refs_4_
  9.6 1.0 %collective-permute-start.2 = (f32[280,128]{1,0:T(8,128)S(1)}, f32[280,128]{1,0:T(8,128)S(1)}, u32[]{:S(2)}, u32[]{:S(2)}) collective-permute-start(f32[280,128]{1,0:T(8,128)S(1)} %get-tuple-element.33), channel_id=1, source_target_pairs={{0,8},{8,0},{16,24},{24,16},{1,9},{9,1},{17,25},{25,17},{2,10},{10... | collective-permute-start | bytes 430088 | tf_op jit(solution)/shard_map/ppermute | solution.py:59
  10.6 3.2 %collective-permute-start.3 = (f32[280,128]{1,0:T(8,128)S(1)}, f32[280,128]{1,0:T(8,128)S(1)}, u32[]{:S(2)}, u32[]{:S(2)}) collective-permute-start(f32[280,128]{1,0:T(8,128)S(1)} %get-tuple-element.34), channel_id=1, source_target_pairs={{8,16},{16,8},{9,17},{17,9},{10,18},{18,10},{11,19},{19,11},{12,20... | collective-permute-start | bytes 430088 | tf_op jit(solution)/shard_map/ppermute | solution.py:59
  13.8 0.0 collective-permute-done.2.xe.refs_3_.refs_5_
  13.8 3.2 %collective-permute-done.3.xo.refs_4_.refs_6_ = f32[280,128]{1,0:T(8,128)S(1)} collective-permute-done((f32[280,128]{1,0:T(8,128)S(1)}, f32[280,128]{1,0:T(8,128)S(1)}, u32[]{:S(2)}, u32[]{:S(2)}) %collective-permute-start.3) | collective-permute-done | bytes 143392 | tf_op jit(solution)/shard_map/ppermute | solution.py:59
  17.0 1.7 %reduce_sums.1 = f32[8,16,128]{2,1,0:T(8,128)} custom-call(f32[3,16,16,128]{3,2,1,0:T(8,128)S(1)} %get-tuple-element.22.v.refs_0_.refs_1_, s32[1,1,96]{2,1,0:T(1,128)S(1)} %get-tuple-element.23.tc.refs_2_, f32[104,128]{1,0:T(8,128)S(1)} %collective-permute-done.ye.refs_1_.refs_3_, f32[104,128]{1,0:T(8,128)S(1)} %collective-permute-done.1.yo.refs_2_.refs_4_, ...), custom_call_target="tpu_custom_call" | custom-call | tf_op jit(solution)/shard_map/reduce_sums/pallas_call | solution.py:63
  18.7 9.0 %all-to-all-start = ((f32[8,16,128]{2,1,0:T(8,128)}), f32[8,16,128]{2,1,0:T(8,128)S(1)}, u32[]{:S(2)}, u32[]{:S(2)}) async-start(f32[8,16,128]{2,1,0:T(8,128)} %reduce_sums.1), calls=%async_computation | async-start | bytes 131072 | tf_op jit(solution)/shard_map/all_to_all | solution.py:424
  27.8 2.4 %edges_y.1.refs_10_ = f32[2,16,16,128]{3,2,1,0:T(8,128)S(1)} custom-call(s32[1,16,384]{2,1,0:T(8,128)S(1)} %get-tuple-element.27.slot.refs_0_, s32[1,16,384]{2,1,0:T(8,128)S(1)} %get-tuple-element.28.height.refs_1_, f32[1,16,384]{2,1,0:T(8,128)S(1)} %get-tuple-element.29.load.refs_2_, f32[104,128]{1,0:T(8,128)S(1)} %collective-permute-done.ye.refs_1_.refs_3_, ...), custom_call_target="tpu_custom_call" | custom-call | flops 150994944 | bytes 1048576 | tf_op jit(solution)/shard_map/edges_y/pallas_call | solution.py:63
  30.1 4.4 %edges_x.1 = (f32[2,16,16,128]{3,2,1,0:T(8,128)S(1)}, f32[3,18,32,128]{3,2,1,0:T(8,128)S(1)}) custom-call(f32[3,16,16,128]{3,2,1,0:T(8,128)S(1)} %get-tuple-element.22.v.refs_0_.refs_1_, f32[104,128]{1,0:T(8,128)S(1)} %collective-permute-done.ye.refs_1_.refs_3_, f32[104,128]{1,0:T(8,128)S(1)} %collective-permute-done.1.yo.refs_2_.refs_4_, ...), custom_call_target="tpu_custom_call" | custom-call | flops 150994944 | bytes 1048576 | tf_op jit(solution)/shard_map/edges_x/pallas_call | solution.py:63
  34.6 0.0 all-to-all-done.refs_0_
  34.6 1.5 %advance.1 = f32[3,16,16,128]{3,2,1,0:T(8,128)} custom-call(f32[8,16,128]{2,1,0:T(8,128)S(1)} %all-to-all-done.refs_0_, f32[3,16,16,128]{3,2,1,0:T(8,128)S(1)} %get-tuple-element.22.v.refs_0_.refs_1_, s32[1,1,96]{2,1,0:T(1,128)S(1)} %get-tuple-element.23.tc.refs_2_, f32[104,128]{1,0:T(8,128)S(1)} %collective-permute-done.ye.refs_1_.refs_3_, ...), custom_call_target="tpu_custom_call" | custom-call | tf_op jit(solution)/shard_map/advance/pallas_call | solution.py:63
  (1 shorter events, 0.0 us)
Async XLA Ops:
  0.0 1.0 %copy-start = (f32[3,16,16,128]{3,2,1,0:T(8,128)S(1)}, f32[3,16,16,128]{3,2,1,0:T(8,128)}, u32[]{:S(2)}) copy-start(f32[3,16,16,128]{3,2,1,0:T(8,128)} %v_hbm.1) | copy-start | bytes 1179652
  1.0 0.7 %copy-start.1 = (s32[1,16,384]{2,1,0:T(8,128)S(1)}, s32[1,16,384]{2,1,0:T(8,128)}, u32[]{:S(2)}) copy-start(s32[1,16,384]{2,1,0:T(8,128)} %slot_hbm.1) | copy-start | bytes 73732
  1.7 0.7 %copy-start.2 = (s32[1,16,384]{2,1,0:T(8,128)S(1)}, s32[1,16,384]{2,1,0:T(8,128)}, u32[]{:S(2)}) copy-start(s32[1,16,384]{2,1,0:T(8,128)} %height_hbm.1) | copy-start | bytes 73732
  2.5 0.7 %copy-start.3 = (f32[1,16,384]{2,1,0:T(8,128)S(1)}, f32[1,16,384]{2,1,0:T(8,128)}, u32[]{:S(2)}) copy-start(f32[1,16,384]{2,1,0:T(8,128)} %load_hbm.1) | copy-start | bytes 73732
  3.2 0.7 %copy-start.4 = (s32[1,1,96]{2,1,0:T(1,128)S(1)}, s32[1,1,96]{2,1,0:T(1,128)}, u32[]{:S(2)}) copy-start(s32[1,1,96]{2,1,0:T(1,128)} %tc_hbm.1) | copy-start | bytes 1156
  3.9 0.7 %copy-start.5 = (s32[1,16]{1,0:T(1,128)S(1)}, s32[1,16]{1,0:T(1,128)}, u32[]{:S(2)}) copy-start(s32[1,16]{1,0:T(1,128)} %owner_hbm.1) | copy-start | bytes 196
  5.0 4.6 %collective-permute-start = (f32[104,128]{1,0:T(8,128)S(1)}, f32[104,128]{1,0:T(8,128)S(1)}, u32[]{:S(2)}, u32[]{:S(2)}) collective-permute-start(f32[104,128]{1,0:T(8,128)S(1)} %get-tuple-element.24), channel_id=1, source_target_pairs={{0,1},{1,0},{2,3},{3,2},{4,5},{5,4},{6,7},{7,6},{8,9},{9,8},{10,11... | collective-permute-start | bytes 159752 | tf_op jit(solution)/shard_map/ppermute | solution.py:59
  7.1 2.5 %collective-permute-start.1 = (f32[104,128]{1,0:T(8,128)S(1)}, f32[104,128]{1,0:T(8,128)S(1)}, u32[]{:S(2)}, u32[]{:S(2)}) collective-permute-start(f32[104,128]{1,0:T(8,128)S(1)} %get-tuple-element.25), channel_id=1, source_target_pairs={{1,2},{2,1},{3,4},{4,3},{5,6},{6,5},{9,10},{10,9},{11,12},{12,11},... | collective-permute-start | bytes 159752 | tf_op jit(solution)/shard_map/ppermute | solution.py:59
  9.6 4.2 %collective-permute-start.2 = (f32[280,128]{1,0:T(8,128)S(1)}, f32[280,128]{1,0:T(8,128)S(1)}, u32[]{:S(2)}, u32[]{:S(2)}) collective-permute-start(f32[280,128]{1,0:T(8,128)S(1)} %get-tuple-element.33), channel_id=1, source_target_pairs={{0,8},{8,0},{16,24},{24,16},{1,9},{9,1},{17,25},{25,17},{2,10},{10... | collective-permute-start | bytes 430088 | tf_op jit(solution)/shard_map/ppermute | solution.py:59
  10.6 6.4 %collective-permute-start.3 = (f32[280,128]{1,0:T(8,128)S(1)}, f32[280,128]{1,0:T(8,128)S(1)}, u32[]{:S(2)}, u32[]{:S(2)}) collective-permute-start(f32[280,128]{1,0:T(8,128)S(1)} %get-tuple-element.34), channel_id=1, source_target_pairs={{8,16},{16,8},{9,17},{17,9},{10,18},{18,10},{11,19},{19,11},{12,20... | collective-permute-start | bytes 430088 | tf_op jit(solution)/shard_map/ppermute | solution.py:59
  18.7 15.8 %all-to-all-start = ((f32[8,16,128]{2,1,0:T(8,128)}), f32[8,16,128]{2,1,0:T(8,128)S(1)}, u32[]{:S(2)}, u32[]{:S(2)}) async-start(f32[8,16,128]{2,1,0:T(8,128)} %reduce_sums.1), calls=%async_computation | async-start | bytes 131072 | tf_op jit(solution)/shard_map/all_to_all | solution.py:424

commit v3 on v2

v3 whole, which is shorter than its diff:
```python
import jax
import jax.numpy as jnp
from jax import lax
from jax.experimental import pallas as pl
from jax.experimental.pallas import tpu as pltpu
from jax.sharding import PartitionSpec as P

SPREAD = 0.12
CARRY = 0.25
FREE_WIND = 1.0
LOAD = 0.6

F32 = jnp.float32
BF16 = jnp.bfloat16
NT = (((1,), (1,)), ((), ()))
LANES = 128
OWN = 8
PLANE = 32
SUMS, SCALE, CELLS = 0, 1, 2


def iota(shape, axis):
    return lax.broadcasted_iota(jnp.int32, shape, axis)


def rounded(x):
    return x.astype(BF16).astype(F32)


def one_hot(count, row):
    places = iota((count, row.shape[1]), 0).astype(BF16)
    return places == row.astype(BF16)


def ones_at(mask):
    return jnp.where(mask, jnp.ones((), BF16), jnp.zeros((), BF16))


def pick_slots(tc, cells):
    slots = tc.shape[2]
    row = jnp.broadcast_to(tc[0, :, :].astype(F32), (slots, slots))
    same = iota((slots, slots), 0) == iota((slots, slots), 1)
    column = jnp.sum(jnp.where(same, row, 0.0), axis=1, keepdims=True).astype(jnp.int32)
    return jnp.where(iota((slots, cells), 1) == column, 1.0, 0.0).astype(BF16)


def even(axis):
    return lax.rem(lax.axis_index(axis), 2) == 0


def swap_pairs(count, first):
    pairs = []
    for i in range(first, count - 1, 2):
        pairs += [(i, i + 1), (i + 1, i)]
    return pairs


def swap(x, axis, first):
    return lax.ppermute(x, axis, swap_pairs(lax.axis_size(axis), first))


def call(kernel, name, outs, args, scratch=(), flops=0, nbytes=0, space=pltpu.VMEM):
    return pl.pallas_call(
        kernel,
        out_shape=[jax.ShapeDtypeStruct(s, d) for s, d in outs],
        in_specs=[pl.BlockSpec(memory_space=space)] * len(args),
        out_specs=[pl.BlockSpec(memory_space=pltpu.VMEM)] * len(outs),
        scratch_shapes=list(scratch),
        compiler_params=pltpu.CompilerParams(vmem_limit_bytes=16 << 20),
        cost_estimate=pl.CostEstimate(flops=flops, bytes_accessed=nbytes, transcendentals=0),
        name=name,
    )(*(pltpu.with_memory_space_constraint(a, space) if space is pltpu.HBM else a for a in args))


def lane_edge(center):
    axis = center.ndim - 1
    lane = iota(center.shape, axis)
    last = center.shape[axis] - 1
    below = jnp.where(lane == 0, 0.0, pltpu.roll(center, 1, axis))
    above = jnp.where(lane == last, 0.0, pltpu.roll(center, last, axis))
    return below + above


def moved(center, before, after, beside):
    beside = beside + before + after
    return center + SPREAD * (beside - 6.0 * center) - CARRY * (center - before)


def stencil(ref, c, x0, nx, ny):
    center = ref[c, x0 : x0 + nx, OWN : OWN + ny, :]
    before = ref[c, x0 - 1 : x0 - 1 + nx, OWN : OWN + ny, :]
    after = ref[c, x0 + 1 : x0 + 1 + nx, OWN : OWN + ny, :]
    beside = ref[c, x0 : x0 + nx, OWN - 1 : OWN - 1 + ny, :] + ref[c, x0 : x0 + nx, OWN + 1 : OWN + 1 + ny, :]
    return moved(center, before, after, beside + lane_edge(center))


def stage(v_hbm, tc_hbm, owner_hbm, slot_hbm, height_hbm, load_hbm, v, tc, owner, slot, height, load, to_even, to_odd, sems):
    pairs = ((v_hbm, v), (tc_hbm, tc), (slot_hbm, slot), (height_hbm, height), (load_hbm, load), (owner_hbm, owner))
    copies = [pltpu.make_async_copy(a, b, sems.at[i]) for i, (a, b) in enumerate(pairs)]
    for copy in copies:
        copy.start()
    copies[0].wait()
    comps, nx, ny, _ = v.shape
    ev = even("gy")
    at = 0
    for c in range(comps):
        for k in range(2):
            high = v[c, :, ny - 2 + k, :]
            low = v[c, :, k, :]
            to_even[at : at + nx, :] = jnp.where(ev, high, low)
            to_odd[at : at + nx, :] = jnp.where(ev, low, high)
            at += nx
    copies[1].wait()
    cells = tc[0, :, :].astype(F32) + 1.0
    slots = cells.shape[1]
    for out in (to_even, to_odd):
        out[at : at + 8, :] = jnp.zeros((8, LANES), F32)
        out[at : at + 1, 0:slots] = cells
    for copy in copies[2:]:
        copy.wait()


def as_column(row, n):
    same = iota((n, n), 0) == iota((n, n), 1)
    return jnp.sum(jnp.where(same, row, 0.0), axis=1, keepdims=True)


def as_row(column, n):
    same = iota((n, n), 0) == iota((n, n), 1)
    return jnp.sum(jnp.where(same, column, 0.0), axis=0, keepdims=True)


def picked(flag, a, b, lo, hi):
    return jnp.where(flag, a[lo:hi, :], b[lo:hi, :])


def histogram(v, tc, owner, slot, height, load, count_ref, load_ref, line, to_even, to_odd, sum_ref):
    _, turbines, points = slot.shape
    slots, levels = count_ref.shape[1:]
    comps, nx, ny, _ = v.shape
    cells = nx * ny
    first = lax.axis_index("gy") * slots
    values = v[0, :, :, :].reshape(cells, levels).astype(BF16)
    rows = jnp.dot(pick_slots(tc, cells), values, preferred_element_type=F32)
    zero = jnp.zeros((), BF16)
    for t in range(turbines):
        a = ones_at(one_hot(slots, slot[0, t : t + 1, :] - first))
        at_z = one_hot(levels, height[0, t : t + 1, :])
        weight = load[0, t : t + 1, :]
        high = weight.astype(BF16)
        low = (weight - high.astype(F32)).astype(BF16)
        b = jnp.concatenate([ones_at(at_z), jnp.where(at_z, high, zero), jnp.where(at_z, low, zero)], axis=0)
        both = lax.dot_general(a, b, NT, preferred_element_type=F32)
        count = both[:, :levels]
        count_ref[t] = count.astype(BF16)
        load_ref[t] = both[:, levels : 2 * levels] + both[:, 2 * levels :]
        sum_ref[t : t + 1, :] = jnp.sum(count * rows, axis=0, keepdims=True)

    owner_row = jnp.broadcast_to(owner[...].astype(F32), (turbines, turbines))
    member = owner_row == as_column(owner_row, turbines)
    load_row = as_row(jnp.sum(load[0, :, :], axis=1, keepdims=True), turbines)
    total = jnp.sum(jnp.where(member, load_row, 0.0), axis=1, keepdims=True)
    number = jnp.sum(jnp.where(member, 1.0, 0.0), axis=1, keepdims=True)
    line[...] = jnp.zeros((8, LANES), F32)
    line[SUMS : SUMS + 1, 0:turbines] = as_row(jnp.sum(sum_ref[...], axis=1, keepdims=True), turbines)
    line[SCALE : SCALE + 1, 0:turbines] = as_row(LOAD / (total / (number * points)), turbines)
    line[CELLS : CELLS + 1, 0:slots] = tc[0, :, :].astype(F32) + 1.0

    local = slot[0, :, :] - first
    inside = (local >= 0) & (local < slots)
    code = jnp.where(inside, local * levels + height[0, :, :] + 1, 0).astype(F32)
    ev = even("gx")
    at = 0
    for c in range(comps):
        for k in range(2):
            right, left = v[c, nx - 2 + k, :, :], v[c, k, :, :]
            to_even[at : at + ny, :] = jnp.where(ev, right, left)
            to_odd[at : at + ny, :] = jnp.where(ev, left, right)
            at += ny
    for part in (code, load[0, :, :]):
        for k in range(0, points, LANES):
            for out in (to_even, to_odd):
                out[at : at + turbines, :] = part[:, k : k + LANES]
            at += turbines
    for out in (to_even, to_odd):
        out[at : at + 8, :] = line[...]


def extend(v, ye, yo, xe, xo, field, comps):
    _, nx, ny, _ = v.shape
    ev_x, ev_y = even("gx"), even("gy")
    for c in comps:
        out = c if len(comps) > 1 else 0
        field[out, 2 : 2 + nx, OWN : OWN + ny, :] = v[c, :, :, :]
        for k in range(2):
            at = (c * 2 + k) * nx
            field[out, 2 : 2 + nx, OWN - 2 + k, :] = picked(ev_y, yo, ye, at, at + nx)
            field[out, 2 : 2 + nx, OWN + ny + k, :] = picked(ev_y, ye, yo, at, at + nx)
            at = (c * 2 + k) * ny
            for x, a, b in ((k, xo, xe), (2 + nx + k, xe, xo)):
                field[out, x, 0:OWN, :] = jnp.zeros((OWN, LANES), F32)
                field[out, x, OWN + ny : PLANE, :] = jnp.zeros((PLANE - OWN - ny, LANES), F32)
                field[out, x, OWN : OWN + ny, :] = picked(ev_x, a, b, at, at + ny)


def spread(wheres, hits, z, weight):
    high = weight.astype(BF16)
    low = (weight - high.astype(F32)).astype(BF16)
    at_z = ones_at(one_hot(LANES, z))
    left = []
    for where, hit in zip(wheres, hits):
        place = jnp.dot(where, hit, preferred_element_type=F32).astype(BF16)
        left += [place * high, place * low]
    both = lax.dot_general(jnp.concatenate(left, axis=0), at_z, NT, preferred_element_type=F32)
    n = wheres[0].shape[0]
    return [both[2 * k * n : (2 * k + 1) * n] + both[(2 * k + 1) * n : (2 * k + 2) * n] for k in range(len(wheres))]


def beside(v, tc, slot, height, load, ye, yo, counts, loads, edge_ref, couple, products):
    _, turbines, slots, levels = (0,) + counts.shape
    _, nx, ny, _ = v.shape
    cells = nx * ny
    rows = jnp.dot(
        pick_slots(tc, cells), v[0, :, :, :].reshape(cells, levels).astype(BF16), preferred_element_type=F32
    )
    for t in range(turbines):
        products[t] = (rows * loads[t]).astype(BF16)
    block = 16
    wide = turbines * block
    gram = jnp.zeros((wide, wide), F32)
    for b in range(0, slots, block):
        left = counts[:, b : b + block, :].reshape(wide, levels)
        right = products[:, b : b + block, :].reshape(wide, levels)
        gram = gram + lax.dot_general(left, right, NT, preferred_element_type=F32)
    keep = (iota((wide, wide), 0) & (block - 1)) == (iota((wide, wide), 1) & (block - 1))
    gram = jnp.sum(jnp.where(keep, gram, 0.0).reshape(turbines, block, wide), axis=1)
    select = jnp.where(iota((wide, LANES), 0) // block == iota((wide, LANES), 1), 1.0, 0.0)
    couple[...] = jnp.dot(gram, select, precision=lax.Precision.HIGHEST, preferred_element_type=F32)

    ev = even("gy")
    me = lax.axis_index("gy")
    at = ye.shape[0] - 8
    wheres = []
    for a, b, y in ((yo, ye, ny - 1), (ye, yo, 0)):
        cell = picked(ev, a, b, at, at + 1)[:, :slots].astype(jnp.int32) - 1
        wheres.append(jnp.where(iota((nx, slots), 0) * ny + y == cell, 1.0, 0.0).astype(BF16))
    for t in range(turbines):
        row = slot[0, t : t + 1, :]
        hits = [ones_at(one_hot(slots, row - (me + k) * slots)) for k in (-1, 1)]
        edge_ref[0, t], edge_ref[1, t] = spread(wheres, hits, height[0, t : t + 1, :], load[0, t : t + 1, :])


def reduce_sums(v, tc, ye, yo, xe, xo, counts, line, couple, out, field, sums):
    _, nx, ny, levels = v.shape
    comps = v.shape[0]
    turbines = counts.shape[0]
    cells = nx * ny
    extend(v, ye, yo, xe, xo, field, (0,))
    update = stencil(field, 0, 2, nx, ny).reshape(cells, levels).astype(BF16)
    rows = jnp.dot(pick_slots(tc, cells), update, preferred_element_type=F32)
    for t in range(turbines):
        sums[t : t + 1, :] = jnp.sum(counts[t].astype(F32) * rows, axis=0, keepdims=True)
    lane = iota((turbines, LANES), 1)
    ev_x = even("gx")
    at = xe.shape[0] - 8 + SUMS
    result = jnp.where(lane == turbines, jnp.sum(sums[...], axis=1, keepdims=True), couple[...])
    rows_of = (line[SUMS : SUMS + 1, :], picked(ev_x, xo, xe, at, at + 1), picked(ev_x, xe, xo, at, at + 1))
    for k, row in enumerate(rows_of):
        result = jnp.where(lane == turbines + 1 + k, as_column(row[:, :turbines], turbines), result)
    me = lax.axis_index("gy")
    for k in range(out.shape[0]):
        out[k, 0:turbines, :] = result
        out[k, turbines : turbines + 8, :] = jnp.zeros((8, LANES), F32)
    above = []
    below = []
    for c in range(comps):
        for a, b, at in ((xo, xe, (c * 2 + 1) * ny), (xe, xo, c * 2 * ny)):
            above.append(picked(ev_x, a, b, at + ny - 1, at + ny))
            below.append(picked(ev_x, a, b, at, at + 1))
    for i in range(2 * comps):
        for k in range(out.shape[0]):
            out[k, turbines + i : turbines + i + 1, :] = jnp.where(me + 1 == k, above[i], below[i])


def edges_x(slots, pieces, v, ye, yo, xe, xo, edge_ref, update_ref, strip_ref, field):
    comps, nx, ny, levels = v.shape
    turbines = edge_ref.shape[1]
    ev, ev_y = even("gx"), even("gy")
    extend(v, ye, yo, xe, xo, field, tuple(range(comps)))
    ends = iota((nx, LANES), 0)
    for c in range(comps):
        update_ref[c] = stencil(field, c, 1, nx + 2, ny)
        for k, (a, b, y) in enumerate(((yo, ye, 0), (ye, yo, ny - 1))):
            near, far = (c * 2 + 1 - k) * nx, (c * 2 + k) * nx
            center = picked(ev_y, a, b, near, near + nx)
            before = jnp.where(ends == 0, 0.0, pltpu.roll(center, 1, 0))
            after = jnp.where(ends == nx - 1, 0.0, pltpu.roll(center, nx - 1, 0))
            others = picked(ev_y, a, b, far, far + nx) + v[c, :, y, :] + lane_edge(center)
            strip_ref[c, k] = moved(center, before, after, others)

    at = xe.shape[0] - 8 + CELLS
    code_at = comps * 2 * ny
    load_at = code_at + pieces * turbines
    shift = levels.bit_length() - 1
    for k, (a, b) in enumerate(((xo, xe), (xe, xo))):
        cell = picked(ev, a, b, at, at + 1)[:, :slots].astype(jnp.int32) - 1
        where = jnp.where(iota((ny, slots), 0) + (1 - k) * (nx - 1) * ny == cell, 1.0, 0.0).astype(BF16)
        codes = [picked(ev, a, b, code_at + i * turbines, code_at + (i + 1) * turbines) for i in range(pieces)]
        codes = jnp.concatenate(codes, axis=1).astype(jnp.int32) - 1
        there = [picked(ev, a, b, load_at + i * turbines, load_at + (i + 1) * turbines) for i in range(pieces)]
        there = jnp.concatenate(there, axis=1)
        for t in range(turbines):
            code = codes[t : t + 1, :]
            hit = ones_at(one_hot(slots, code >> shift))
            (edge_ref[k, t],) = spread([where], [hit], code & (levels - 1), there[t : t + 1, :])


def advance(points, got, v, tc, ye, yo, xe, xo, line, loads, edge_x, edge_y, update_ref, strip_ref, out, field, parts):
    comps, nx, ny, levels = v.shape
    turbines, slots, _ = loads.shape
    cells = nx * ny
    ev_x, ev_y = even("gx"), even("gy")
    total = got[0, 0:turbines, :]
    for k in range(1, got.shape[0]):
        total = total + got[k, 0:turbines, :]
    lane = iota((turbines, LANES), 1)

    def column(k):
        return jnp.sum(jnp.where(lane == k, total, 0.0), axis=1, keepdims=True)

    def coefs(scales, sums):
        return -(scales * (FREE_WIND + sums / points))

    at = xe.shape[0] - 8 + SCALE
    scale = as_column(line[SCALE : SCALE + 1, :turbines], turbines)
    own = coefs(scale, column(turbines + 1))
    left = coefs(as_column(picked(ev_x, xo, xe, at, at + 1)[:, :turbines], turbines), column(turbines + 2))
    right = coefs(as_column(picked(ev_x, xe, xo, at, at + 1)[:, :turbines], turbines), column(turbines + 3))
    own_row = jnp.sum(jnp.where(iota((turbines, LANES), 0) == lane, own, 0.0), axis=0, keepdims=True)
    forced = jnp.sum(jnp.where(lane < turbines, total * own_row, 0.0), axis=1, keepdims=True)
    later = coefs(scale, column(turbines) + forced)

    for s in range(0, slots, 16):
        first = jnp.zeros((16, levels), F32)
        second = first
        for t in range(turbines):
            part = loads[t, s : s + 16, :]
            first = first + own[t : t + 1, :] * part
            second = second + later[t : t + 1, :] * part
        for i, rest in enumerate((first, second)):
            for k in range(3):
                piece = rest.astype(BF16)
                rest = rest - piece.astype(F32)
                at = (3 * i + k) * levels
                parts[s : s + 16, at : at + levels] = piece
    row = tc[0, :, :]
    put = jnp.where(iota((cells, slots), 0) == row, 1.0, 0.0).astype(BF16)
    spread_out = jnp.dot(put, parts[...], preferred_element_type=F32)
    pieces = [spread_out[:, k * levels : (k + 1) * levels] for k in range(6)]
    first = ((pieces[0] + pieces[1]) + pieces[2]).reshape(nx, ny, levels)
    second = ((pieces[3] + pieces[4]) + pieces[5]).reshape(nx, ny, levels)
    for c in range(comps):
        push = rounded(rounded(v[c, :, :, :]) * first)
        field[c, 1 : 1 + nx, OWN : OWN + ny, :] = update_ref[c, 1 : 1 + nx, :, :] + push

    sums = []
    for edge, coef in ((edge_x.at[0], left), (edge_x.at[1], right), (edge_y.at[0], own), (edge_y.at[1], own)):
        side = coef[0:1, :] * edge[0]
        for t in range(1, turbines):
            side = side + coef[t : t + 1, :] * edge[t]
        sums.append(side)
    ix, iy = lax.axis_index("gx"), lax.axis_index("gy")
    last_y = lax.axis_size("gy") - 1
    there_x = (ix > 0, ix < lax.axis_size("gx") - 1)
    there_y = (iy > 0, iy < last_y)
    beside_y = (jnp.maximum(iy - 1, 0), jnp.minimum(iy + 1, last_y))
    corner_rows = [jnp.where(there_y[k], got[beside_y[k], turbines : turbines + 8, :], 0.0) for k in range(2)]
    row_x, row_y = iota((nx, LANES), 0), iota((ny, LANES), 0)
    for c in range(comps):
        corner = [[corner_rows[y][c * 2 + x : c * 2 + x + 1, :] for y in range(2)] for x in range(2)]
        for k, (a, b) in enumerate(((xo, xe), (xe, xo))):
            at = (c * 2 + 1 - k) * ny
            x = k * (nx + 1)
            push = rounded(rounded(picked(ev_x, a, b, at, at + ny)) * sums[k])
            extra = jnp.where(row_y == 0, corner[k][0], 0.0) + jnp.where(row_y == ny - 1, corner[k][1], 0.0)
            value = update_ref[c, x, :, :] + SPREAD * extra + push
            field[c, x, OWN : OWN + ny, :] = jnp.where(there_x[k], value, 0.0)
        for k, (a, b) in enumerate(((yo, ye), (ye, yo))):
            at = (c * 2 + 1 - k) * nx
            y = OWN - 1 + k * (ny + 1)
            push = rounded(rounded(picked(ev_y, a, b, at, at + nx)) * sums[2 + k])
            extra = jnp.where(row_x == 0, (SPREAD + CARRY) * corner[0][k], 0.0)
            extra = extra + jnp.where(row_x == nx - 1, SPREAD * corner[1][k], 0.0)
            value = strip_ref[c, k] + extra + push
            field[c, 1 : 1 + nx, y, :] = jnp.where(there_y[k], value, 0.0)
    for c in range(comps):
        now = field[c, 1 : 1 + nx, OWN : OWN + ny, :]
        out[c] = stencil(field, c, 1, nx, ny) + rounded(rounded(now) * second)


def body(velocity, tile_cells, owner, point_slot, point_z, loading):
    comps, nx, ny, levels = velocity.shape
    _, turbines, points = point_slot.shape
    slots = tile_cells.shape[2]
    tiles_y = lax.axis_size("gy")
    pieces = points // LANES
    rows_y = comps * 2 * nx + 8
    rows_x = comps * 2 * ny + 2 * pieces * turbines + 8
    args = (velocity, tile_cells, owner, point_slot, point_z, loading)
    work = {"flops": 26 * turbines * slots * points * levels, "nbytes": 1 << 20}

    def field(n, planes):
        return pltpu.VMEM((n, planes, PLANE, levels), F32)

    v, tc, own, slot, height, load, y_even, y_odd = call(
        stage,
        "stage",
        [(x.shape, x.dtype) for x in args] + [((rows_y, levels), F32)] * 2,
        args,
        [pltpu.SemaphoreType.DMA((len(args),))],
        space=pltpu.HBM,
    )
    yo, ye = swap(y_odd, "gy", 1), swap(y_even, "gy", 0)
    counts, loads, line, x_even, x_odd = call(
        histogram,
        "histogram",
        [
            ((turbines, slots, levels), BF16),
            ((turbines, slots, levels), F32),
            ((8, LANES), F32),
            ((rows_x, levels), F32),
            ((rows_x, levels), F32),
        ],
        (v, tc, own, slot, height, load),
        [pltpu.VMEM((turbines, levels), F32)],
        **work,
    )
    xo, xe = swap(x_odd, "gx", 1), swap(x_even, "gx", 0)
    edge_y, couple = call(
        beside,
        "beside",
        [((2, turbines, nx, levels), F32), ((turbines, LANES), F32)],
        (v, tc, slot, height, load, ye, yo, counts, loads),
        [pltpu.VMEM((turbines, slots, levels), BF16)],
        **work,
    )
    (chunk,) = call(
        reduce_sums,
        "reduce_sums",
        [((tiles_y, turbines + 8, LANES), F32)],
        (v, tc, ye, yo, xe, xo, counts, line, couple),
        [field(1, nx + 4), pltpu.VMEM((turbines, levels), F32)],
    )
    got = lax.all_to_all(chunk, "gy", 0, 0)

    def edges_x_of(*refs):
        return edges_x(slots, pieces, *refs)

    edge_x, update, strip = call(
        edges_x_of,
        "edges_x",
        [
            ((2, turbines, ny, levels), F32),
            ((comps, nx + 2, ny, levels), F32),
            ((comps, 2, nx, levels), F32),
        ],
        (v, ye, yo, xe, xo),
        [field(comps, nx + 4)],
        **work,
    )

    def advance_by(*refs):
        return advance(points, *refs)

    (out,) = call(
        advance_by,
        "advance",
        [(velocity.shape, F32)],
        (got, v, tc, ye, yo, xe, xo, line, loads, edge_x, edge_y, update, strip),
        [field(comps, nx + 2), pltpu.VMEM((slots, 6 * levels), BF16)],
    )
    return out


def solution(mesh):
    in_specs = (
        P(None, "gx", "gy", None),
        P("gx", "gy", None),
        P("gx", None),
        P("gx", None, None),
        P("gx", None, None),
        P("gx", None, None),
    )
    out_specs = P(None, "gx", "gy", None)
    return jax.shard_map(body, mesh=mesh, in_specs=in_specs, out_specs=out_specs, check_vma=False)
```

time: 36.5 us -> 29.5 us (0.81)
  the two profiles are of different devices: /device:TPU:1 before, /device:TPU:0 now
where the time goes in v3:
time: 29.5 us; the launch traced here: 29.2 us
  Pallas kernels  13.3 us (45%)
  starting transfers between devices  13 us (44%)
  waiting for transfers between devices  2.85 us (10%)
    pallas_call x6, Pallas kernels, call(): pl.pallas_call(kernel, out_shape=[jax.ShapeDtypeStruct(s, d) for s, d in...  13.3 us
    all_to_all x1, starting transfers between devices, body(): got = lax.all_to_all(chunk, 'gy', 0, 0)  8.57 us
    ppermute x4, starting transfers between devices, swap(): return lax.ppermute(x, axis, swap_pairs(lax.axis_size(axis), first))  4.39 us
    all_to_all x1, waiting for transfers between devices, body(): got = lax.all_to_all(chunk, 'gy', 0, 0)  2.84 us
  transfers between devices with their start and end apart: 5, of which 1 were waited for; matrix products, arithmetic and copies ran while one was open for 0% of the time, Pallas kernels for 33%

profile of v3, /device:TPU:0, one launch (start us, length us, event | category | flops | bytes accessed | tf_op | source)
XLA Modules:
  0.0 29.2 jit_solution(18237360033297778232)
XLA Ops:
  0.0 1.1 %stage.1 = (f32[3,16,16,128]{3,2,1,0:T(8,128)S(1)}, s32[1,1,96]{2,1,0:T(1,128)S(1)}, s32[1,16]{1,0:T(1,128)S(1)}, s32[1,16,384]{2,1,0:T(8,128)S(1)}, s32[1,16,38...) custom-call(f32[3,16,16,128]{3,2,1,0:T(8,128)} %v_hbm.1, ...), custom_call_target="tpu_custom_call" | custom-call | tf_op jit(solution)/shard_map/stage/pallas_call | solution.py:63
  1.1 3.0 %collective-permute-start = (f32[104,128]{1,0:T(8,128)S(1)}, f32[104,128]{1,0:T(8,128)S(1)}, u32[]{:S(2)}, u32[]{:S(2)}) collective-permute-start(f32[104,128]{1,0:T(8,128)S(1)} %get-tuple-element.25), channel_id=1, source_target_pairs={{0,1},{1,0},{2,3},{3,2},{4,5},{5,4},{6,7},{7,6},{8,9},{9,8},{10,11... | collective-permute-start | bytes 159752 | tf_op jit(solution)/shard_map/ppermute | solution.py:59
  4.2 0.7 %collective-permute-start.1 = (f32[104,128]{1,0:T(8,128)S(1)}, f32[104,128]{1,0:T(8,128)S(1)}, u32[]{:S(2)}, u32[]{:S(2)}) collective-permute-start(f32[104,128]{1,0:T(8,128)S(1)} %get-tuple-element.26), channel_id=1, source_target_pairs={{1,2},{2,1},{3,4},{4,3},{5,6},{6,5},{9,10},{10,9},{11,12},{12,11},... | collective-permute-start | bytes 159752 | tf_op jit(solution)/shard_map/ppermute | solution.py:59
  4.8 1.8 %histogram.1 = (bf16[16,96,128]{2,1,0:T(8,128)(2,1)S(1)}, f32[16,96,128]{2,1,0:T(8,128)S(1)}, f32[8,128]{1,0:T(8,128)S(1)}, f32[200,128]{1,0:T(8,128)S(1)}, f32[200,128]{1,0:T(8,128)S(1)}) custom-call(f32[3,16,16,128]{3,2,1,0:T(8,128)S(1)} %get-tuple-element.23.v.refs_0_.refs_1_, s32[1,1,96]{2,1,0:T(1,128)S(1)} %get-tuple-element.24.tc.refs_2_, ...), custom_call_target="tpu_custom_call" | custom-call | flops 1962934272 | bytes 1048576 | tf_op jit(solution)/shard_map/histogram/pallas_call | solution.py:63
  6.7 0.0 collective-permute-start.2
  6.7 0.7 %collective-permute-start.3 = (f32[200,128]{1,0:T(8,128)S(1)}, f32[200,128]{1,0:T(8,128)S(1)}, u32[]{:S(2)}, u32[]{:S(2)}) collective-permute-start(f32[200,128]{1,0:T(8,128)S(1)} %get-tuple-element.32), channel_id=1, source_target_pairs={{8,16},{16,8},{9,17},{17,9},{10,18},{18,10},{11,19},{19,11},{12,20... | collective-permute-start | bytes 307208 | tf_op jit(solution)/shard_map/ppermute | solution.py:59
  7.4 0.0 collective-permute-done.ye.refs_1_.refs_3_
  7.4 0.0 collective-permute-done.1.yo.refs_2_.refs_4_
  7.4 3.3 %beside.1 = (f32[2,16,16,128]{3,2,1,0:T(8,128)S(1)}, f32[16,128]{1,0:T(8,128)S(1)}) custom-call(f32[3,16,16,128]{3,2,1,0:T(8,128)S(1)} %get-tuple-element.23.v.refs_0_.refs_1_, s32[1,1,96]{2,1,0:T(1,128)S(1)} %get-tuple-element.24.tc.refs_2_, s32[1,16,384]{2,1,0:T(8,128)S(1)} %get-tuple-element.28.slot, s32[1,16,384]{2,1,0:T(8,128)S(1)} %get-tuple-element.29.height, ...), custom_call_target="tpu_custom_call" | custom-call | flops 1962934272 | bytes 1048576 | tf_op jit(solution)/shard_map/beside/pallas_call | solution.py:63
  10.7 0.0 collective-permute-done.2.xe.refs_3_.refs_5_
  10.7 0.0 collective-permute-done.3.xo.refs_4_.refs_6_
  10.7 1.1 %reduce_sums.1 = f32[8,24,128]{2,1,0:T(8,128)} custom-call(f32[3,16,16,128]{3,2,1,0:T(8,128)S(1)} %get-tuple-element.23.v.refs_0_.refs_1_, s32[1,1,96]{2,1,0:T(1,128)S(1)} %get-tuple-element.24.tc.refs_2_, f32[104,128]{1,0:T(8,128)S(1)} %collective-permute-done.ye.refs_1_.refs_3_, f32[104,128]{1,0:T(8,128)S(1)} %collective-permute-done.1.yo.refs_2_.refs_4_, ...), custom_call_target="tpu_custom_call" | custom-call | tf_op jit(solution)/shard_map/reduce_sums/pallas_call | solution.py:63
  11.9 8.6 %all-to-all-start = ((f32[8,24,128]{2,1,0:T(8,128)}), f32[8,24,128]{2,1,0:T(8,128)S(1)}, u32[]{:S(2)}, u32[]{:S(2)}) async-start(f32[8,24,128]{2,1,0:T(8,128)} %reduce_sums.1), calls=%async_computation | async-start | bytes 196608 | tf_op jit(solution)/shard_map/all_to_all | solution.py:454
  20.4 4.4 %edges_x.1 = (f32[2,16,16,128]{3,2,1,0:T(8,128)S(1)}, f32[3,18,16,128]{3,2,1,0:T(8,128)S(1)}, f32[3,2,16,128]{3,2,1,0:T(8,128)S(1)}) custom-call(f32[3,16,16,128]{3,2,1,0:T(8,128)S(1)} %get-tuple-element.23.v.refs_0_.refs_1_, f32[104,128]{1,0:T(8,128)S(1)} %collective-permute-done.ye.refs_1_.refs_3_, ...), custom_call_target="tpu_custom_call" | custom-call | flops 1962934272 | bytes 1048576 | tf_op jit(solution)/shard_map/edges_x/pallas_call | solution.py:63
  24.8 2.8 %all-to-all-done.refs_0_ = f32[8,24,128]{2,1,0:T(8,128)S(1)} async-done(((f32[8,24,128]{2,1,0:T(8,128)}), f32[8,24,128]{2,1,0:T(8,128)S(1)}, u32[]{:S(2)}, u32[]{:S(2)}) %all-to-all-start) | async-done | bytes 98336 | tf_op jit(solution)/shard_map/all_to_all | solution.py:454
  27.6 1.5 %advance.1 = f32[3,16,16,128]{3,2,1,0:T(8,128)} custom-call(f32[8,24,128]{2,1,0:T(8,128)S(1)} %all-to-all-done.refs_0_, f32[3,16,16,128]{3,2,1,0:T(8,128)S(1)} %get-tuple-element.23.v.refs_0_.refs_1_, s32[1,1,96]{2,1,0:T(1,128)S(1)} %get-tuple-element.24.tc.refs_2_, f32[104,128]{1,0:T(8,128)S(1)} %collective-permute-done.ye.refs_1_.refs_3_, ...), custom_call_target="tpu_custom_call" | custom-call | tf_op jit(solution)/shard_map/advance/pallas_call | solution.py:63
Async XLA Ops:
  1.1 6.2 %collective-permute-start = (f32[104,128]{1,0:T(8,128)S(1)}, f32[104,128]{1,0:T(8,128)S(1)}, u32[]{:S(2)}, u32[]{:S(2)}) collective-permute-start(f32[104,128]{1,0:T(8,128)S(1)} %get-tuple-element.25), channel_id=1, source_target_pairs={{0,1},{1,0},{2,3},{3,2},{4,5},{5,4},{6,7},{7,6},{8,9},{9,8},{10,11... | collective-permute-start | bytes 159752 | tf_op jit(solution)/shard_map/ppermute | solution.py:59
  4.2 3.2 %collective-permute-start.1 = (f32[104,128]{1,0:T(8,128)S(1)}, f32[104,128]{1,0:T(8,128)S(1)}, u32[]{:S(2)}, u32[]{:S(2)}) collective-permute-start(f32[104,128]{1,0:T(8,128)S(1)} %get-tuple-element.26), channel_id=1, source_target_pairs={{1,2},{2,1},{3,4},{4,3},{5,6},{6,5},{9,10},{10,9},{11,12},{12,11},... | collective-permute-start | bytes 159752 | tf_op jit(solution)/shard_map/ppermute | solution.py:59
  6.7 4.1 %collective-permute-start.2 = (f32[200,128]{1,0:T(8,128)S(1)}, f32[200,128]{1,0:T(8,128)S(1)}, u32[]{:S(2)}, u32[]{:S(2)}) collective-permute-start(f32[200,128]{1,0:T(8,128)S(1)} %get-tuple-element.31), channel_id=1, source_target_pairs={{0,8},{8,0},{16,24},{24,16},{1,9},{9,1},{17,25},{25,17},{2,10},{10... | collective-permute-start | bytes 307208 | tf_op jit(solution)/shard_map/ppermute | solution.py:59
  6.7 4.0 %collective-permute-start.3 = (f32[200,128]{1,0:T(8,128)S(1)}, f32[200,128]{1,0:T(8,128)S(1)}, u32[]{:S(2)}, u32[]{:S(2)}) collective-permute-start(f32[200,128]{1,0:T(8,128)S(1)} %get-tuple-element.32), channel_id=1, source_target_pairs={{8,16},{16,8},{9,17},{17,9},{10,18},{18,10},{11,19},{19,11},{12,20... | collective-permute-start | bytes 307208 | tf_op jit(solution)/shard_map/ppermute | solution.py:59
  11.9 15.8 %all-to-all-start = ((f32[8,24,128]{2,1,0:T(8,128)}), f32[8,24,128]{2,1,0:T(8,128)S(1)}, u32[]{:S(2)}, u32[]{:S(2)}) async-start(f32[8,24,128]{2,1,0:T(8,128)} %reduce_sums.1), calls=%async_computation | async-start | bytes 196608 | tf_op jit(solution)/shard_map/all_to_all | solution.py:454

commit v4 on v3

--- a/solution.py
+++ b/solution.py
@@ -16,6 +16,7 @@
 LANES = 128
 OWN = 8
 PLANE = 32
+NO_SLOT = -30000.0
 SUMS, SCALE, CELLS = 0, 1, 2
 
 
@@ -186,7 +187,7 @@
         out[at : at + 8, :] = line[...]
 
 
-def extend(v, ye, yo, xe, xo, field, comps):
+def extend(v, yo, ye, xo, xe, field, comps):
     _, nx, ny, _ = v.shape
     ev_x, ev_y = even("gx"), even("gy")
     for c in comps:
@@ -203,28 +204,47 @@
                 field[out, x, OWN : OWN + ny, :] = picked(ev_x, a, b, at, at + ny)
 
 
-def spread(wheres, hits, z, weight):
+def edge_slots(cell_row, cells):
+    n, slots = cells.shape[0], cell_row.shape[1]
+    slot = iota((n, slots), 1).astype(F32)
+    return jnp.max(jnp.where(cell_row == cells, slot, NO_SLOT), axis=1, keepdims=True).astype(BF16)
+
+
+def spread(places, z, weight):
     high = weight.astype(BF16)
     low = (weight - high.astype(F32)).astype(BF16)
+    zero = jnp.zeros((), BF16)
     at_z = ones_at(one_hot(LANES, z))
     left = []
-    for where, hit in zip(wheres, hits):
-        place = jnp.dot(where, hit, preferred_element_type=F32).astype(BF16)
-        left += [place * high, place * low]
+    for edge, slot in places:
+        here = edge == slot.astype(BF16)
+        left += [jnp.where(here, high, zero), jnp.where(here, low, zero)]
     both = lax.dot_general(jnp.concatenate(left, axis=0), at_z, NT, preferred_element_type=F32)
-    n = wheres[0].shape[0]
-    return [both[2 * k * n : (2 * k + 1) * n] + both[(2 * k + 1) * n : (2 * k + 2) * n] for k in range(len(wheres))]
-
-
-def beside(v, tc, slot, height, load, ye, yo, counts, loads, edge_ref, couple, products):
-    _, turbines, slots, levels = (0,) + counts.shape
+    n = both.shape[0] // len(left)
+    return [both[2 * k * n : (2 * k + 1) * n] + both[(2 * k + 1) * n : (2 * k + 2) * n] for k in range(len(places))]
+
+
+def beside(v, tc, yo, ye, counts, loads, couple, edge_counts, products, field, sums):
+    turbines, slots, levels = counts.shape
     _, nx, ny, _ = v.shape
     cells = nx * ny
-    rows = jnp.dot(
-        pick_slots(tc, cells), v[0, :, :, :].reshape(cells, levels).astype(BF16), preferred_element_type=F32
-    )
+    ev = even("gy")
+    field[0, 1 : 1 + nx, OWN : OWN + ny, :] = v[0, :, :, :]
+    field[0, 1 : 1 + nx, OWN - 1, :] = picked(ev, yo, ye, nx, 2 * nx)
+    field[0, 1 : 1 + nx, OWN + ny, :] = picked(ev, ye, yo, 0, nx)
+    for x in (0, nx + 1):
+        field[0, x, OWN : OWN + ny, :] = jnp.zeros((ny, levels), F32)
+    update = stencil(field, 0, 1, nx, ny).reshape(cells, levels).astype(BF16)
+    values = v[0, :, :, :].reshape(cells, levels).astype(BF16)
+    both = jnp.dot(pick_slots(tc, cells), jnp.concatenate([values, update], axis=1), preferred_element_type=F32)
+    rows, later = both[:, :levels], both[:, levels:]
+    row_x = iota((2 * ny, slots), 0)
+    edge = jnp.where(row_x < ny, row_x, row_x + (nx - 2) * ny)
+    select = jnp.where(edge == tc[0, :, :], 1.0, 0.0).astype(BF16)
     for t in range(turbines):
         products[t] = (rows * loads[t]).astype(BF16)
+        sums[t : t + 1, :] = jnp.sum(counts[t].astype(F32) * later, axis=0, keepdims=True)
+        edge_counts[t] = jnp.dot(select, counts[t], preferred_element_type=F32)
     block = 16
     wide = turbines * block
     gram = jnp.zeros((wide, wide), F32)
@@ -235,35 +255,22 @@
     keep = (iota((wide, wide), 0) & (block - 1)) == (iota((wide, wide), 1) & (block - 1))
     gram = jnp.sum(jnp.where(keep, gram, 0.0).reshape(turbines, block, wide), axis=1)
     select = jnp.where(iota((wide, LANES), 0) // block == iota((wide, LANES), 1), 1.0, 0.0)
-    couple[...] = jnp.dot(gram, select, precision=lax.Precision.HIGHEST, preferred_element_type=F32)
-
-    ev = even("gy")
-    me = lax.axis_index("gy")
-    at = ye.shape[0] - 8
-    wheres = []
-    for a, b, y in ((yo, ye, ny - 1), (ye, yo, 0)):
-        cell = picked(ev, a, b, at, at + 1)[:, :slots].astype(jnp.int32) - 1
-        wheres.append(jnp.where(iota((nx, slots), 0) * ny + y == cell, 1.0, 0.0).astype(BF16))
+    matrix = jnp.dot(gram, select, precision=lax.Precision.HIGHEST, preferred_element_type=F32)
+    column = jnp.sum(sums[...], axis=1, keepdims=True)
+    couple[...] = jnp.where(iota((turbines, LANES), 1) == turbines, column, matrix)
+
+
+def reduce_sums(comps, ny, yo, ye, xo, xe, edge_counts, line, couple, out, sums):
+    turbines = edge_counts.shape[0]
+    ev_x = even("gx")
+    left = (SPREAD + CARRY) * picked(ev_x, xo, xe, ny, 2 * ny)
+    right = SPREAD * picked(ev_x, xe, xo, 0, ny)
     for t in range(turbines):
-        row = slot[0, t : t + 1, :]
-        hits = [ones_at(one_hot(slots, row - (me + k) * slots)) for k in (-1, 1)]
-        edge_ref[0, t], edge_ref[1, t] = spread(wheres, hits, height[0, t : t + 1, :], load[0, t : t + 1, :])
-
-
-def reduce_sums(v, tc, ye, yo, xe, xo, counts, line, couple, out, field, sums):
-    _, nx, ny, levels = v.shape
-    comps = v.shape[0]
-    turbines = counts.shape[0]
-    cells = nx * ny
-    extend(v, ye, yo, xe, xo, field, (0,))
-    update = stencil(field, 0, 2, nx, ny).reshape(cells, levels).astype(BF16)
-    rows = jnp.dot(pick_slots(tc, cells), update, preferred_element_type=F32)
-    for t in range(turbines):
-        sums[t : t + 1, :] = jnp.sum(counts[t].astype(F32) * rows, axis=0, keepdims=True)
+        sides = edge_counts[t, 0:ny, :] * left + edge_counts[t, ny : 2 * ny, :] * right
+        sums[t : t + 1, :] = jnp.sum(sides, axis=0, keepdims=True)
     lane = iota((turbines, LANES), 1)
-    ev_x = even("gx")
     at = xe.shape[0] - 8 + SUMS
-    result = jnp.where(lane == turbines, jnp.sum(sums[...], axis=1, keepdims=True), couple[...])
+    result = couple[...] + jnp.where(lane == turbines, jnp.sum(sums[...], axis=1, keepdims=True), 0.0)
     rows_of = (line[SUMS : SUMS + 1, :], picked(ev_x, xo, xe, at, at + 1), picked(ev_x, xe, xo, at, at + 1))
     for k, row in enumerate(rows_of):
         result = jnp.where(lane == turbines + 1 + k, as_column(row[:, :turbines], turbines), result)
@@ -282,11 +289,11 @@
             out[k, turbines + i : turbines + i + 1, :] = jnp.where(me + 1 == k, above[i], below[i])
 
 
-def edges_x(slots, pieces, v, ye, yo, xe, xo, edge_ref, update_ref, strip_ref, field):
+def edges(slots, pieces, v, slot, height, load, yo, ye, xo, xe, edge_x, edge_y, update_ref, strip_ref, field):
     comps, nx, ny, levels = v.shape
-    turbines = edge_ref.shape[1]
+    turbines = edge_x.shape[1]
     ev, ev_y = even("gx"), even("gy")
-    extend(v, ye, yo, xe, xo, field, tuple(range(comps)))
+    extend(v, yo, ye, xo, xe, field, tuple(range(comps)))
     ends = iota((nx, LANES), 0)
     for c in range(comps):
         update_ref[c] = stencil(field, c, 1, nx + 2, ny)
@@ -304,18 +311,28 @@
     shift = levels.bit_length() - 1
     for k, (a, b) in enumerate(((xo, xe), (xe, xo))):
         cell = picked(ev, a, b, at, at + 1)[:, :slots].astype(jnp.int32) - 1
-        where = jnp.where(iota((ny, slots), 0) + (1 - k) * (nx - 1) * ny == cell, 1.0, 0.0).astype(BF16)
+        edge = edge_slots(cell, iota((ny, slots), 0) + (1 - k) * (nx - 1) * ny)
         codes = [picked(ev, a, b, code_at + i * turbines, code_at + (i + 1) * turbines) for i in range(pieces)]
         codes = jnp.concatenate(codes, axis=1).astype(jnp.int32) - 1
         there = [picked(ev, a, b, load_at + i * turbines, load_at + (i + 1) * turbines) for i in range(pieces)]
         there = jnp.concatenate(there, axis=1)
         for t in range(turbines):
             code = codes[t : t + 1, :]
-            hit = ones_at(one_hot(slots, code >> shift))
-            (edge_ref[k, t],) = spread([where], [hit], code & (levels - 1), there[t : t + 1, :])
-
-
-def advance(points, got, v, tc, ye, yo, xe, xo, line, loads, edge_x, edge_y, update_ref, strip_ref, out, field, parts):
+            (edge_x[k, t],) = spread([(edge, code >> shift)], code & (levels - 1), there[t : t + 1, :])
+
+    me = lax.axis_index("gy")
+    at = ye.shape[0] - 8
+    lists = []
+    for a, b, y in ((yo, ye, ny - 1), (ye, yo, 0)):
+        cell = picked(ev_y, a, b, at, at + 1)[:, :slots].astype(jnp.int32) - 1
+        lists.append(edge_slots(cell, iota((nx, slots), 0) * ny + y))
+    for t in range(turbines):
+        row = slot[0, t : t + 1, :]
+        places = [(edge, row - (me + k) * slots) for edge, k in zip(lists, (-1, 1))]
+        edge_y[0, t], edge_y[1, t] = spread(places, height[0, t : t + 1, :], load[0, t : t + 1, :])
+
+
+def advance(points, got, v, tc, yo, ye, xo, xe, line, loads, edge_x, edge_y, update_ref, strip_ref, out, field, parts):
     comps, nx, ny, levels = v.shape
     turbines, slots, _ = loads.shape
     cells = nx * ny
@@ -348,17 +365,17 @@
             first = first + own[t : t + 1, :] * part
             second = second + later[t : t + 1, :] * part
         for i, rest in enumerate((first, second)):
-            for k in range(3):
+            for k in range(2):
                 piece = rest.astype(BF16)
                 rest = rest - piece.astype(F32)
-                at = (3 * i + k) * levels
+                at = (2 * i + k) * levels
                 parts[s : s + 16, at : at + levels] = piece
     row = tc[0, :, :]
     put = jnp.where(iota((cells, slots), 0) == row, 1.0, 0.0).astype(BF16)
     spread_out = jnp.dot(put, parts[...], preferred_element_type=F32)
-    pieces = [spread_out[:, k * levels : (k + 1) * levels] for k in range(6)]
-    first = ((pieces[0] + pieces[1]) + pieces[2]).reshape(nx, ny, levels)
-    second = ((pieces[3] + pieces[4]) + pieces[5]).reshape(nx, ny, levels)
+    pieces = [spread_out[:, k * levels : (k + 1) * levels] for k in range(4)]
+    first = (pieces[0] + pieces[1]).reshape(nx, ny, levels)
+    second = (pieces[2] + pieces[3]).reshape(nx, ny, levels)
     for c in range(comps):
         push = rounded(rounded(v[c, :, :, :]) * first)
         field[c, 1 : 1 + nx, OWN : OWN + ny, :] = update_ref[c, 1 : 1 + nx, :, :] + push
@@ -436,35 +453,40 @@
         **work,
     )
     xo, xe = swap(x_odd, "gx", 1), swap(x_even, "gx", 0)
-    edge_y, couple = call(
+    couple, edge_counts = call(
         beside,
         "beside",
-        [((2, turbines, nx, levels), F32), ((turbines, LANES), F32)],
-        (v, tc, slot, height, load, ye, yo, counts, loads),
-        [pltpu.VMEM((turbines, slots, levels), BF16)],
+        [((turbines, LANES), F32), ((turbines, 2 * ny, levels), F32)],
+        (v, tc, yo, ye, counts, loads),
+        [pltpu.VMEM((turbines, slots, levels), BF16), field(1, nx + 2), pltpu.VMEM((turbines, levels), F32)],
         **work,
     )
+
+    def reduce_of(*refs):
+        return reduce_sums(comps, ny, *refs)
+
     (chunk,) = call(
-        reduce_sums,
+        reduce_of,
         "reduce_sums",
         [((tiles_y, turbines + 8, LANES), F32)],
-        (v, tc, ye, yo, xe, xo, counts, line, couple),
-        [field(1, nx + 4), pltpu.VMEM((turbines, levels), F32)],
+        (yo, ye, xo, xe, edge_counts, line, couple),
+        [pltpu.VMEM((turbines, levels), F32)],
     )
     got = lax.all_to_all(chunk, "gy", 0, 0)
 
-    def edges_x_of(*refs):
-        return edges_x(slots, pieces, *refs)
-
-    edge_x, update, strip = call(
-        edges_x_of,
-        "edges_x",
+    def edges_of(*refs):
+        return edges(slots, pieces, *refs)
+
+    edge_x, edge_y, update, strip = call(
+        edges_of,
+        "edges",
         [
             ((2, turbines, ny, levels), F32),
+            ((2, turbines, nx, levels), F32),
             ((comps, nx + 2, ny, levels), F32),
             ((comps, 2, nx, levels), F32),
         ],
-        (v, ye, yo, xe, xo),
+        (v, slot, height, load, yo, ye, xo, xe),
         [field(comps, nx + 4)],
         **work,
     )
@@ -476,8 +498,8 @@
         advance_by,
         "advance",
         [(velocity.shape, F32)],
-        (got, v, tc, ye, yo, xe, xo, line, loads, edge_x, edge_y, update, strip),
-        [field(comps, nx + 2), pltpu.VMEM((slots, 6 * levels), BF16)],
+        (got, v, tc, yo, ye, xo, xe, line, loads, edge_x, edge_y, update, strip),
+        [field(comps, nx + 2), pltpu.VMEM((slots, 4 * levels), BF16)],
     )
     return out
 

time: 29.5 us -> 29.1 us (0.986)
  Pallas kernels: 13.3 us -> 8.35 us
  waiting for transfers between devices: 2.85 us -> 5.68 us
  starting transfers between devices: 13 us -> 14.7 us
    ppermute x4, starting transfers between devices: 4.39 us -> 10 us  [swap(): return lax.ppermute(x, axis, swap_pairs(lax.axis_size(axis), first))]
    pallas_call x6, Pallas kernels: 13.3 us -> 8.35 us  [call(): pl.pallas_call(kernel, out_shape=[jax.ShapeDtypeStruct(s, d) for s, d in...]
    all_to_all x1, starting transfers between devices: 8.57 us -> 4.71 us  [body(): got = lax.all_to_all(chunk, 'gy', 0, 0)]
    all_to_all x1, waiting for transfers between devices: 2.84 us -> 5.66 us  [body(): got = lax.all_to_all(chunk, 'gy', 0, 0)]
  transfers between devices with their start and end apart: 5 -> 5, of which waited for: 1 -> 1; matrix products, arithmetic and copies ran while one was open for 0% -> 0% of each run, Pallas kernels for 33% -> 17%
where the time goes in v4:
time: 29.1 us; the launch traced here: 28.8 us
  starting transfers between devices  14.7 us (51%)
  Pallas kernels  8.35 us (29%)
  waiting for transfers between devices  5.68 us (20%)
    ppermute x4, starting transfers between devices, swap(): return lax.ppermute(x, axis, swap_pairs(lax.axis_size(axis), first))  10 us
    pallas_call x6, Pallas kernels, call(): pl.pallas_call(kernel, out_shape=[jax.ShapeDtypeStruct(s, d) for s, d in...  8.35 us
    all_to_all x1, waiting for transfers between devices, body(): got = lax.all_to_all(chunk, 'gy', 0, 0)  5.66 us
    all_to_all x1, starting transfers between devices, body(): got = lax.all_to_all(chunk, 'gy', 0, 0)  4.71 us
  transfers between devices with their start and end apart: 5, of which 1 were waited for; matrix products, arithmetic and copies ran while one was open for 0% of the time, Pallas kernels for 17%

profile of v4, /device:TPU:0, one launch (start us, length us, event | category | flops | bytes accessed | tf_op | source)
XLA Modules:
  0.0 28.8 jit_solution(10455064960030541982)
XLA Ops:
  0.0 1.1 %stage.1 = (f32[3,16,16,128]{3,2,1,0:T(8,128)S(1)}, s32[1,1,96]{2,1,0:T(1,128)S(1)}, s32[1,16]{1,0:T(1,128)S(1)}, s32[1,16,384]{2,1,0:T(8,128)S(1)}, s32[1,16,38...) custom-call(f32[3,16,16,128]{3,2,1,0:T(8,128)} %v_hbm.1, ...), custom_call_target="tpu_custom_call" | custom-call | tf_op jit(solution)/shard_map/stage/pallas_call | solution.py:64
  1.1 0.7 %collective-permute-start = (f32[104,128]{1,0:T(8,128)S(1)}, f32[104,128]{1,0:T(8,128)S(1)}, u32[]{:S(2)}, u32[]{:S(2)}) collective-permute-start(f32[104,128]{1,0:T(8,128)S(1)} %get-tuple-element.24), channel_id=1, source_target_pairs={{1,2},{2,1},{3,4},{4,3},{5,6},{6,5},{9,10},{10,9},{11,12},{12,11},... | collective-permute-start | bytes 159752 | tf_op jit(solution)/shard_map/ppermute | solution.py:60
  1.8 5.8 %collective-permute-start.1 = (f32[104,128]{1,0:T(8,128)S(1)}, f32[104,128]{1,0:T(8,128)S(1)}, u32[]{:S(2)}, u32[]{:S(2)}) collective-permute-start(f32[104,128]{1,0:T(8,128)S(1)} %get-tuple-element.25), channel_id=1, source_target_pairs={{0,1},{1,0},{2,3},{3,2},{4,5},{5,4},{6,7},{7,6},{8,9},{9,8},{10,11... | collective-permute-start | bytes 159752 | tf_op jit(solution)/shard_map/ppermute | solution.py:60
  7.6 1.8 %histogram.1 = (bf16[16,96,128]{2,1,0:T(8,128)(2,1)S(1)}, f32[16,96,128]{2,1,0:T(8,128)S(1)}, f32[8,128]{1,0:T(8,128)S(1)}, f32[200,128]{1,0:T(8,128)S(1)}, f32[200,128]{1,0:T(8,128)S(1)}) custom-call(f32[3,16,16,128]{3,2,1,0:T(8,128)S(1)} %get-tuple-element.26.v.refs_0_.refs_1_, s32[1,1,96]{2,1,0:T(1,128)S(1)} %get-tuple-element.27.tc.refs_2_, ...), custom_call_target="tpu_custom_call" | custom-call | flops 1962934272 | bytes 1048576 | tf_op jit(solution)/shard_map/histogram/pallas_call | solution.py:64
  9.4 0.7 %collective-permute-start.2 = (f32[200,128]{1,0:T(8,128)S(1)}, f32[200,128]{1,0:T(8,128)S(1)}, u32[]{:S(2)}, u32[]{:S(2)}) collective-permute-start(f32[200,128]{1,0:T(8,128)S(1)} %get-tuple-element.32), channel_id=1, source_target_pairs={{8,16},{16,8},{9,17},{17,9},{10,18},{18,10},{11,19},{19,11},{12,20... | collective-permute-start | bytes 307208 | tf_op jit(solution)/shard_map/ppermute | solution.py:60
  10.1 2.9 %collective-permute-start.3 = (f32[200,128]{1,0:T(8,128)S(1)}, f32[200,128]{1,0:T(8,128)S(1)}, u32[]{:S(2)}, u32[]{:S(2)}) collective-permute-start(f32[200,128]{1,0:T(8,128)S(1)} %get-tuple-element.33), channel_id=1, source_target_pairs={{0,8},{8,0},{16,24},{24,16},{1,9},{9,1},{17,25},{25,17},{2,10},{10... | collective-permute-start | bytes 307208 | tf_op jit(solution)/shard_map/ppermute | solution.py:60
  13.0 0.0 collective-permute-done.yo.refs_0_.refs_4_.refs_3_
  13.0 0.0 collective-permute-done.1.ye.refs_1_.refs_5_.refs_4_
  13.0 1.0 %beside.1 = (f32[16,128]{1,0:T(8,128)S(1)}, f32[16,32,128]{2,1,0:T(8,128)S(1)}) custom-call(f32[3,16,16,128]{3,2,1,0:T(8,128)S(1)} %get-tuple-element.26.v.refs_0_.refs_1_, s32[1,1,96]{2,1,0:T(1,128)S(1)} %get-tuple-element.27.tc.refs_2_, f32[104,128]{1,0:T(8,128)S(1)} %collective-permute-done.yo.refs_0_.refs_4_.refs_3_, ...), custom_call_target="tpu_custom_call" | custom-call | flops 1962934272 | bytes 1048576 | tf_op jit(solution)/shard_map/beside/pallas_call | solution.py:64
  14.0 0.0 collective-permute-done.2.refs_2_.refs_6_.refs_5_
  14.0 0.0 collective-permute-done.3.refs_3_.refs_7_.refs_6_
  14.0 0.8 %reduce_sums.1 = f32[8,24,128]{2,1,0:T(8,128)} custom-call(f32[104,128]{1,0:T(8,128)S(1)} %collective-permute-done.yo.refs_0_.refs_4_.refs_3_, f32[104,128]{1,0:T(8,128)S(1)} %collective-permute-done.1.ye.refs_1_.refs_5_.refs_4_, f32[200,128]{1,0:T(8,128)S(1)} %collective-permute-done.2.refs_2_.refs_6_.refs_5_, ...), custom_call_target="tpu_custom_call" | custom-call | tf_op jit(solution)/shard_map/reduce_sums/pallas_call | solution.py:64
  14.8 4.7 %all-to-all-start = ((f32[8,24,128]{2,1,0:T(8,128)}), f32[8,24,128]{2,1,0:T(8,128)S(1)}, u32[]{:S(2)}, u32[]{:S(2)}) async-start(f32[8,24,128]{2,1,0:T(8,128)} %reduce_sums.1), calls=%async_computation | async-start | bytes 196608 | tf_op jit(solution)/shard_map/all_to_all | solution.py:475
  19.5 2.1 %edges.1 = (f32[2,16,16,128]{3,2,1,0:T(8,128)S(1)}, f32[2,16,16,128]{3,2,1,0:T(8,128)S(1)}, f32[3,18,16,128]{3,2,1,0:T(8,128)S(1)}, f32[3,2,16,128]{3,2,1,0:T(8,128)S(1)}) custom-call(f32[3,16,16,128]{3,2,1,0:T(8,128)S(1)} %get-tuple-element.26.v.refs_0_.refs_1_, s32[1,16,384]{2,1,0:T(8,128)S(1)} %get-tuple-element.29.slot.refs_1_, ...), custom_call_target="tpu_custom_call" | custom-call | flops 1962934272 | bytes 1048576 | tf_op jit(solution)/shard_map/edges/pallas_call | solution.py:64
  21.7 5.7 %all-to-all-done.refs_0_ = f32[8,24,128]{2,1,0:T(8,128)S(1)} async-done(((f32[8,24,128]{2,1,0:T(8,128)}), f32[8,24,128]{2,1,0:T(8,128)S(1)}, u32[]{:S(2)}, u32[]{:S(2)}) %all-to-all-start) | async-done | bytes 98336 | tf_op jit(solution)/shard_map/all_to_all | solution.py:475
  27.3 1.5 %advance.1 = f32[3,16,16,128]{3,2,1,0:T(8,128)} custom-call(f32[8,24,128]{2,1,0:T(8,128)S(1)} %all-to-all-done.refs_0_, f32[3,16,16,128]{3,2,1,0:T(8,128)S(1)} %get-tuple-element.26.v.refs_0_.refs_1_, s32[1,1,96]{2,1,0:T(1,128)S(1)} %get-tuple-element.27.tc.refs_2_, f32[104,128]{1,0:T(8,128)S(1)} %collective-permute-done.yo.refs_0_.refs_4_.refs_3_, ...), custom_call_target="tpu_custom_call" | custom-call | tf_op jit(solution)/shard_map/advance/pallas_call | solution.py:64
Async XLA Ops:
  1.1 11.9 %collective-permute-start = (f32[104,128]{1,0:T(8,128)S(1)}, f32[104,128]{1,0:T(8,128)S(1)}, u32[]{:S(2)}, u32[]{:S(2)}) collective-permute-start(f32[104,128]{1,0:T(8,128)S(1)} %get-tuple-element.24), channel_id=1, source_target_pairs={{1,2},{2,1},{3,4},{4,3},{5,6},{6,5},{9,10},{10,9},{11,12},{12,11},... | collective-permute-start | bytes 159752 | tf_op jit(solution)/shard_map/ppermute | solution.py:60
  1.8 11.2 %collective-permute-start.1 = (f32[104,128]{1,0:T(8,128)S(1)}, f32[104,128]{1,0:T(8,128)S(1)}, u32[]{:S(2)}, u32[]{:S(2)}) collective-permute-start(f32[104,128]{1,0:T(8,128)S(1)} %get-tuple-element.25), channel_id=1, source_target_pairs={{0,1},{1,0},{2,3},{3,2},{4,5},{5,4},{6,7},{7,6},{8,9},{9,8},{10,11... | collective-permute-start | bytes 159752 | tf_op jit(solution)/shard_map/ppermute | solution.py:60
  9.4 4.6 %collective-permute-start.2 = (f32[200,128]{1,0:T(8,128)S(1)}, f32[200,128]{1,0:T(8,128)S(1)}, u32[]{:S(2)}, u32[]{:S(2)}) collective-permute-start(f32[200,128]{1,0:T(8,128)S(1)} %get-tuple-element.32), channel_id=1, source_target_pairs={{8,16},{16,8},{9,17},{17,9},{10,18},{18,10},{11,19},{19,11},{12,20... | collective-permute-start | bytes 307208 | tf_op jit(solution)/shard_map/ppermute | solution.py:60
  10.1 3.9 %collective-permute-start.3 = (f32[200,128]{1,0:T(8,128)S(1)}, f32[200,128]{1,0:T(8,128)S(1)}, u32[]{:S(2)}, u32[]{:S(2)}) collective-permute-start(f32[200,128]{1,0:T(8,128)S(1)} %get-tuple-element.33), channel_id=1, source_target_pairs={{0,8},{8,0},{16,24},{24,16},{1,9},{9,1},{17,25},{25,17},{2,10},{10... | collective-permute-start | bytes 307208 | tf_op jit(solution)/shard_map/ppermute | solution.py:60
  14.8 12.5 %all-to-all-start = ((f32[8,24,128]{2,1,0:T(8,128)}), f32[8,24,128]{2,1,0:T(8,128)S(1)}, u32[]{:S(2)}, u32[]{:S(2)}) async-start(f32[8,24,128]{2,1,0:T(8,128)} %reduce_sums.1), calls=%async_computation | async-start | bytes 196608 | tf_op jit(solution)/shard_map/all_to_all | solution.py:475

commit v5 on v4

--- a/solution.py
+++ b/solution.py
@@ -49,15 +49,14 @@
     return lax.rem(lax.axis_index(axis), 2) == 0
 
 
-def swap_pairs(count, first):
-    pairs = []
-    for i in range(first, count - 1, 2):
-        pairs += [(i, i + 1), (i + 1, i)]
-    return pairs
-
-
-def swap(x, axis, first):
-    return lax.ppermute(x, axis, swap_pairs(lax.axis_size(axis), first))
+def swap(x, axis):
+    return lax.ppermute(x, axis, [(i, i ^ 1) for i in range(lax.axis_size(axis))])
+
+
+def hop(x, axis):
+    count = lax.axis_size(axis)
+    steps = [(i, i + 2 - 4 * (i % 2)) for i in range(count)]
+    return lax.ppermute(x, axis, [(i, k) for i, k in steps if 0 <= k < count])
 
 
 def call(kernel, name, outs, args, scratch=(), flops=0, nbytes=0, space=pltpu.VMEM):
@@ -95,7 +94,7 @@
     return moved(center, before, after, beside + lane_edge(center))
 
 
-def stage(v_hbm, tc_hbm, owner_hbm, slot_hbm, height_hbm, load_hbm, v, tc, owner, slot, height, load, to_even, to_odd, sems):
+def stage(v_hbm, tc_hbm, owner_hbm, slot_hbm, height_hbm, load_hbm, v, tc, owner, slot, height, load, out, sems):
     pairs = ((v_hbm, v), (tc_hbm, tc), (slot_hbm, slot), (height_hbm, height), (load_hbm, load), (owner_hbm, owner))
     copies = [pltpu.make_async_copy(a, b, sems.at[i]) for i, (a, b) in enumerate(pairs)]
     for copy in copies:
@@ -103,20 +102,20 @@
     copies[0].wait()
     comps, nx, ny, _ = v.shape
     ev = even("gy")
+    rest = comps * 2 * nx + 8
     at = 0
     for c in range(comps):
         for k in range(2):
             high = v[c, :, ny - 2 + k, :]
             low = v[c, :, k, :]
-            to_even[at : at + nx, :] = jnp.where(ev, high, low)
-            to_odd[at : at + nx, :] = jnp.where(ev, low, high)
+            out[at : at + nx, :] = jnp.where(ev, low, high)
+            out[at + rest : at + rest + nx, :] = jnp.where(ev, high, low)
             at += nx
     copies[1].wait()
     cells = tc[0, :, :].astype(F32) + 1.0
     slots = cells.shape[1]
-    for out in (to_even, to_odd):
-        out[at : at + 8, :] = jnp.zeros((8, LANES), F32)
-        out[at : at + 1, 0:slots] = cells
+    out[at : at + 8, :] = jnp.zeros((8, LANES), F32)
+    out[at : at + 1, 0:slots] = cells
     for copy in copies[2:]:
         copy.wait()
 
@@ -135,7 +134,18 @@
     return jnp.where(flag, a[lo:hi, :], b[lo:hi, :])
 
 
-def histogram(v, tc, owner, slot, height, load, count_ref, load_ref, line, to_even, to_odd, sum_ref):
+def edge_rows(flag, low, near, far, lo, hi):
+    at = far.shape[0]
+    here, there = near[at + lo : at + hi, :], far[lo:hi, :]
+    return jnp.where(flag, there, here) if low else jnp.where(flag, here, there)
+
+
+def pass_on(near, *refs):
+    out = refs[-1]
+    out[...] = near[0 : out.shape[0], :]
+
+
+def histogram(v, tc, owner, slot, height, load, count_ref, load_ref, line, out, sum_ref):
     _, turbines, points = slot.shape
     slots, levels = count_ref.shape[1:]
     comps, nx, ny, _ = v.shape
@@ -171,20 +181,19 @@
     inside = (local >= 0) & (local < slots)
     code = jnp.where(inside, local * levels + height[0, :, :] + 1, 0).astype(F32)
     ev = even("gx")
+    rest = out.shape[0] - comps * 2 * ny
     at = 0
     for c in range(comps):
         for k in range(2):
             right, left = v[c, nx - 2 + k, :, :], v[c, k, :, :]
-            to_even[at : at + ny, :] = jnp.where(ev, right, left)
-            to_odd[at : at + ny, :] = jnp.where(ev, left, right)
+            out[at : at + ny, :] = jnp.where(ev, left, right)
+            out[at + rest : at + rest + ny, :] = jnp.where(ev, right, left)
             at += ny
     for part in (code, load[0, :, :]):
         for k in range(0, points, LANES):
-            for out in (to_even, to_odd):
-                out[at : at + turbines, :] = part[:, k : k + LANES]
+            out[at : at + turbines, :] = part[:, k : k + LANES]
             at += turbines
-    for out in (to_even, to_odd):
-        out[at : at + 8, :] = line[...]
+    out[at : at + 8, :] = line[...]
 
 
 def extend(v, yo, ye, xo, xe, field, comps):
@@ -195,13 +204,13 @@
         field[out, 2 : 2 + nx, OWN : OWN + ny, :] = v[c, :, :, :]
         for k in range(2):
             at = (c * 2 + k) * nx
-            field[out, 2 : 2 + nx, OWN - 2 + k, :] = picked(ev_y, yo, ye, at, at + nx)
-            field[out, 2 : 2 + nx, OWN + ny + k, :] = picked(ev_y, ye, yo, at, at + nx)
+            field[out, 2 : 2 + nx, OWN - 2 + k, :] = edge_rows(ev_y, True, ye, yo, at, at + nx)
+            field[out, 2 : 2 + nx, OWN + ny + k, :] = edge_rows(ev_y, False, ye, yo, at, at + nx)
             at = (c * 2 + k) * ny
-            for x, a, b in ((k, xo, xe), (2 + nx + k, xe, xo)):
+            for x, low in ((k, True), (2 + nx + k, False)):
                 field[out, x, 0:OWN, :] = jnp.zeros((OWN, LANES), F32)
                 field[out, x, OWN + ny : PLANE, :] = jnp.zeros((PLANE - OWN - ny, LANES), F32)
-                field[out, x, OWN : OWN + ny, :] = picked(ev_x, a, b, at, at + ny)
+                field[out, x, OWN : OWN + ny, :] = edge_rows(ev_x, low, xe, xo, at, at + ny)
 
 
 def edge_slots(cell_row, cells):
@@ -224,26 +233,17 @@
     return [both[2 * k * n : (2 * k + 1) * n] + both[(2 * k + 1) * n : (2 * k + 2) * n] for k in range(len(places))]
 
 
-def beside(v, tc, yo, ye, counts, loads, couple, edge_counts, products, field, sums):
+def pair_up(v, tc, counts, loads, matrix, edge_counts, products):
     turbines, slots, levels = counts.shape
     _, nx, ny, _ = v.shape
     cells = nx * ny
-    ev = even("gy")
-    field[0, 1 : 1 + nx, OWN : OWN + ny, :] = v[0, :, :, :]
-    field[0, 1 : 1 + nx, OWN - 1, :] = picked(ev, yo, ye, nx, 2 * nx)
-    field[0, 1 : 1 + nx, OWN + ny, :] = picked(ev, ye, yo, 0, nx)
-    for x in (0, nx + 1):
-        field[0, x, OWN : OWN + ny, :] = jnp.zeros((ny, levels), F32)
-    update = stencil(field, 0, 1, nx, ny).reshape(cells, levels).astype(BF16)
     values = v[0, :, :, :].reshape(cells, levels).astype(BF16)
-    both = jnp.dot(pick_slots(tc, cells), jnp.concatenate([values, update], axis=1), preferred_element_type=F32)
-    rows, later = both[:, :levels], both[:, levels:]
+    rows = jnp.dot(pick_slots(tc, cells), values, preferred_element_type=F32)
     row_x = iota((2 * ny, slots), 0)
     edge = jnp.where(row_x < ny, row_x, row_x + (nx - 2) * ny)
     select = jnp.where(edge == tc[0, :, :], 1.0, 0.0).astype(BF16)
     for t in range(turbines):
         products[t] = (rows * loads[t]).astype(BF16)
-        sums[t : t + 1, :] = jnp.sum(counts[t].astype(F32) * later, axis=0, keepdims=True)
         edge_counts[t] = jnp.dot(select, counts[t], preferred_element_type=F32)
     block = 16
     wide = turbines * block
@@ -255,21 +255,37 @@
     keep = (iota((wide, wide), 0) & (block - 1)) == (iota((wide, wide), 1) & (block - 1))
     gram = jnp.sum(jnp.where(keep, gram, 0.0).reshape(turbines, block, wide), axis=1)
     select = jnp.where(iota((wide, LANES), 0) // block == iota((wide, LANES), 1), 1.0, 0.0)
-    matrix = jnp.dot(gram, select, precision=lax.Precision.HIGHEST, preferred_element_type=F32)
+    matrix[...] = jnp.dot(gram, select, precision=lax.Precision.HIGHEST, preferred_element_type=F32)
+
+
+def beside(v, tc, yo, ye, counts, matrix, couple, field, sums):
+    turbines, _, levels = counts.shape
+    _, nx, ny, _ = v.shape
+    cells = nx * ny
+    ev = even("gy")
+    field[0, 1 : 1 + nx, OWN : OWN + ny, :] = v[0, :, :, :]
+    field[0, 1 : 1 + nx, OWN - 1, :] = edge_rows(ev, True, ye, yo, nx, 2 * nx)
+    field[0, 1 : 1 + nx, OWN + ny, :] = edge_rows(ev, False, ye, yo, 0, nx)
+    for x in (0, nx + 1):
+        field[0, x, OWN : OWN + ny, :] = jnp.zeros((ny, levels), F32)
+    update = stencil(field, 0, 1, nx, ny).reshape(cells, levels).astype(BF16)
+    later = jnp.dot(pick_slots(tc, cells), update, preferred_element_type=F32)
+    for t in range(turbines):
+        sums[t : t + 1, :] = jnp.sum(counts[t].astype(F32) * later, axis=0, keepdims=True)
     column = jnp.sum(sums[...], axis=1, keepdims=True)
-    couple[...] = jnp.where(iota((turbines, LANES), 1) == turbines, column, matrix)
+    couple[...] = jnp.where(iota((turbines, LANES), 1) == turbines, column, matrix[...])
 
 
 def reduce_sums(comps, ny, yo, ye, xo, xe, edge_counts, line, couple, out, sums):
     turbines = edge_counts.shape[0]
     ev_x = even("gx")
-    left = (SPREAD + CARRY) * picked(ev_x, xo, xe, ny, 2 * ny)
-    right = SPREAD * picked(ev_x, xe, xo, 0, ny)
+    left = (SPREAD + CARRY) * edge_rows(ev_x, True, xe, xo, ny, 2 * ny)
+    right = SPREAD * edge_rows(ev_x, False, xe, xo, 0, ny)
     for t in range(turbines):
         sides = edge_counts[t, 0:ny, :] * left + edge_counts[t, ny : 2 * ny, :] * right
         sums[t : t + 1, :] = jnp.sum(sides, axis=0, keepdims=True)
     lane = iota((turbines, LANES), 1)
-    at = xe.shape[0] - 8 + SUMS
+    at = xo.shape[0] - 8 + SUMS
     result = couple[...] + jnp.where(lane == turbines, jnp.sum(sums[...], axis=1, keepdims=True), 0.0)
     rows_of = (line[SUMS : SUMS + 1, :], picked(ev_x, xo, xe, at, at + 1), picked(ev_x, xe, xo, at, at + 1))
     for k, row in enumerate(rows_of):
@@ -281,9 +297,9 @@
     above = []
     below = []
     for c in range(comps):
-        for a, b, at in ((xo, xe, (c * 2 + 1) * ny), (xe, xo, c * 2 * ny)):
-            above.append(picked(ev_x, a, b, at + ny - 1, at + ny))
-            below.append(picked(ev_x, a, b, at, at + 1))
+        for low, at in ((True, (c * 2 + 1) * ny), (False, c * 2 * ny)):
+            above.append(edge_rows(ev_x, low, xe, xo, at + ny - 1, at + ny))
+            below.append(edge_rows(ev_x, low, xe, xo, at, at + 1))
     for i in range(2 * comps):
         for k in range(out.shape[0]):
             out[k, turbines + i : turbines + i + 1, :] = jnp.where(me + 1 == k, above[i], below[i])
@@ -297,15 +313,15 @@
     ends = iota((nx, LANES), 0)
     for c in range(comps):
         update_ref[c] = stencil(field, c, 1, nx + 2, ny)
-        for k, (a, b, y) in enumerate(((yo, ye, 0), (ye, yo, ny - 1))):
+        for k, y in enumerate((0, ny - 1)):
             near, far = (c * 2 + 1 - k) * nx, (c * 2 + k) * nx
-            center = picked(ev_y, a, b, near, near + nx)
+            center = edge_rows(ev_y, k == 0, ye, yo, near, near + nx)
             before = jnp.where(ends == 0, 0.0, pltpu.roll(center, 1, 0))
             after = jnp.where(ends == nx - 1, 0.0, pltpu.roll(center, nx - 1, 0))
-            others = picked(ev_y, a, b, far, far + nx) + v[c, :, y, :] + lane_edge(center)
+            others = edge_rows(ev_y, k == 0, ye, yo, far, far + nx) + v[c, :, y, :] + lane_edge(center)
             strip_ref[c, k] = moved(center, before, after, others)
 
-    at = xe.shape[0] - 8 + CELLS
+    at = xo.shape[0] - 8 + CELLS
     code_at = comps * 2 * ny
     load_at = code_at + pieces * turbines
     shift = levels.bit_length() - 1
@@ -321,7 +337,7 @@
             (edge_x[k, t],) = spread([(edge, code >> shift)], code & (levels - 1), there[t : t + 1, :])
 
     me = lax.axis_index("gy")
-    at = ye.shape[0] - 8
+    at = yo.shape[0] - 8
     lists = []
     for a, b, y in ((yo, ye, ny - 1), (ye, yo, 0)):
         cell = picked(ev_y, a, b, at, at + 1)[:, :slots].astype(jnp.int32) - 1
@@ -348,7 +364,7 @@
     def coefs(scales, sums):
         return -(scales * (FREE_WIND + sums / points))
 
-    at = xe.shape[0] - 8 + SCALE
+    at = xo.shape[0] - 8 + SCALE
     scale = as_column(line[SCALE : SCALE + 1, :turbines], turbines)
     own = coefs(scale, column(turbines + 1))
     left = coefs(as_column(picked(ev_x, xo, xe, at, at + 1)[:, :turbines], turbines), column(turbines + 2))
@@ -395,17 +411,17 @@
     row_x, row_y = iota((nx, LANES), 0), iota((ny, LANES), 0)
     for c in range(comps):
         corner = [[corner_rows[y][c * 2 + x : c * 2 + x + 1, :] for y in range(2)] for x in range(2)]
-        for k, (a, b) in enumerate(((xo, xe), (xe, xo))):
+        for k in range(2):
             at = (c * 2 + 1 - k) * ny
             x = k * (nx + 1)
-            push = rounded(rounded(picked(ev_x, a, b, at, at + ny)) * sums[k])
+            push = rounded(rounded(edge_rows(ev_x, k == 0, xe, xo, at, at + ny)) * sums[k])
             extra = jnp.where(row_y == 0, corner[k][0], 0.0) + jnp.where(row_y == ny - 1, corner[k][1], 0.0)
             value = update_ref[c, x, :, :] + SPREAD * extra + push
             field[c, x, OWN : OWN + ny, :] = jnp.where(there_x[k], value, 0.0)
-        for k, (a, b) in enumerate(((yo, ye), (ye, yo))):
+        for k in range(2):
             at = (c * 2 + 1 - k) * nx
             y = OWN - 1 + k * (ny + 1)
-            push = rounded(rounded(picked(ev_y, a, b, at, at + nx)) * sums[2 + k])
+            push = rounded(rounded(edge_rows(ev_y, k == 0, ye, yo, at, at + nx)) * sums[2 + k])
             extra = jnp.where(row_x == 0, (SPREAD + CARRY) * corner[0][k], 0.0)
             extra = extra + jnp.where(row_x == nx - 1, SPREAD * corner[1][k], 0.0)
             value = strip_ref[c, k] + extra + push
@@ -421,45 +437,58 @@
     slots = tile_cells.shape[2]
     tiles_y = lax.axis_size("gy")
     pieces = points // LANES
-    rows_y = comps * 2 * nx + 8
-    rows_x = comps * 2 * ny + 2 * pieces * turbines + 8
+    edge_y_rows, edge_x_rows = comps * 2 * nx, comps * 2 * ny
+    rows_y = edge_y_rows + 8
+    rows_x = edge_x_rows + 2 * pieces * turbines + 8
     args = (velocity, tile_cells, owner, point_slot, point_z, loading)
-    work = {"flops": 26 * turbines * slots * points * levels, "nbytes": 1 << 20}
+    work = {"flops": 104 * turbines * slots * points * levels, "nbytes": 1 << 20}
 
     def field(n, planes):
         return pltpu.VMEM((n, planes, PLANE, levels), F32)
 
-    v, tc, own, slot, height, load, y_even, y_odd = call(
+    v, tc, own, slot, height, load, to_y = call(
         stage,
         "stage",
-        [(x.shape, x.dtype) for x in args] + [((rows_y, levels), F32)] * 2,
+        [(x.shape, x.dtype) for x in args] + [((edge_y_rows + rows_y, levels), F32)],
         args,
         [pltpu.SemaphoreType.DMA((len(args),))],
         space=pltpu.HBM,
     )
-    yo, ye = swap(y_odd, "gy", 1), swap(y_even, "gy", 0)
-    counts, loads, line, x_even, x_odd = call(
+    ye = swap(to_y, "gy")
+    counts, loads, line, to_x = call(
         histogram,
         "histogram",
         [
             ((turbines, slots, levels), BF16),
             ((turbines, slots, levels), F32),
             ((8, LANES), F32),
-            ((rows_x, levels), F32),
-            ((rows_x, levels), F32),
+            ((edge_x_rows + rows_x, levels), F32),
         ],
         (v, tc, own, slot, height, load),
         [pltpu.VMEM((turbines, levels), F32)],
         **work,
     )
-    xo, xe = swap(x_odd, "gx", 1), swap(x_even, "gx", 0)
-    couple, edge_counts = call(
+    xe = swap(to_x, "gx")
+    matrix, edge_counts = call(
+        pair_up,
+        "pair_up",
+        [((turbines, LANES), F32), ((turbines, 2 * ny, levels), F32)],
+        (v, tc, counts, loads),
+        [pltpu.VMEM((turbines, slots, levels), BF16)],
+        **work,
+    )
+    (on_y,) = call(pass_on, "pass_on_y", [((rows_y, levels), F32)], (ye, matrix))
+    yo = hop(on_y, "gy")
+    (on_x,) = call(pass_on, "pass_on_x", [((rows_x, levels), F32)], (xe,))
+    xo = hop(on_x, "gx")
+    (couple,) = call(
         beside,
         "beside",
-        [((turbines, LANES), F32), ((turbines, 2 * ny, levels), F32)],
-        (v, tc, yo, ye, counts, loads),
-        [pltpu.VMEM((turbines, slots, levels), BF16), field(1, nx + 2), pltpu.VMEM((turbines, levels), F32)],
-        **work,
+        [((turbines, LANES), F32)],
+        (v, tc, yo, ye, counts, matrix),
+        [field(1, nx + 2), pltpu.VMEM((turbines, levels), F32)],
+        flops=work["flops"] // 4,
+        nbytes=work["nbytes"],
     )
 
     def reduce_of(*refs):

time: 29.1 us -> 30.9 us (1.062)
  waiting for transfers between devices: 5.68 us -> 6.95 us
  Pallas kernels: 8.35 us -> 8.68 us
    ppermute x4, waiting for transfers between devices: 0.02 us -> 1.94 us  [the longest x2 1.76 us: hop(): return lax.ppermute(x, axis, [(i, k) for i, k in steps if 0 <= k < count])]
    all_to_all x1, waiting for transfers between devices: 5.66 us -> 5.01 us  [body(): got = lax.all_to_all(chunk, 'gy', 0, 0)]
    pallas_call x6 -> x9, Pallas kernels: 8.35 us -> 8.68 us  [call(): pl.pallas_call(kernel, out_shape=[jax.ShapeDtypeStruct(s, d) for s, d in...]
  transfers between devices with their start and end apart: 5 -> 5, of which waited for: 1 -> 3; matrix products, arithmetic and copies ran while one was open for 0% -> 0% of each run, Pallas kernels for 17% -> 17%
where the time goes in v5:
time: 30.9 us; the launch traced here: 30.6 us
  starting transfers between devices  14.9 us (48%)
  Pallas kernels  8.68 us (28%)
  waiting for transfers between devices  6.95 us (22%)
    pallas_call x9, Pallas kernels, call(): pl.pallas_call(kernel, out_shape=[jax.ShapeDtypeStruct(s, d) for s, d in...  8.68 us
    ppermute x2, starting transfers between devices, hop(): return lax.ppermute(x, axis, [(i, k) for i, k in steps if 0 <= k < count])  7.13 us
    all_to_all x1, waiting for transfers between devices, body(): got = lax.all_to_all(chunk, 'gy', 0, 0)  5.01 us
    all_to_all x1, starting transfers between devices, body(): got = lax.all_to_all(chunk, 'gy', 0, 0)  4.71 us
    ppermute x2, starting transfers between devices, swap(): lax.ppermute(x, axis, [(i, i ^ 1) for i in range(lax.axis_size(axis))])  3.07 us
    ppermute x2, waiting for transfers between devices, hop(): return lax.ppermute(x, axis, [(i, k) for i, k in steps if 0 <= k < count])  1.76 us
  transfers between devices with their start and end apart: 5, of which 3 were waited for; matrix products, arithmetic and copies ran while one was open for 0% of the time, Pallas kernels for 17%

profile of v5, /device:TPU:0, one launch (start us, length us, event | category | flops | bytes accessed | tf_op | source)
XLA Modules:
  0.0 30.6 jit_solution(17859350892959619763)
XLA Ops:
  0.0 1.1 %stage.1 = (f32[3,16,16,128]{3,2,1,0:T(8,128)S(1)}, s32[1,1,96]{2,1,0:T(1,128)S(1)}, s32[1,16]{1,0:T(1,128)S(1)}, s32[1,16,384]{2,1,0:T(8,128)S(1)}, s32[1,16,38...) custom-call(f32[3,16,16,128]{3,2,1,0:T(8,128)} %v_hbm.1, s32[1,1,96]{2,1,0:T(1,128)} %tc_hbm.1, ...), custom_call_target="tpu_custom_call" | custom-call | tf_op jit(solution)/shard_map/stage/pallas_call | solution.py:63
  1.1 3.0 %collective-permute-start = (f32[200,128]{1,0:T(8,128)S(1)}, f32[200,128]{1,0:T(8,128)S(1)}, u32[]{:S(2)}, u32[]{:S(2)}) collective-permute-start(f32[200,128]{1,0:T(8,128)S(1)} %get-tuple-element.22), channel_id=1, source_target_pairs={{0,1},{1,0},{2,3},{3,2},{4,5},{5,4},{6,7},{7,6},{8,9},{9,8},{10,11... | collective-permute-start | bytes 307208 | tf_op jit(solution)/shard_map/ppermute | solution.py:53
  4.2 1.8 %histogram.1 = (bf16[16,96,128]{2,1,0:T(8,128)(2,1)S(1)}, f32[16,96,128]{2,1,0:T(8,128)S(1)}, f32[8,128]{1,0:T(8,128)S(1)}, f32[296,128]{1,0:T(8,128)S(1)}) custom-call(f32[3,16,16,128]{3,2,1,0:T(8,128)S(1)} %get-tuple-element.23.v.refs_0_.refs_1_, s32[1,1,96]{2,1,0:T(1,128)S(1)} %get-tuple-element.24.tc.refs_2_, s32[1,16]{1,0:T(1,128)S(1)} %get-tuple-element.25.owner, ...), custom_call_target="tpu_custom_call" | custom-call | flops 7851737088 | bytes 1048576 | tf_op jit(solution)/shard_map/histogram/pallas_call | solution.py:63
  6.0 0.0 collective-permute-start.2
  6.1 0.8 %pair_up.1 = (f32[16,128]{1,0:T(8,128)S(1)}, f32[16,32,128]{2,1,0:T(8,128)S(1)}) custom-call(f32[3,16,16,128]{3,2,1,0:T(8,128)S(1)} %get-tuple-element.23.v.refs_0_.refs_1_, s32[1,1,96]{2,1,0:T(1,128)S(1)} %get-tuple-element.24.tc.refs_2_, bf16[16,96,128]{2,1,0:T(8,128)(2,1)S(1)} %get-tuple-element.29.counts, f32[16,96,128]{2,1,0:T(8,128)S(1)} %get-tuple-element.30.loads.refs_8_), custom_call_target="tpu_custom_call" | custom-call | flops 7851737088 | bytes 1048576 | tf_op jit(solution)/shard_map/pair_up/pallas_call | solution.py:63
  6.9 0.2 collective-permute-done.near.ye.refs_1_.refs_5_.refs_4_
  7.1 3.7 %collective-permute-start.1 = (f32[104,128]{1,0:T(8,128)S(1)}, f32[104,128]{1,0:T(8,128)S(1)}, u32[]{:S(2)}, u32[]{:S(2)}) collective-permute-start(f32[104,128]{1,0:T(8,128)S(1)} %pass_on_y.1), channel_id=1, source_target_pairs={{0,2},{2,4},{3,1},{4,6},{5,3},{7,5},{8,10},{10,12},{11,9},{12,14},... | collective-permute-start | bytes 159752 | tf_op jit(solution)/shard_map/ppermute | solution.py:59
  10.8 0.0 collective-permute-done.2.near.refs_3_.refs_7_.refs_6_
  10.8 3.4 %collective-permute-start.3 = (f32[200,128]{1,0:T(8,128)S(1)}, f32[200,128]{1,0:T(8,128)S(1)}, u32[]{:S(2)}, u32[]{:S(2)}) collective-permute-start(f32[200,128]{1,0:T(8,128)S(1)} %pass_on_x.1), channel_id=1, source_target_pairs={{0,16},{24,8},{1,17},{25,9},{2,18},{26,10},{3,19},{27,11},{4,20},{... | collective-permute-start | bytes 307208 | tf_op jit(solution)/shard_map/ppermute | solution.py:59
  14.2 0.0 collective-permute-done.1.yo.refs_0_.refs_4_.refs_3_
  14.3 0.5 %beside.1.refs_6_ = f32[16,128]{1,0:T(8,128)S(1)} custom-call(f32[3,16,16,128]{3,2,1,0:T(8,128)S(1)} %get-tuple-element.23.v.refs_0_.refs_1_, s32[1,1,96]{2,1,0:T(1,128)S(1)} %get-tuple-element.24.tc.refs_2_, f32[104,128]{1,0:T(8,128)S(1)} %collective-permute-done.1.yo.refs_0_.refs_4_.refs_3_, ...), custom_call_target="tpu_custom_call" | custom-call | flops 1962934272 | bytes 1048576 | tf_op jit(solution)/shard_map/beside/pallas_call | solution.py:63
  14.7 1.8 %collective-permute-done.3.refs_2_.refs_6_.refs_5_ = f32[200,128]{1,0:T(8,128)S(1)} collective-permute-done((f32[200,128]{1,0:T(8,128)S(1)}, f32[200,128]{1,0:T(8,128)S(1)}, u32[]{:S(2)}, u32[]{:S(2)}) %collective-permute-start.3) | collective-permute-done | bytes 102432 | tf_op jit(solution)/shard_map/ppermute | solution.py:59
  16.5 0.8 %reduce_sums.1 = f32[8,24,128]{2,1,0:T(8,128)} custom-call(f32[104,128]{1,0:T(8,128)S(1)} %collective-permute-done.1.yo.refs_0_.refs_4_.refs_3_, f32[200,128]{1,0:T(8,128)S(1)} %collective-permute-done.near.ye.refs_1_.refs_5_.refs_4_, f32[200,128]{1,0:T(8,128)S(1)} %collective-permute-done.3.refs_2_.refs_6_.refs_5_, ...), custom_call_target="tpu_custom_call" | custom-call | tf_op jit(solution)/shard_map/reduce_sums/pallas_call | solution.py:63
  17.3 4.7 %all-to-all-start = ((f32[8,24,128]{2,1,0:T(8,128)}), f32[8,24,128]{2,1,0:T(8,128)S(1)}, u32[]{:S(2)}, u32[]{:S(2)}) async-start(f32[8,24,128]{2,1,0:T(8,128)} %reduce_sums.1), calls=%async_computation | async-start | bytes 196608 | tf_op jit(solution)/shard_map/all_to_all | solution.py:504
  22.0 2.1 %edges.1 = (f32[2,16,16,128]{3,2,1,0:T(8,128)S(1)}, f32[2,16,16,128]{3,2,1,0:T(8,128)S(1)}, f32[3,18,16,128]{3,2,1,0:T(8,128)S(1)}, f32[3,2,16,128]{3,2,1,0:T(8,128)S(1)}) custom-call(f32[3,16,16,128]{3,2,1,0:T(8,128)S(1)} %get-tuple-element.23.v.refs_0_.refs_1_, s32[1,16,384]{2,1,0:T(8,128)S(1)} %get-tuple-element.26.slot.refs_1_, ...), custom_call_target="tpu_custom_call" | custom-call | flops 7851737088 | bytes 1048576 | tf_op jit(solution)/shard_map/edges/pallas_call | solution.py:63
  24.1 5.0 %all-to-all-done.refs_0_ = f32[8,24,128]{2,1,0:T(8,128)S(1)} async-done(((f32[8,24,128]{2,1,0:T(8,128)}), f32[8,24,128]{2,1,0:T(8,128)S(1)}, u32[]{:S(2)}, u32[]{:S(2)}) %all-to-all-start) | async-done | bytes 98336 | tf_op jit(solution)/shard_map/all_to_all | solution.py:504
  29.1 1.5 %advance.1 = f32[3,16,16,128]{3,2,1,0:T(8,128)} custom-call(f32[8,24,128]{2,1,0:T(8,128)S(1)} %all-to-all-done.refs_0_, f32[3,16,16,128]{3,2,1,0:T(8,128)S(1)} %get-tuple-element.23.v.refs_0_.refs_1_, s32[1,1,96]{2,1,0:T(1,128)S(1)} %get-tuple-element.24.tc.refs_2_, f32[104,128]{1,0:T(8,128)S(1)} %collective-permute-done.1.yo.refs_0_.refs_4_.refs_3_, ...), custom_call_target="tpu_custom_call" | custom-call | tf_op jit(solution)/shard_map/advance/pallas_call | solution.py:63
  (2 shorter events, 0.0 us)
Async XLA Ops:
  1.1 5.9 %collective-permute-start = (f32[200,128]{1,0:T(8,128)S(1)}, f32[200,128]{1,0:T(8,128)S(1)}, u32[]{:S(2)}, u32[]{:S(2)}) collective-permute-start(f32[200,128]{1,0:T(8,128)S(1)} %get-tuple-element.22), channel_id=1, source_target_pairs={{0,1},{1,0},{2,3},{3,2},{4,5},{5,4},{6,7},{7,6},{8,9},{9,8},{10,11... | collective-permute-start | bytes 307208 | tf_op jit(solution)/shard_map/ppermute | solution.py:53
  6.0 4.8 %collective-permute-start.2 = (f32[296,128]{1,0:T(8,128)S(1)}, f32[296,128]{1,0:T(8,128)S(1)}, u32[]{:S(2)}, u32[]{:S(2)}) collective-permute-start(f32[296,128]{1,0:T(8,128)S(1)} %get-tuple-element.32), channel_id=1, source_target_pairs={{0,8},{8,0},{16,24},{24,16},{1,9},{9,1},{17,25},{25,17},{2,10},{10... | collective-permute-start | bytes 454664 | tf_op jit(solution)/shard_map/ppermute | solution.py:53
  7.1 7.2 %collective-permute-start.1 = (f32[104,128]{1,0:T(8,128)S(1)}, f32[104,128]{1,0:T(8,128)S(1)}, u32[]{:S(2)}, u32[]{:S(2)}) collective-permute-start(f32[104,128]{1,0:T(8,128)S(1)} %pass_on_y.1), channel_id=1, source_target_pairs={{0,2},{2,4},{3,1},{4,6},{5,3},{7,5},{8,10},{10,12},{11,9},{12,14},... | collective-permute-start | bytes 159752 | tf_op jit(solution)/shard_map/ppermute | solution.py:59
  10.8 5.6 %collective-permute-start.3 = (f32[200,128]{1,0:T(8,128)S(1)}, f32[200,128]{1,0:T(8,128)S(1)}, u32[]{:S(2)}, u32[]{:S(2)}) collective-permute-start(f32[200,128]{1,0:T(8,128)S(1)} %pass_on_x.1), channel_id=1, source_target_pairs={{0,16},{24,8},{1,17},{25,9},{2,18},{26,10},{3,19},{27,11},{4,20},{... | collective-permute-start | bytes 307208 | tf_op jit(solution)/shard_map/ppermute | solution.py:59
  17.3 11.8 %all-to-all-start = ((f32[8,24,128]{2,1,0:T(8,128)}), f32[8,24,128]{2,1,0:T(8,128)S(1)}, u32[]{:S(2)}, u32[]{:S(2)}) async-start(f32[8,24,128]{2,1,0:T(8,128)} %reduce_sums.1), calls=%async_computation | async-start | bytes 196608 | tf_op jit(solution)/shard_map/all_to_all | solution.py:504

commit v6 on v4

--- a/solution.py
+++ b/solution.py
@@ -49,15 +49,19 @@
     return lax.rem(lax.axis_index(axis), 2) == 0
 
 
-def swap_pairs(count, first):
-    pairs = []
-    for i in range(first, count - 1, 2):
-        pairs += [(i, i + 1), (i + 1, i)]
-    return pairs
-
-
 def swap(x, axis, first):
-    return lax.ppermute(x, axis, swap_pairs(lax.axis_size(axis), first))
+    counts = {name: lax.axis_size(name) for name in ("gx", "gy")}
+    other = "gy" if axis == "gx" else "gx"
+
+    def device(along, across):
+        at = {axis: along, other: across}
+        return at["gx"] * counts["gy"] + at["gy"]
+
+    last = counts[axis] - 1
+    pairs = [(device(i, k), device(i + 1, k)) for i in range(first, last, 2) for k in range(counts[other])]
+    if first:
+        pairs += [(device(i, k), device(i, k + 1)) for i in (0, last) for k in range(0, counts[other], 2)]
+    return lax.ppermute(x, ("gx", "gy"), pairs + [(b, a) for a, b in pairs])
 
 
 def call(kernel, name, outs, args, scratch=(), flops=0, nbytes=0, space=pltpu.VMEM):
@@ -133,6 +137,15 @@
 
 def picked(flag, a, b, lo, hi):
     return jnp.where(flag, a[lo:hi, :], b[lo:hi, :])
+
+
+def low_edge(axis, odd, even_, lo, hi):
+    return jnp.where(lax.axis_index(axis) > 0, picked(even(axis), odd, even_, lo, hi), 0.0)
+
+
+def high_edge(axis, odd, even_, lo, hi):
+    there = lax.axis_index(axis) < lax.axis_size(axis) - 1
+    return jnp.where(there, picked(even(axis), even_, odd, lo, hi), 0.0)
 
 
 def histogram(v, tc, owner, slot, height, load, count_ref, load_ref, line, to_even, to_odd, sum_ref):
@@ -189,19 +202,18 @@
 
 def extend(v, yo, ye, xo, xe, field, comps):
     _, nx, ny, _ = v.shape
-    ev_x, ev_y = even("gx"), even("gy")
     for c in comps:
         out = c if len(comps) > 1 else 0
         field[out, 2 : 2 + nx, OWN : OWN + ny, :] = v[c, :, :, :]
         for k in range(2):
             at = (c * 2 + k) * nx
-            field[out, 2 : 2 + nx, OWN - 2 + k, :] = picked(ev_y, yo, ye, at, at + nx)
-            field[out, 2 : 2 + nx, OWN + ny + k, :] = picked(ev_y, ye, yo, at, at + nx)
+            field[out, 2 : 2 + nx, OWN - 2 + k, :] = low_edge("gy", yo, ye, at, at + nx)
+            field[out, 2 : 2 + nx, OWN + ny + k, :] = high_edge("gy", yo, ye, at, at + nx)
             at = (c * 2 + k) * ny
-            for x, a, b in ((k, xo, xe), (2 + nx + k, xe, xo)):
+            for x, edge in ((k, low_edge), (2 + nx + k, high_edge)):
                 field[out, x, 0:OWN, :] = jnp.zeros((OWN, LANES), F32)
                 field[out, x, OWN + ny : PLANE, :] = jnp.zeros((PLANE - OWN - ny, LANES), F32)
-                field[out, x, OWN : OWN + ny, :] = picked(ev_x, a, b, at, at + ny)
+                field[out, x, OWN : OWN + ny, :] = edge("gx", xo, xe, at, at + ny)
 
 
 def edge_slots(cell_row, cells):
@@ -228,10 +240,9 @@
     turbines, slots, levels = counts.shape
     _, nx, ny, _ = v.shape
     cells = nx * ny
-    ev = even("gy")
     field[0, 1 : 1 + nx, OWN : OWN + ny, :] = v[0, :, :, :]
-    field[0, 1 : 1 + nx, OWN - 1, :] = picked(ev, yo, ye, nx, 2 * nx)
-    field[0, 1 : 1 + nx, OWN + ny, :] = picked(ev, ye, yo, 0, nx)
+    field[0, 1 : 1 + nx, OWN - 1, :] = low_edge("gy", yo, ye, nx, 2 * nx)
+    field[0, 1 : 1 + nx, OWN + ny, :] = high_edge("gy", yo, ye, 0, nx)
     for x in (0, nx + 1):
         field[0, x, OWN : OWN + ny, :] = jnp.zeros((ny, levels), F32)
     update = stencil(field, 0, 1, nx, ny).reshape(cells, levels).astype(BF16)
@@ -263,8 +274,8 @@
 def reduce_sums(comps, ny, yo, ye, xo, xe, edge_counts, line, couple, out, sums):
     turbines = edge_counts.shape[0]
     ev_x = even("gx")
-    left = (SPREAD + CARRY) * picked(ev_x, xo, xe, ny, 2 * ny)
-    right = SPREAD * picked(ev_x, xe, xo, 0, ny)
+    left = (SPREAD + CARRY) * low_edge("gx", xo, xe, ny, 2 * ny)
+    right = SPREAD * high_edge("gx", xo, xe, 0, ny)
     for t in range(turbines):
         sides = edge_counts[t, 0:ny, :] * left + edge_counts[t, ny : 2 * ny, :] * right
         sums[t : t + 1, :] = jnp.sum(sides, axis=0, keepdims=True)
@@ -281,9 +292,9 @@
     above = []
     below = []
     for c in range(comps):
-        for a, b, at in ((xo, xe, (c * 2 + 1) * ny), (xe, xo, c * 2 * ny)):
-            above.append(picked(ev_x, a, b, at + ny - 1, at + ny))
-            below.append(picked(ev_x, a, b, at, at + 1))
+        for edge, at in ((low_edge, (c * 2 + 1) * ny), (high_edge, c * 2 * ny)):
+            above.append(edge("gx", xo, xe, at + ny - 1, at + ny))
+            below.append(edge("gx", xo, xe, at, at + 1))
     for i in range(2 * comps):
         for k in range(out.shape[0]):
             out[k, turbines + i : turbines + i + 1, :] = jnp.where(me + 1 == k, above[i], below[i])

time: 29.1 us -> 26.6 us (0.914)
  starting transfers between devices: 14.7 us -> 10.9 us
  waiting for transfers between devices: 5.68 us -> 7.06 us
    ppermute x4, starting transfers between devices: 10 us -> 6.18 us  [swap(): return lax.ppermute(x, ('gx', 'gy'), pairs + [(b, a) for a, b in pairs])]
    ppermute x4, waiting for transfers between devices: 0.02 us -> 2.07 us  [swap(): return lax.ppermute(x, ('gx', 'gy'), pairs + [(b, a) for a, b in pairs])]
    all_to_all x1, waiting for transfers between devices: 5.66 us -> 4.99 us  [body(): got = lax.all_to_all(chunk, 'gy', 0, 0)]
  transfers between devices with their start and end apart: 5 -> 5, of which waited for: 1 -> 2; matrix products, arithmetic and copies ran while one was open for 0% -> 0% of each run, Pallas kernels for 17% -> 19%
where the time goes in v6:
time: 26.6 us; the launch traced here: 26.3 us
  starting transfers between devices  10.9 us (41%)
  Pallas kernels  8.37 us (31%)
  waiting for transfers between devices  7.06 us (27%)
    pallas_call x6, Pallas kernels, call(): pl.pallas_call(kernel, out_shape=[jax.ShapeDtypeStruct(s, d) for s, d in...  8.37 us
    ppermute x4, starting transfers between devices, swap(): return lax.ppermute(x, ('gx', 'gy'), pairs + [(b, a) for a, b in pairs])  6.18 us
    all_to_all x1, waiting for transfers between devices, body(): got = lax.all_to_all(chunk, 'gy', 0, 0)  4.99 us
    all_to_all x1, starting transfers between devices, body(): got = lax.all_to_all(chunk, 'gy', 0, 0)  4.71 us
    ppermute x4, waiting for transfers between devices, swap(): return lax.ppermute(x, ('gx', 'gy'), pairs + [(b, a) for a, b in pairs])  2.07 us
  transfers between devices with their start and end apart: 5, of which 2 were waited for; matrix products, arithmetic and copies ran while one was open for 0% of the time, Pallas kernels for 19%

profile of v6, /device:TPU:0, one launch (start us, length us, event | category | flops | bytes accessed | tf_op | source)
XLA Modules:
  0.0 26.3 jit_solution(5059213352842533430)
XLA Ops:
  0.0 1.1 %stage.1 = (f32[3,16,16,128]{3,2,1,0:T(8,128)S(1)}, s32[1,1,96]{2,1,0:T(1,128)S(1)}, s32[1,16]{1,0:T(1,128)S(1)}, s32[1,16,384]{2,1,0:T(8,128)S(1)}, s32[1,16,38...) custom-call(f32[3,16,16,128]{3,2,1,0:T(8,128)} %v_hbm.1, ...), custom_call_target="tpu_custom_call" | custom-call | tf_op jit(solution)/shard_map/stage/pallas_call | solution.py:68
  1.1 0.5 %collective-permute-start = (f32[104,128]{1,0:T(8,128)S(1)}, f32[104,128]{1,0:T(8,128)S(1)}, u32[]{:S(2)}, u32[]{:S(2)}) collective-permute-start(f32[104,128]{1,0:T(8,128)S(1)} %get-tuple-element.24), channel_id=1, source_target_pairs={{1,2},{9,10},{17,18},{25,26},{3,4},{11,12},{19,20},{27,28},{5,6},{... | collective-permute-start | bytes 159752 | tf_op jit(solution)/shard_map/ppermute | solution.py:64
  1.7 4.0 %collective-permute-start.1 = (f32[104,128]{1,0:T(8,128)S(1)}, f32[104,128]{1,0:T(8,128)S(1)}, u32[]{:S(2)}, u32[]{:S(2)}) collective-permute-start(f32[104,128]{1,0:T(8,128)S(1)} %get-tuple-element.25), channel_id=1, source_target_pairs={{0,1},{8,9},{16,17},{24,25},{2,3},{10,11},{18,19},{26,27},{4,5},{1... | collective-permute-start | bytes 159752 | tf_op jit(solution)/shard_map/ppermute | solution.py:64
  5.7 1.8 %histogram.1 = (bf16[16,96,128]{2,1,0:T(8,128)(2,1)S(1)}, f32[16,96,128]{2,1,0:T(8,128)S(1)}, f32[8,128]{1,0:T(8,128)S(1)}, f32[200,128]{1,0:T(8,128)S(1)}, f32[200,128]{1,0:T(8,128)S(1)}) custom-call(f32[3,16,16,128]{3,2,1,0:T(8,128)S(1)} %get-tuple-element.26.v.refs_0_.refs_1_, s32[1,1,96]{2,1,0:T(1,128)S(1)} %get-tuple-element.27.tc.refs_2_, ...), custom_call_target="tpu_custom_call" | custom-call | flops 1962934272 | bytes 1048576 | tf_op jit(solution)/shard_map/histogram/pallas_call | solution.py:68
  7.5 0.0 collective-permute-start.2
  7.6 1.6 %collective-permute-start.3 = (f32[200,128]{1,0:T(8,128)S(1)}, f32[200,128]{1,0:T(8,128)S(1)}, u32[]{:S(2)}, u32[]{:S(2)}) collective-permute-start(f32[200,128]{1,0:T(8,128)S(1)} %get-tuple-element.33), channel_id=1, source_target_pairs={{0,8},{1,9},{2,10},{3,11},{4,12},{5,13},{6,14},{7,15},{16,24},{17,... | collective-permute-start | bytes 307208 | tf_op jit(solution)/shard_map/ppermute | solution.py:64
  9.2 0.0 collective-permute-done.yo.refs_0_.refs_4_.refs_3_
  9.2 0.0 collective-permute-done.1.ye.refs_1_.refs_5_.refs_4_
  9.2 1.0 %beside.1 = (f32[16,128]{1,0:T(8,128)S(1)}, f32[16,32,128]{2,1,0:T(8,128)S(1)}) custom-call(f32[3,16,16,128]{3,2,1,0:T(8,128)S(1)} %get-tuple-element.26.v.refs_0_.refs_1_, s32[1,1,96]{2,1,0:T(1,128)S(1)} %get-tuple-element.27.tc.refs_2_, f32[104,128]{1,0:T(8,128)S(1)} %collective-permute-done.yo.refs_0_.refs_4_.refs_3_, ...), custom_call_target="tpu_custom_call" | custom-call | flops 1962934272 | bytes 1048576 | tf_op jit(solution)/shard_map/beside/pallas_call | solution.py:68
  10.2 2.1 %collective-permute-done.2.refs_2_.refs_6_.refs_5_ = f32[200,128]{1,0:T(8,128)S(1)} collective-permute-done((f32[200,128]{1,0:T(8,128)S(1)}, f32[200,128]{1,0:T(8,128)S(1)}, u32[]{:S(2)}, u32[]{:S(2)}) %collective-permute-start.2) | collective-permute-done | bytes 102432 | tf_op jit(solution)/shard_map/ppermute | solution.py:64
  12.2 0.0 collective-permute-done.3.refs_3_.refs_7_.refs_6_
  12.2 0.8 %reduce_sums.1 = f32[8,24,128]{2,1,0:T(8,128)} custom-call(f32[104,128]{1,0:T(8,128)S(1)} %collective-permute-done.yo.refs_0_.refs_4_.refs_3_, f32[104,128]{1,0:T(8,128)S(1)} %collective-permute-done.1.ye.refs_1_.refs_5_.refs_4_, f32[200,128]{1,0:T(8,128)S(1)} %collective-permute-done.2.refs_2_.refs_6_.refs_5_, ...), custom_call_target="tpu_custom_call" | custom-call | tf_op jit(solution)/shard_map/reduce_sums/pallas_call | solution.py:68
  13.0 4.7 %all-to-all-start = ((f32[8,24,128]{2,1,0:T(8,128)}), f32[8,24,128]{2,1,0:T(8,128)S(1)}, u32[]{:S(2)}, u32[]{:S(2)}) async-start(f32[8,24,128]{2,1,0:T(8,128)} %reduce_sums.1), calls=%async_computation | async-start | bytes 196608 | tf_op jit(solution)/shard_map/all_to_all | solution.py:486
  17.7 2.1 %edges.1 = (f32[2,16,16,128]{3,2,1,0:T(8,128)S(1)}, f32[2,16,16,128]{3,2,1,0:T(8,128)S(1)}, f32[3,18,16,128]{3,2,1,0:T(8,128)S(1)}, f32[3,2,16,128]{3,2,1,0:T(8,128)S(1)}) custom-call(f32[3,16,16,128]{3,2,1,0:T(8,128)S(1)} %get-tuple-element.26.v.refs_0_.refs_1_, s32[1,16,384]{2,1,0:T(8,128)S(1)} %get-tuple-element.29.slot.refs_1_, ...), custom_call_target="tpu_custom_call" | custom-call | flops 1962934272 | bytes 1048576 | tf_op jit(solution)/shard_map/edges/pallas_call | solution.py:68
  19.8 5.0 %all-to-all-done.refs_0_ = f32[8,24,128]{2,1,0:T(8,128)S(1)} async-done(((f32[8,24,128]{2,1,0:T(8,128)}), f32[8,24,128]{2,1,0:T(8,128)S(1)}, u32[]{:S(2)}, u32[]{:S(2)}) %all-to-all-start) | async-done | bytes 98336 | tf_op jit(solution)/shard_map/all_to_all | solution.py:486
  24.8 1.5 %advance.1 = f32[3,16,16,128]{3,2,1,0:T(8,128)} custom-call(f32[8,24,128]{2,1,0:T(8,128)S(1)} %all-to-all-done.refs_0_, f32[3,16,16,128]{3,2,1,0:T(8,128)S(1)} %get-tuple-element.26.v.refs_0_.refs_1_, s32[1,1,96]{2,1,0:T(1,128)S(1)} %get-tuple-element.27.tc.refs_2_, f32[104,128]{1,0:T(8,128)S(1)} %collective-permute-done.yo.refs_0_.refs_4_.refs_3_, ...), custom_call_target="tpu_custom_call" | custom-call | tf_op jit(solution)/shard_map/advance/pallas_call | solution.py:68
Async XLA Ops:
  1.1 8.0 %collective-permute-start = (f32[104,128]{1,0:T(8,128)S(1)}, f32[104,128]{1,0:T(8,128)S(1)}, u32[]{:S(2)}, u32[]{:S(2)}) collective-permute-start(f32[104,128]{1,0:T(8,128)S(1)} %get-tuple-element.24), channel_id=1, source_target_pairs={{1,2},{9,10},{17,18},{25,26},{3,4},{11,12},{19,20},{27,28},{5,6},{... | collective-permute-start | bytes 159752 | tf_op jit(solution)/shard_map/ppermute | solution.py:64
  1.7 7.5 %collective-permute-start.1 = (f32[104,128]{1,0:T(8,128)S(1)}, f32[104,128]{1,0:T(8,128)S(1)}, u32[]{:S(2)}, u32[]{:S(2)}) collective-permute-start(f32[104,128]{1,0:T(8,128)S(1)} %get-tuple-element.25), channel_id=1, source_target_pairs={{0,1},{8,9},{16,17},{24,25},{2,3},{10,11},{18,19},{26,27},{4,5},{1... | collective-permute-start | bytes 159752 | tf_op jit(solution)/shard_map/ppermute | solution.py:64
  7.5 4.7 %collective-permute-start.2 = (f32[200,128]{1,0:T(8,128)S(1)}, f32[200,128]{1,0:T(8,128)S(1)}, u32[]{:S(2)}, u32[]{:S(2)}) collective-permute-start(f32[200,128]{1,0:T(8,128)S(1)} %get-tuple-element.32), channel_id=1, source_target_pairs={{8,16},{9,17},{10,18},{11,19},{12,20},{13,21},{14,22},{15,23},{0,1... | collective-permute-start | bytes 307208 | tf_op jit(solution)/shard_map/ppermute | solution.py:64
  7.6 4.7 %collective-permute-start.3 = (f32[200,128]{1,0:T(8,128)S(1)}, f32[200,128]{1,0:T(8,128)S(1)}, u32[]{:S(2)}, u32[]{:S(2)}) collective-permute-start(f32[200,128]{1,0:T(8,128)S(1)} %get-tuple-element.33), channel_id=1, source_target_pairs={{0,8},{1,9},{2,10},{3,11},{4,12},{5,13},{6,14},{7,15},{16,24},{17,... | collective-permute-start | bytes 307208 | tf_op jit(solution)/shard_map/ppermute | solution.py:64
  13.0 11.8 %all-to-all-start = ((f32[8,24,128]{2,1,0:T(8,128)}), f32[8,24,128]{2,1,0:T(8,128)S(1)}, u32[]{:S(2)}, u32[]{:S(2)}) async-start(f32[8,24,128]{2,1,0:T(8,128)} %reduce_sums.1), calls=%async_computation | async-start | bytes 196608 | tf_op jit(solution)/shard_map/all_to_all | solution.py:486

commit v7 on v6

--- a/solution.py
+++ b/solution.py
@@ -18,6 +18,7 @@
 PLANE = 32
 NO_SLOT = -30000.0
 SUMS, SCALE, CELLS = 0, 1, 2
+SIDE = 64
 
 
 def iota(shape, axis):
@@ -64,12 +65,12 @@
     return lax.ppermute(x, ("gx", "gy"), pairs + [(b, a) for a, b in pairs])
 
 
-def call(kernel, name, outs, args, scratch=(), flops=0, nbytes=0, space=pltpu.VMEM):
+def call(kernel, name, outs, args, scratch=(), flops=0, nbytes=0, space=pltpu.VMEM, out_space=pltpu.VMEM):
     return pl.pallas_call(
         kernel,
         out_shape=[jax.ShapeDtypeStruct(s, d) for s, d in outs],
         in_specs=[pl.BlockSpec(memory_space=space)] * len(args),
-        out_specs=[pl.BlockSpec(memory_space=pltpu.VMEM)] * len(outs),
+        out_specs=[pl.BlockSpec(memory_space=out_space)] * len(outs),
         scratch_shapes=list(scratch),
         compiler_params=pltpu.CompilerParams(vmem_limit_bytes=16 << 20),
         cost_estimate=pl.CostEstimate(flops=flops, bytes_accessed=nbytes, transcendentals=0),
@@ -125,14 +126,14 @@
         copy.wait()
 
 
-def as_column(row, n):
-    same = iota((n, n), 0) == iota((n, n), 1)
-    return jnp.sum(jnp.where(same, row, 0.0), axis=1, keepdims=True)
-
-
-def as_row(column, n):
-    same = iota((n, n), 0) == iota((n, n), 1)
-    return jnp.sum(jnp.where(same, column, 0.0), axis=0, keepdims=True)
+def as_column(row, n, start=0):
+    shape = (n, row.shape[1])
+    return jnp.sum(jnp.where(iota(shape, 0) + start == iota(shape, 1), row, 0.0), axis=1, keepdims=True)
+
+
+def as_row(column, lanes, start=0):
+    shape = (column.shape[0], lanes)
+    return jnp.sum(jnp.where(iota(shape, 0) + start == iota(shape, 1), column, 0.0), axis=0, keepdims=True)
 
 
 def picked(flag, a, b, lo, hi):
@@ -148,7 +149,7 @@
     return jnp.where(there, picked(even(axis), even_, odd, lo, hi), 0.0)
 
 
-def histogram(v, tc, owner, slot, height, load, count_ref, load_ref, line, to_even, to_odd, sum_ref):
+def histogram(v, tc, owner, slot, height, load, count_ref, line, to_even, to_odd, sum_ref):
     _, turbines, points = slot.shape
     slots, levels = count_ref.shape[1:]
     comps, nx, ny, _ = v.shape
@@ -156,18 +157,11 @@
     first = lax.axis_index("gy") * slots
     values = v[0, :, :, :].reshape(cells, levels).astype(BF16)
     rows = jnp.dot(pick_slots(tc, cells), values, preferred_element_type=F32)
-    zero = jnp.zeros((), BF16)
     for t in range(turbines):
         a = ones_at(one_hot(slots, slot[0, t : t + 1, :] - first))
-        at_z = one_hot(levels, height[0, t : t + 1, :])
-        weight = load[0, t : t + 1, :]
-        high = weight.astype(BF16)
-        low = (weight - high.astype(F32)).astype(BF16)
-        b = jnp.concatenate([ones_at(at_z), jnp.where(at_z, high, zero), jnp.where(at_z, low, zero)], axis=0)
-        both = lax.dot_general(a, b, NT, preferred_element_type=F32)
-        count = both[:, :levels]
+        b = ones_at(one_hot(levels, height[0, t : t + 1, :]))
+        count = lax.dot_general(a, b, NT, preferred_element_type=F32)
         count_ref[t] = count.astype(BF16)
-        load_ref[t] = both[:, levels : 2 * levels] + both[:, 2 * levels :]
         sum_ref[t : t + 1, :] = jnp.sum(count * rows, axis=0, keepdims=True)
 
     owner_row = jnp.broadcast_to(owner[...].astype(F32), (turbines, turbines))
@@ -176,8 +170,8 @@
     total = jnp.sum(jnp.where(member, load_row, 0.0), axis=1, keepdims=True)
     number = jnp.sum(jnp.where(member, 1.0, 0.0), axis=1, keepdims=True)
     line[...] = jnp.zeros((8, LANES), F32)
-    line[SUMS : SUMS + 1, 0:turbines] = as_row(jnp.sum(sum_ref[...], axis=1, keepdims=True), turbines)
-    line[SCALE : SCALE + 1, 0:turbines] = as_row(LOAD / (total / (number * points)), turbines)
+    line[SUMS : SUMS + 1, :] = as_row(jnp.sum(sum_ref[...], axis=1, keepdims=True), LANES, SIDE)
+    line[SCALE : SCALE + 1, :] = as_row(LOAD / (total / (number * points)), LANES)
     line[CELLS : CELLS + 1, 0:slots] = tc[0, :, :].astype(F32) + 1.0
 
     local = slot[0, :, :] - first
@@ -236,25 +230,28 @@
     return [both[2 * k * n : (2 * k + 1) * n] + both[(2 * k + 1) * n : (2 * k + 2) * n] for k in range(len(places))]
 
 
-def beside(v, tc, yo, ye, counts, loads, couple, edge_counts, products, field, sums):
+def pair_up(v, tc, slot, height, load, counts, loads, matrix, edge_counts, products):
     turbines, slots, levels = counts.shape
     _, nx, ny, _ = v.shape
     cells = nx * ny
-    field[0, 1 : 1 + nx, OWN : OWN + ny, :] = v[0, :, :, :]
-    field[0, 1 : 1 + nx, OWN - 1, :] = low_edge("gy", yo, ye, nx, 2 * nx)
-    field[0, 1 : 1 + nx, OWN + ny, :] = high_edge("gy", yo, ye, 0, nx)
-    for x in (0, nx + 1):
-        field[0, x, OWN : OWN + ny, :] = jnp.zeros((ny, levels), F32)
-    update = stencil(field, 0, 1, nx, ny).reshape(cells, levels).astype(BF16)
+    first = lax.axis_index("gy") * slots
+    zero = jnp.zeros((), BF16)
     values = v[0, :, :, :].reshape(cells, levels).astype(BF16)
-    both = jnp.dot(pick_slots(tc, cells), jnp.concatenate([values, update], axis=1), preferred_element_type=F32)
-    rows, later = both[:, :levels], both[:, levels:]
+    rows = jnp.dot(pick_slots(tc, cells), values, preferred_element_type=F32)
     row_x = iota((2 * ny, slots), 0)
     edge = jnp.where(row_x < ny, row_x, row_x + (nx - 2) * ny)
     select = jnp.where(edge == tc[0, :, :], 1.0, 0.0).astype(BF16)
     for t in range(turbines):
-        products[t] = (rows * loads[t]).astype(BF16)
-        sums[t : t + 1, :] = jnp.sum(counts[t].astype(F32) * later, axis=0, keepdims=True)
+        a = ones_at(one_hot(slots, slot[0, t : t + 1, :] - first))
+        at_z = one_hot(levels, height[0, t : t + 1, :])
+        weight = load[0, t : t + 1, :]
+        high = weight.astype(BF16)
+        low = (weight - high.astype(F32)).astype(BF16)
+        b = jnp.concatenate([jnp.where(at_z, high, zero), jnp.where(at_z, low, zero)], axis=0)
+        both = lax.dot_general(a, b, NT, preferred_element_type=F32)
+        both = both[:, :levels] + both[:, levels:]
+        loads[t] = both
+        products[t] = (rows * both).astype(BF16)
         edge_counts[t] = jnp.dot(select, counts[t], preferred_element_type=F32)
     block = 16
     wide = turbines * block
@@ -266,12 +263,27 @@
     keep = (iota((wide, wide), 0) & (block - 1)) == (iota((wide, wide), 1) & (block - 1))
     gram = jnp.sum(jnp.where(keep, gram, 0.0).reshape(turbines, block, wide), axis=1)
     select = jnp.where(iota((wide, LANES), 0) // block == iota((wide, LANES), 1), 1.0, 0.0)
-    matrix = jnp.dot(gram, select, precision=lax.Precision.HIGHEST, preferred_element_type=F32)
+    matrix[...] = jnp.dot(gram, select, precision=lax.Precision.HIGHEST, preferred_element_type=F32)
+
+
+def beside(v, tc, yo, ye, counts, matrix, couple, field, sums):
+    turbines, _, levels = counts.shape
+    _, nx, ny, _ = v.shape
+    cells = nx * ny
+    field[0, 1 : 1 + nx, OWN : OWN + ny, :] = v[0, :, :, :]
+    field[0, 1 : 1 + nx, OWN - 1, :] = low_edge("gy", yo, ye, nx, 2 * nx)
+    field[0, 1 : 1 + nx, OWN + ny, :] = high_edge("gy", yo, ye, 0, nx)
+    for x in (0, nx + 1):
+        field[0, x, OWN : OWN + ny, :] = jnp.zeros((ny, levels), F32)
+    update = stencil(field, 0, 1, nx, ny).reshape(cells, levels).astype(BF16)
+    later = jnp.dot(pick_slots(tc, cells), update, preferred_element_type=F32)
+    for t in range(turbines):
+        sums[t : t + 1, :] = jnp.sum(counts[t].astype(F32) * later, axis=0, keepdims=True)
     column = jnp.sum(sums[...], axis=1, keepdims=True)
-    couple[...] = jnp.where(iota((turbines, LANES), 1) == turbines, column, matrix)
-
-
-def reduce_sums(comps, ny, yo, ye, xo, xe, edge_counts, line, couple, out, sums):
+    couple[...] = jnp.where(iota((turbines, LANES), 1) == turbines, column, matrix[...])
+
+
+def reduce_sums(comps, ny, yo, ye, xo, xe, edge_counts, line, couple, out, sums, corners):
     turbines = edge_counts.shape[0]
     ev_x = even("gx")
     left = (SPREAD + CARRY) * low_edge("gx", xo, xe, ny, 2 * ny)
@@ -279,28 +291,26 @@
     for t in range(turbines):
         sides = edge_counts[t, 0:ny, :] * left + edge_counts[t, ny : 2 * ny, :] * right
         sums[t : t + 1, :] = jnp.sum(sides, axis=0, keepdims=True)
-    lane = iota((turbines, LANES), 1)
+    corners[...] = jnp.zeros((2, 8, LANES), F32)
+    for c in range(comps):
+        for i, (edge, at) in enumerate(((low_edge, (c * 2 + 1) * ny), (high_edge, c * 2 * ny))):
+            corners[0, 2 * c + i : 2 * c + i + 1, :] = edge("gx", xo, xe, at, at + 1)
+            corners[1, 2 * c + i : 2 * c + i + 1, :] = edge("gx", xo, xe, at + ny - 1, at + ny)
     at = xe.shape[0] - 8 + SUMS
-    result = couple[...] + jnp.where(lane == turbines, jnp.sum(sums[...], axis=1, keepdims=True), 0.0)
+    lane, row = iota((turbines, LANES), 1), iota((turbines, LANES), 0)
+    result = couple[...]
     rows_of = (line[SUMS : SUMS + 1, :], picked(ev_x, xo, xe, at, at + 1), picked(ev_x, xe, xo, at, at + 1))
-    for k, row in enumerate(rows_of):
-        result = jnp.where(lane == turbines + 1 + k, as_column(row[:, :turbines], turbines), result)
+    for k, sums_row in enumerate(rows_of):
+        result = result + jnp.where(row == k, sums_row, 0.0)
+    result = result + jnp.where(lane == turbines, jnp.sum(sums[...], axis=1, keepdims=True), 0.0)
     me = lax.axis_index("gy")
+    below, above = corners[0], corners[1]
     for k in range(out.shape[0]):
         out[k, 0:turbines, :] = result
-        out[k, turbines : turbines + 8, :] = jnp.zeros((8, LANES), F32)
-    above = []
-    below = []
-    for c in range(comps):
-        for edge, at in ((low_edge, (c * 2 + 1) * ny), (high_edge, c * 2 * ny)):
-            above.append(edge("gx", xo, xe, at + ny - 1, at + ny))
-            below.append(edge("gx", xo, xe, at, at + 1))
-    for i in range(2 * comps):
-        for k in range(out.shape[0]):
-            out[k, turbines + i : turbines + i + 1, :] = jnp.where(me + 1 == k, above[i], below[i])
-
-
-def edges(slots, pieces, v, slot, height, load, yo, ye, xo, xe, edge_x, edge_y, update_ref, strip_ref, field):
+        out[k, turbines : turbines + 8, :] = jnp.where(me + 1 == k, above, below)
+
+
+def edges(slots, pieces, v, slot, height, load, yo, ye, xo, xe, line, edge_x, edge_y, update_ref, strip_ref, scales, field):
     comps, nx, ny, levels = v.shape
     turbines = edge_x.shape[1]
     ev, ev_y = even("gx"), even("gy")
@@ -316,6 +326,10 @@
             others = picked(ev_y, a, b, far, far + nx) + v[c, :, y, :] + lane_edge(center)
             strip_ref[c, k] = moved(center, before, after, others)
 
+    at = xe.shape[0] - 8 + SCALE
+    rows_of = (line[SCALE : SCALE + 1, :], picked(ev, xo, xe, at, at + 1), picked(ev, xe, xo, at, at + 1))
+    for k, row in enumerate(rows_of):
+        scales[k] = jnp.broadcast_to(as_column(row, turbines), (turbines, LANES))
     at = xe.shape[0] - 8 + CELLS
     code_at = comps * 2 * ny
     load_at = code_at + pieces * turbines
@@ -343,7 +357,7 @@
         edge_y[0, t], edge_y[1, t] = spread(places, height[0, t : t + 1, :], load[0, t : t + 1, :])
 
 
-def advance(points, got, v, tc, yo, ye, xo, xe, line, loads, edge_x, edge_y, update_ref, strip_ref, out, field, parts):
+def advance(points, got, v, tc, yo, ye, xo, xe, scales, loads, edge_x, edge_y, update_ref, strip_ref, out, field, parts, result, sems):
     comps, nx, ny, levels = v.shape
     turbines, slots, _ = loads.shape
     cells = nx * ny
@@ -353,20 +367,14 @@
         total = total + got[k, 0:turbines, :]
     lane = iota((turbines, LANES), 1)
 
-    def column(k):
-        return jnp.sum(jnp.where(lane == k, total, 0.0), axis=1, keepdims=True)
-
-    def coefs(scales, sums):
-        return -(scales * (FREE_WIND + sums / points))
-
-    at = xe.shape[0] - 8 + SCALE
-    scale = as_column(line[SCALE : SCALE + 1, :turbines], turbines)
-    own = coefs(scale, column(turbines + 1))
-    left = coefs(as_column(picked(ev_x, xo, xe, at, at + 1)[:, :turbines], turbines), column(turbines + 2))
-    right = coefs(as_column(picked(ev_x, xe, xo, at, at + 1)[:, :turbines], turbines), column(turbines + 3))
+    def coefs(scale, sums):
+        return -(scale * (FREE_WIND + sums / points))
+
+    own, left, right = (coefs(scales[k], as_column(total[k : k + 1, :], turbines, SIDE)) for k in range(3))
     own_row = jnp.sum(jnp.where(iota((turbines, LANES), 0) == lane, own, 0.0), axis=0, keepdims=True)
     forced = jnp.sum(jnp.where(lane < turbines, total * own_row, 0.0), axis=1, keepdims=True)
-    later = coefs(scale, column(turbines) + forced)
+    plain = jnp.sum(jnp.where(lane == turbines, total, 0.0), axis=1, keepdims=True)
+    later = coefs(scales[0], plain + forced)
 
     for s in range(0, slots, 16):
         first = jnp.zeros((16, levels), F32)
@@ -421,9 +429,14 @@
             extra = extra + jnp.where(row_x == nx - 1, SPREAD * corner[1][k], 0.0)
             value = strip_ref[c, k] + extra + push
             field[c, 1 : 1 + nx, y, :] = jnp.where(there_y[k], value, 0.0)
+    copies = []
     for c in range(comps):
         now = field[c, 1 : 1 + nx, OWN : OWN + ny, :]
-        out[c] = stencil(field, c, 1, nx, ny) + rounded(rounded(now) * second)
+        result[c] = stencil(field, c, 1, nx, ny) + rounded(rounded(now) * second)
+        copies.append(pltpu.make_async_copy(result.at[c], out.at[c], sems.at[c]))
+        copies[c].start()
+    for copy in copies:
+        copy.wait()
 
 
 def body(velocity, tile_cells, owner, point_slot, point_z, loading):
@@ -449,12 +462,11 @@
         space=pltpu.HBM,
     )
     yo, ye = swap(y_odd, "gy", 1), swap(y_even, "gy", 0)
-    counts, loads, line, x_even, x_odd = call(
+    counts, line, x_even, x_odd = call(
         histogram,
         "histogram",
         [
             ((turbines, slots, levels), BF16),
-            ((turbines, slots, levels), F32),
             ((8, LANES), F32),
             ((rows_x, levels), F32),
             ((rows_x, levels), F32),
@@ -464,13 +476,22 @@
         **work,
     )
     xo, xe = swap(x_odd, "gx", 1), swap(x_even, "gx", 0)
-    couple, edge_counts = call(
+    loads, matrix, edge_counts = call(
+        pair_up,
+        "pair_up",
+        [((turbines, slots, levels), F32), ((turbines, LANES), F32), ((turbines, 2 * ny, levels), F32)],
+        (v, tc, slot, height, load, counts),
+        [pltpu.VMEM((turbines, slots, levels), BF16)],
+        **work,
+    )
+    (couple,) = call(
         beside,
         "beside",
-        [((turbines, LANES), F32), ((turbines, 2 * ny, levels), F32)],
-        (v, tc, yo, ye, counts, loads),
-        [pltpu.VMEM((turbines, slots, levels), BF16), field(1, nx + 2), pltpu.VMEM((turbines, levels), F32)],
-        **work,
+        [((turbines, LANES), F32)],
+        (v, tc, yo, ye, counts, matrix),
+        [field(1, nx + 2), pltpu.VMEM((turbines, levels), F32)],
+        flops=work["flops"] // 4,
+        nbytes=work["nbytes"],
     )
 
     def reduce_of(*refs):
@@ -481,14 +502,14 @@
         "reduce_sums",
         [((tiles_y, turbines + 8, LANES), F32)],
         (yo, ye, xo, xe, edge_counts, line, couple),
-        [pltpu.VMEM((turbines, levels), F32)],
+        [pltpu.VMEM((turbines, levels), F32), pltpu.VMEM((2, 8, LANES), F32)],
     )
     got = lax.all_to_all(chunk, "gy", 0, 0)
 
     def edges_of(*refs):
         return edges(slots, pieces, *refs)
 
-    edge_x, edge_y, update, strip = call(
+    edge_x, edge_y, update, strip, scales = call(
         edges_of,
         "edges",
         [
@@ -496,8 +517,9 @@
             ((2, turbines, nx, levels), F32),
             ((comps, nx + 2, ny, levels), F32),
             ((comps, 2, nx, levels), F32),
+            ((3, turbines, LANES), F32),
         ],
-        (v, slot, height, load, yo, ye, xo, xe),
+        (v, slot, height, load, yo, ye, xo, xe, line),
         [field(comps, nx + 4)],
         **work,
     )
@@ -509,8 +531,14 @@
         advance_by,
         "advance",
         [(velocity.shape, F32)],
-        (got, v, tc, yo, ye, xo, xe, line, loads, edge_x, edge_y, update, strip),
-        [field(comps, nx + 2), pltpu.VMEM((slots, 4 * levels), BF16)],
+        (got, v, tc, yo, ye, xo, xe, scales, loads, edge_x, edge_y, update, strip),
+        [
+            field(comps, nx + 2),
+            pltpu.VMEM((slots, 4 * levels), BF16),
+            pltpu.VMEM(velocity.shape, F32),
+            pltpu.SemaphoreType.DMA((comps,)),
+        ],
+        out_space=pltpu.HBM,
     )
     return out
 

time: 26.6 us -> 25.7 us (0.966)
  waiting for transfers between devices: 7.06 us -> 5.39 us
  Pallas kernels: 8.37 us -> 9.12 us
    ppermute x4, waiting for transfers between devices: 2.07 us -> 0.43 us  [swap(): return lax.ppermute(x, ('gx', 'gy'), pairs + [(b, a) for a, b in pairs])]
    pallas_call x6 -> x7, Pallas kernels: 8.37 us -> 9.12 us  [call(): pl.pallas_call(kernel, out_shape=[jax.ShapeDtypeStruct(s, d) for s, d in...]
  transfers between devices with their start and end apart: 5 -> 5, of which waited for: 2 -> 2; matrix products, arithmetic and copies ran while one was open for 0% -> 0% of each run, Pallas kernels for 19% -> 23%
where the time goes in v7:
time: 25.7 us; the launch traced here: 25.4 us
  starting transfers between devices  10.9 us (42%)
  Pallas kernels  9.12 us (35%)
  waiting for transfers between devices  5.39 us (21%)
    pallas_call x7, Pallas kernels, call(): pl.pallas_call(kernel, out_shape=[jax.ShapeDtypeStruct(s, d) for s, d in...  9.12 us
    ppermute x4, starting transfers between devices, swap(): return lax.ppermute(x, ('gx', 'gy'), pairs + [(b, a) for a, b in pairs])  6.16 us
    all_to_all x1, waiting for transfers between devices, body(): got = lax.all_to_all(chunk, 'gy', 0, 0)  4.97 us
    all_to_all x1, starting transfers between devices, body(): got = lax.all_to_all(chunk, 'gy', 0, 0)  4.71 us
  transfers between devices with their start and end apart: 5, of which 2 were waited for; matrix products, arithmetic and copies ran while one was open for 0% of the time, Pallas kernels for 23%

profile of v7, /device:TPU:0, one launch (start us, length us, event | category | flops | bytes accessed | tf_op | source)
XLA Modules:
  0.0 25.4 jit_solution(11832291617265660164)
XLA Ops:
  0.0 1.1 %stage.1 = (f32[3,16,16,128]{3,2,1,0:T(8,128)S(1)}, s32[1,1,96]{2,1,0:T(1,128)S(1)}, s32[1,16]{1,0:T(1,128)S(1)}, s32[1,16,384]{2,1,0:T(8,128)S(1)}, s32[1,16,38...) custom-call(f32[3,16,16,128]{3,2,1,0:T(8,128)} %v_hbm.1, ...), custom_call_target="tpu_custom_call" | custom-call | tf_op jit(solution)/shard_map/stage/pallas_call | solution.py:69
  1.1 0.5 %collective-permute-start = (f32[104,128]{1,0:T(8,128)S(1)}, f32[104,128]{1,0:T(8,128)S(1)}, u32[]{:S(2)}, u32[]{:S(2)}) collective-permute-start(f32[104,128]{1,0:T(8,128)S(1)} %get-tuple-element.25), channel_id=1, source_target_pairs={{1,2},{9,10},{17,18},{25,26},{3,4},{11,12},{19,20},{27,28},{5,6},{... | collective-permute-start | bytes 159752 | tf_op jit(solution)/shard_map/ppermute | solution.py:65
  1.7 4.0 %collective-permute-start.1 = (f32[104,128]{1,0:T(8,128)S(1)}, f32[104,128]{1,0:T(8,128)S(1)}, u32[]{:S(2)}, u32[]{:S(2)}) collective-permute-start(f32[104,128]{1,0:T(8,128)S(1)} %get-tuple-element.26), channel_id=1, source_target_pairs={{0,1},{8,9},{16,17},{24,25},{2,3},{10,11},{18,19},{26,27},{4,5},{1... | collective-permute-start | bytes 159752 | tf_op jit(solution)/shard_map/ppermute | solution.py:65
  5.7 1.0 %histogram.1 = (bf16[16,96,128]{2,1,0:T(8,128)(2,1)S(1)}, f32[8,128]{1,0:T(8,128)S(1)}, f32[200,128]{1,0:T(8,128)S(1)}, f32[200,128]{1,0:T(8,128)S(1)}) custom-call(f32[3,16,16,128]{3,2,1,0:T(8,128)S(1)} %get-tuple-element.27.v.refs_0_.refs_1_, s32[1,1,96]{2,1,0:T(1,128)S(1)} %get-tuple-element.28.tc.refs_2_, s32[1,16]{1,0:T(1,128)S(1)} %get-tuple-element.29.owner, ...), custom_call_target="tpu_custom_call" | custom-call | flops 1962934272 | bytes 1048576 | tf_op jit(solution)/shard_map/histogram/pallas_call | solution.py:69
  6.7 0.0 collective-permute-start.2
  6.7 1.6 %collective-permute-start.3 = (f32[200,128]{1,0:T(8,128)S(1)}, f32[200,128]{1,0:T(8,128)S(1)}, u32[]{:S(2)}, u32[]{:S(2)}) collective-permute-start(f32[200,128]{1,0:T(8,128)S(1)} %get-tuple-element.34), channel_id=1, source_target_pairs={{0,8},{1,9},{2,10},{3,11},{4,12},{5,13},{6,14},{7,15},{16,24},{17,... | collective-permute-start | bytes 307208 | tf_op jit(solution)/shard_map/ppermute | solution.py:65
  8.3 2.2 %pair_up.1 = (f32[16,96,128]{2,1,0:T(8,128)S(1)}, f32[16,128]{1,0:T(8,128)S(1)}, f32[16,32,128]{2,1,0:T(8,128)S(1)}) custom-call(f32[3,16,16,128]{3,2,1,0:T(8,128)S(1)} %get-tuple-element.27.v.refs_0_.refs_1_, s32[1,1,96]{2,1,0:T(1,128)S(1)} %get-tuple-element.28.tc.refs_2_, s32[1,16,384]{2,1,0:T(8,128)S(1)} %get-tuple-element.30.slot.refs_1_, ...), custom_call_target="tpu_custom_call" | custom-call | flops 1962934272 | bytes 1048576 | tf_op jit(solution)/shard_map/pair_up/pallas_call | solution.py:69
  10.4 0.0 collective-permute-done.yo.refs_0_.refs_4_.refs_3_
  10.4 0.0 collective-permute-done.1.ye.refs_1_.refs_5_.refs_4_
  10.5 0.5 %beside.1.refs_6_ = f32[16,128]{1,0:T(8,128)S(1)} custom-call(f32[3,16,16,128]{3,2,1,0:T(8,128)S(1)} %get-tuple-element.27.v.refs_0_.refs_1_, s32[1,1,96]{2,1,0:T(1,128)S(1)} %get-tuple-element.28.tc.refs_2_, f32[104,128]{1,0:T(8,128)S(1)} %collective-permute-done.yo.refs_0_.refs_4_.refs_3_, ...), custom_call_target="tpu_custom_call" | custom-call | flops 490733568 | bytes 1048576 | tf_op jit(solution)/shard_map/beside/pallas_call | solution.py:69
  10.9 0.4 %collective-permute-done.2.refs_2_.refs_6_.refs_5_ = f32[200,128]{1,0:T(8,128)S(1)} collective-permute-done((f32[200,128]{1,0:T(8,128)S(1)}, f32[200,128]{1,0:T(8,128)S(1)}, u32[]{:S(2)}, u32[]{:S(2)}) %collective-permute-start.2) | collective-permute-done | bytes 102432 | tf_op jit(solution)/shard_map/ppermute | solution.py:65
  11.3 0.0 collective-permute-done.3.refs_3_.refs_7_.refs_6_
  11.3 0.8 %reduce_sums.1 = f32[8,24,128]{2,1,0:T(8,128)} custom-call(f32[104,128]{1,0:T(8,128)S(1)} %collective-permute-done.yo.refs_0_.refs_4_.refs_3_, f32[104,128]{1,0:T(8,128)S(1)} %collective-permute-done.1.ye.refs_1_.refs_5_.refs_4_, f32[200,128]{1,0:T(8,128)S(1)} %collective-permute-done.2.refs_2_.refs_6_.refs_5_, ...), custom_call_target="tpu_custom_call" | custom-call | tf_op jit(solution)/shard_map/reduce_sums/pallas_call | solution.py:69
  12.1 4.7 %all-to-all-start = ((f32[8,24,128]{2,1,0:T(8,128)}), f32[8,24,128]{2,1,0:T(8,128)S(1)}, u32[]{:S(2)}, u32[]{:S(2)}) async-start(f32[8,24,128]{2,1,0:T(8,128)} %reduce_sums.1), calls=%async_computation | async-start | bytes 196608 | tf_op jit(solution)/shard_map/all_to_all | solution.py:507
  16.8 2.2 %edges.1 = (f32[2,16,16,128]{3,2,1,0:T(8,128)S(1)}, f32[2,16,16,128]{3,2,1,0:T(8,128)S(1)}, f32[3,18,16,128]{3,2,1,0:T(8,128)S(1)}, f32[3,2,16,128]{3,2,1,0:T(8,128)S(1)}, f32[3,16,128]{2,1,0:T(8,128)S(1)}) custom-call(f32[3,16,16,128]{3,2,1,0:T(8,128)S(1)} %get-tuple-element.27.v.refs_0_.refs_1_, s32[1,16,384]{2,1,0:T(8,128)S(1)} %get-tuple-element.30.slot.refs_1_, ...), custom_call_target="tpu_custom_call" | custom-call | flops 1962934272 | bytes 1048576 | tf_op jit(solution)/shard_map/edges/pallas_call | solution.py:69
  19.0 5.0 %all-to-all-done.refs_0_ = f32[8,24,128]{2,1,0:T(8,128)S(1)} async-done(((f32[8,24,128]{2,1,0:T(8,128)}), f32[8,24,128]{2,1,0:T(8,128)S(1)}, u32[]{:S(2)}, u32[]{:S(2)}) %all-to-all-start) | async-done | bytes 98336 | tf_op jit(solution)/shard_map/all_to_all | solution.py:507
  23.9 1.5 %advance.1 = f32[3,16,16,128]{3,2,1,0:T(8,128)} custom-call(f32[8,24,128]{2,1,0:T(8,128)S(1)} %all-to-all-done.refs_0_, f32[3,16,16,128]{3,2,1,0:T(8,128)S(1)} %get-tuple-element.27.v.refs_0_.refs_1_, s32[1,1,96]{2,1,0:T(1,128)S(1)} %get-tuple-element.28.tc.refs_2_, f32[104,128]{1,0:T(8,128)S(1)} %collective-permute-done.yo.refs_0_.refs_4_.refs_3_, ...), custom_call_target="tpu_custom_call" | custom-call | tf_op jit(solution)/shard_map/advance/pallas_call | solution.py:69
Async XLA Ops:
  1.1 9.3 %collective-permute-start = (f32[104,128]{1,0:T(8,128)S(1)}, f32[104,128]{1,0:T(8,128)S(1)}, u32[]{:S(2)}, u32[]{:S(2)}) collective-permute-start(f32[104,128]{1,0:T(8,128)S(1)} %get-tuple-element.25), channel_id=1, source_target_pairs={{1,2},{9,10},{17,18},{25,26},{3,4},{11,12},{19,20},{27,28},{5,6},{... | collective-permute-start | bytes 159752 | tf_op jit(solution)/shard_map/ppermute | solution.py:65
  1.7 8.8 %collective-permute-start.1 = (f32[104,128]{1,0:T(8,128)S(1)}, f32[104,128]{1,0:T(8,128)S(1)}, u32[]{:S(2)}, u32[]{:S(2)}) collective-permute-start(f32[104,128]{1,0:T(8,128)S(1)} %get-tuple-element.26), channel_id=1, source_target_pairs={{0,1},{8,9},{16,17},{24,25},{2,3},{10,11},{18,19},{26,27},{4,5},{1... | collective-permute-start | bytes 159752 | tf_op jit(solution)/shard_map/ppermute | solution.py:65
  6.7 4.7 %collective-permute-start.2 = (f32[200,128]{1,0:T(8,128)S(1)}, f32[200,128]{1,0:T(8,128)S(1)}, u32[]{:S(2)}, u32[]{:S(2)}) collective-permute-start(f32[200,128]{1,0:T(8,128)S(1)} %get-tuple-element.33), channel_id=1, source_target_pairs={{8,16},{9,17},{10,18},{11,19},{12,20},{13,21},{14,22},{15,23},{0,1... | collective-permute-start | bytes 307208 | tf_op jit(solution)/shard_map/ppermute | solution.py:65
  6.7 4.7 %collective-permute-start.3 = (f32[200,128]{1,0:T(8,128)S(1)}, f32[200,128]{1,0:T(8,128)S(1)}, u32[]{:S(2)}, u32[]{:S(2)}) collective-permute-start(f32[200,128]{1,0:T(8,128)S(1)} %get-tuple-element.34), channel_id=1, source_target_pairs={{0,8},{1,9},{2,10},{3,11},{4,12},{5,13},{6,14},{7,15},{16,24},{17,... | collective-permute-start | bytes 307208 | tf_op jit(solution)/shard_map/ppermute | solution.py:65
  12.1 11.8 %all-to-all-start = ((f32[8,24,128]{2,1,0:T(8,128)}), f32[8,24,128]{2,1,0:T(8,128)S(1)}, u32[]{:S(2)}, u32[]{:S(2)}) async-start(f32[8,24,128]{2,1,0:T(8,128)} %reduce_sums.1), calls=%async_computation | async-start | bytes 196608 | tf_op jit(solution)/shard_map/all_to_all | solution.py:507

commit v8 on v7

--- a/solution.py
+++ b/solution.py
@@ -18,7 +18,6 @@
 PLANE = 32
 NO_SLOT = -30000.0
 SUMS, SCALE, CELLS = 0, 1, 2
-SIDE = 64
 
 
 def iota(shape, axis):
@@ -88,8 +87,8 @@
 
 
 def moved(center, before, after, beside):
-    beside = beside + before + after
-    return center + SPREAD * (beside - 6.0 * center) - CARRY * (center - before)
+    own = (1.0 - 6.0 * SPREAD - CARRY) * center
+    return own + SPREAD * (beside + after) + (SPREAD + CARRY) * before
 
 
 def stencil(ref, c, x0, nx, ny):
@@ -100,67 +99,79 @@
     return moved(center, before, after, beside + lane_edge(center))
 
 
-def stage(v_hbm, tc_hbm, owner_hbm, slot_hbm, height_hbm, load_hbm, v, tc, owner, slot, height, load, to_even, to_odd, sems):
-    pairs = ((v_hbm, v), (tc_hbm, tc), (slot_hbm, slot), (height_hbm, height), (load_hbm, load), (owner_hbm, owner))
+def as_column(row, n, start=0):
+    shape = (n, row.shape[1])
+    return jnp.sum(jnp.where(iota(shape, 0) + start == iota(shape, 1), row, 0.0), axis=1, keepdims=True)
+
+
+def as_row(column, lanes, start=0):
+    shape = (column.shape[0], lanes)
+    return jnp.sum(jnp.where(iota(shape, 0) + start == iota(shape, 1), column, 0.0), axis=0, keepdims=True)
+
+
+def packing(turbines):
+    per_row = LANES // turbines
+    rows = turbines // per_row
+    return rows, per_row, 2 * rows + 3, -(-(2 * rows + 9) // 16) * 16
+
+
+def in_parts(x, count):
+    parts = []
+    for _ in range(count):
+        parts.append(rounded(x))
+        x = x - parts[-1]
+    return parts
+
+
+def picked(flag, a, b, lo, hi):
+    return jnp.where(flag, a[lo:hi, :], b[lo:hi, :])
+
+
+def low_edge(axis, odd, even_, lo, hi):
+    return jnp.where(lax.axis_index(axis) > 0, picked(even(axis), odd, even_, lo, hi), 0.0)
+
+
+def high_edge(axis, odd, even_, lo, hi):
+    there = lax.axis_index(axis) < lax.axis_size(axis) - 1
+    return jnp.where(there, picked(even(axis), even_, odd, lo, hi), 0.0)
+
+
+def prepare(
+    v_hbm, tc_hbm, owner_hbm, slot_hbm, height_hbm, load_hbm,
+    v, tc, slot, height, load, count_ref, line, y_even, y_odd, x_even, x_odd,
+    owner, exact, sum_ref, sems,
+):
+    pairs = ((slot_hbm, slot), (height_hbm, height), (tc_hbm, tc), (load_hbm, load), (owner_hbm, owner), (v_hbm, v))
     copies = [pltpu.make_async_copy(a, b, sems.at[i]) for i, (a, b) in enumerate(pairs)]
     for copy in copies:
         copy.start()
-    copies[0].wait()
-    comps, nx, ny, _ = v.shape
-    ev = even("gy")
-    at = 0
-    for c in range(comps):
-        for k in range(2):
-            high = v[c, :, ny - 2 + k, :]
-            low = v[c, :, k, :]
-            to_even[at : at + nx, :] = jnp.where(ev, high, low)
-            to_odd[at : at + nx, :] = jnp.where(ev, low, high)
-            at += nx
-    copies[1].wait()
-    cells = tc[0, :, :].astype(F32) + 1.0
-    slots = cells.shape[1]
-    for out in (to_even, to_odd):
-        out[at : at + 8, :] = jnp.zeros((8, LANES), F32)
-        out[at : at + 1, 0:slots] = cells
-    for copy in copies[2:]:
-        copy.wait()
-
-
-def as_column(row, n, start=0):
-    shape = (n, row.shape[1])
-    return jnp.sum(jnp.where(iota(shape, 0) + start == iota(shape, 1), row, 0.0), axis=1, keepdims=True)
-
-
-def as_row(column, lanes, start=0):
-    shape = (column.shape[0], lanes)
-    return jnp.sum(jnp.where(iota(shape, 0) + start == iota(shape, 1), column, 0.0), axis=0, keepdims=True)
-
-
-def picked(flag, a, b, lo, hi):
-    return jnp.where(flag, a[lo:hi, :], b[lo:hi, :])
-
-
-def low_edge(axis, odd, even_, lo, hi):
-    return jnp.where(lax.axis_index(axis) > 0, picked(even(axis), odd, even_, lo, hi), 0.0)
-
-
-def high_edge(axis, odd, even_, lo, hi):
-    there = lax.axis_index(axis) < lax.axis_size(axis) - 1
-    return jnp.where(there, picked(even(axis), even_, odd, lo, hi), 0.0)
-
-
-def histogram(v, tc, owner, slot, height, load, count_ref, line, to_even, to_odd, sum_ref):
     _, turbines, points = slot.shape
     slots, levels = count_ref.shape[1:]
     comps, nx, ny, _ = v.shape
     cells = nx * ny
     first = lax.axis_index("gy") * slots
+    copies[0].wait()
+    copies[1].wait()
+    for t in range(turbines):
+        a = ones_at(one_hot(slots, slot[0, t : t + 1, :] - first))
+        b = ones_at(one_hot(levels, height[0, t : t + 1, :]))
+        exact[t] = lax.dot_general(a, b, NT, preferred_element_type=F32)
+    for copy in copies[2:]:
+        copy.wait()
+
+    ev = even("gy")
+    at = 0
+    for c in range(comps):
+        for k in range(2):
+            high = v[c, :, ny - 2 + k, :]
+            low = v[c, :, k, :]
+            y_even[at : at + nx, :] = jnp.where(ev, high, low)
+            y_odd[at : at + nx, :] = jnp.where(ev, low, high)
+            at += nx
     values = v[0, :, :, :].reshape(cells, levels).astype(BF16)
     rows = jnp.dot(pick_slots(tc, cells), values, preferred_element_type=F32)
     for t in range(turbines):
-        a = ones_at(one_hot(slots, slot[0, t : t + 1, :] - first))
-        b = ones_at(one_hot(levels, height[0, t : t + 1, :]))
-        count = lax.dot_general(a, b, NT, preferred_element_type=F32)
+        count = exact[t]
         count_ref[t] = count.astype(BF16)
         sum_ref[t : t + 1, :] = jnp.sum(count * rows, axis=0, keepdims=True)
 
@@ -170,9 +181,12 @@
     total = jnp.sum(jnp.where(member, load_row, 0.0), axis=1, keepdims=True)
     number = jnp.sum(jnp.where(member, 1.0, 0.0), axis=1, keepdims=True)
     line[...] = jnp.zeros((8, LANES), F32)
-    line[SUMS : SUMS + 1, :] = as_row(jnp.sum(sum_ref[...], axis=1, keepdims=True), LANES, SIDE)
+    line[SUMS : SUMS + 1, :] = as_row(jnp.sum(sum_ref[...], axis=1, keepdims=True), LANES)
     line[SCALE : SCALE + 1, :] = as_row(LOAD / (total / (number * points)), LANES)
     line[CELLS : CELLS + 1, 0:slots] = tc[0, :, :].astype(F32) + 1.0
+    for out in (y_even, y_odd):
+        out[at : at + 8, :] = jnp.zeros((8, LANES), F32)
+        out[at : at + 1, :] = line[CELLS : CELLS + 1, :]
 
     local = slot[0, :, :] - first
     inside = (local >= 0) & (local < slots)
@@ -182,15 +196,15 @@
     for c in range(comps):
         for k in range(2):
             right, left = v[c, nx - 2 + k, :, :], v[c, k, :, :]
-            to_even[at : at + ny, :] = jnp.where(ev, right, left)
-            to_odd[at : at + ny, :] = jnp.where(ev, left, right)
+            x_even[at : at + ny, :] = jnp.where(ev, right, left)
+            x_odd[at : at + ny, :] = jnp.where(ev, left, right)
             at += ny
     for part in (code, load[0, :, :]):
         for k in range(0, points, LANES):
-            for out in (to_even, to_odd):
+            for out in (x_even, x_odd):
                 out[at : at + turbines, :] = part[:, k : k + LANES]
             at += turbines
-    for out in (to_even, to_odd):
+    for out in (x_even, x_odd):
         out[at : at + 8, :] = line[...]
 
 
@@ -252,7 +266,10 @@
         both = both[:, :levels] + both[:, levels:]
         loads[t] = both
         products[t] = (rows * both).astype(BF16)
-        edge_counts[t] = jnp.dot(select, counts[t], preferred_element_type=F32)
+    for t in range(0, turbines, 2):
+        pair = jnp.concatenate([counts[t], counts[t + 1]], axis=1)
+        both = jnp.dot(select, pair, preferred_element_type=F32)
+        edge_counts[t], edge_counts[t + 1] = both[:, :levels], both[:, levels:]
     block = 16
     wide = turbines * block
     gram = jnp.zeros((wide, wide), F32)
@@ -262,11 +279,17 @@
         gram = gram + lax.dot_general(left, right, NT, preferred_element_type=F32)
     keep = (iota((wide, wide), 0) & (block - 1)) == (iota((wide, wide), 1) & (block - 1))
     gram = jnp.sum(jnp.where(keep, gram, 0.0).reshape(turbines, block, wide), axis=1)
-    select = jnp.where(iota((wide, LANES), 0) // block == iota((wide, LANES), 1), 1.0, 0.0)
-    matrix[...] = jnp.dot(gram, select, precision=lax.Precision.HIGHEST, preferred_element_type=F32)
-
-
-def beside(v, tc, yo, ye, counts, matrix, couple, field, sums):
+    select = jnp.where(iota((wide, LANES), 0) // block == iota((wide, LANES), 1) % turbines, 1.0, 0.0).astype(BF16)
+    both = jnp.dot(jnp.concatenate(in_parts(gram, 2), axis=0).astype(BF16), select, preferred_element_type=F32)
+    both = both[:turbines] + both[turbines:]
+    rows, per_row, _, _ = packing(turbines)
+    row, lane = iota((turbines, LANES), 0), iota((turbines, LANES), 1)
+    for r in range(rows):
+        here = (row // per_row == r) & (lane // turbines == row % per_row)
+        matrix[r : r + 1, :] = jnp.sum(jnp.where(here, both, 0.0), axis=0, keepdims=True)
+
+
+def beside(v, tc, yo, ye, counts, part, field, sums):
     turbines, _, levels = counts.shape
     _, nx, ny, _ = v.shape
     cells = nx * ny
@@ -279,11 +302,11 @@
     later = jnp.dot(pick_slots(tc, cells), update, preferred_element_type=F32)
     for t in range(turbines):
         sums[t : t + 1, :] = jnp.sum(counts[t].astype(F32) * later, axis=0, keepdims=True)
-    column = jnp.sum(sums[...], axis=1, keepdims=True)
-    couple[...] = jnp.where(iota((turbines, LANES), 1) == turbines, column, matrix[...])
-
-
-def reduce_sums(comps, ny, yo, ye, xo, xe, edge_counts, line, couple, out, sums, corners):
+    row = as_row(jnp.sum(sums[...], axis=1, keepdims=True), LANES, 3 * turbines)
+    part[...] = jnp.broadcast_to(row, (8, LANES))
+
+
+def reduce_sums(comps, ny, yo, ye, xo, xe, edge_counts, line, matrix, part, out, sums, box):
     turbines = edge_counts.shape[0]
     ev_x = even("gx")
     left = (SPREAD + CARRY) * low_edge("gx", xo, xe, ny, 2 * ny)
@@ -291,23 +314,28 @@
     for t in range(turbines):
         sides = edge_counts[t, 0:ny, :] * left + edge_counts[t, ny : 2 * ny, :] * right
         sums[t : t + 1, :] = jnp.sum(sides, axis=0, keepdims=True)
-    corners[...] = jnp.zeros((2, 8, LANES), F32)
+    rows, _, corner, _ = packing(turbines)
+    box[...] = jnp.zeros(box.shape, F32)
     for c in range(comps):
         for i, (edge, at) in enumerate(((low_edge, (c * 2 + 1) * ny), (high_edge, c * 2 * ny))):
-            corners[0, 2 * c + i : 2 * c + i + 1, :] = edge("gx", xo, xe, at, at + 1)
-            corners[1, 2 * c + i : 2 * c + i + 1, :] = edge("gx", xo, xe, at + ny - 1, at + ny)
+            to = corner + 2 * c + i
+            box[0, to : to + 1, :] = edge("gx", xo, xe, at, at + 1)
+            box[1, to : to + 1, :] = edge("gx", xo, xe, at + ny - 1, at + ny)
     at = xe.shape[0] - 8 + SUMS
-    lane, row = iota((turbines, LANES), 1), iota((turbines, LANES), 0)
-    result = couple[...]
-    rows_of = (line[SUMS : SUMS + 1, :], picked(ev_x, xo, xe, at, at + 1), picked(ev_x, xe, xo, at, at + 1))
-    for k, sums_row in enumerate(rows_of):
-        result = result + jnp.where(row == k, sums_row, 0.0)
-    result = result + jnp.where(lane == turbines, jnp.sum(sums[...], axis=1, keepdims=True), 0.0)
+    before, after = picked(ev_x, xo, xe, at, at + 1), picked(ev_x, xe, xo, at, at + 1)
+    row = part[0:1, :] + line[SUMS : SUMS + 1, :]
+    row = row + as_row(jnp.sum(sums[...], axis=1, keepdims=True), LANES, 3 * turbines)
+    for k, other in ((1, before), (2, after)):
+        row = row + pltpu.roll(jnp.broadcast_to(other, (8, LANES)), k * turbines, 1)[0:1, :]
+    for side in range(2):
+        for k, piece in enumerate(in_parts(matrix[0:rows, :], 2)):
+            box[side, k * rows : (k + 1) * rows, :] = piece
+        for k, piece in enumerate(in_parts(row, 3)):
+            box[side, 2 * rows + k : 2 * rows + k + 1, :] = piece
     me = lax.axis_index("gy")
-    below, above = corners[0], corners[1]
+    below, above = box[0], box[1]
     for k in range(out.shape[0]):
-        out[k, 0:turbines, :] = result
-        out[k, turbines : turbines + 8, :] = jnp.where(me + 1 == k, above, below)
+        out[k] = jnp.where(me + 1 == k, above, below).astype(BF16)
 
 
 def edges(slots, pieces, v, slot, height, load, yo, ye, xo, xe, line, edge_x, edge_y, update_ref, strip_ref, scales, field):
@@ -362,19 +390,27 @@
     turbines, slots, _ = loads.shape
     cells = nx * ny
     ev_x, ev_y = even("gx"), even("gy")
-    total = got[0, 0:turbines, :]
+    rows, per_row, corner, _ = packing(turbines)
+    total = got[0].astype(F32)
     for k in range(1, got.shape[0]):
-        total = total + got[k, 0:turbines, :]
-    lane = iota((turbines, LANES), 1)
+        total = total + got[k].astype(F32)
+    matrix = total[0:rows, :] + total[rows : 2 * rows, :]
+    sums_row = total[2 * rows : 2 * rows + 1, :] + total[2 * rows + 1 : 2 * rows + 2, :]
+    sums_row = sums_row + total[2 * rows + 2 : 2 * rows + 3, :]
 
     def coefs(scale, sums):
         return -(scale * (FREE_WIND + sums / points))
 
-    own, left, right = (coefs(scales[k], as_column(total[k : k + 1, :], turbines, SIDE)) for k in range(3))
-    own_row = jnp.sum(jnp.where(iota((turbines, LANES), 0) == lane, own, 0.0), axis=0, keepdims=True)
-    forced = jnp.sum(jnp.where(lane < turbines, total * own_row, 0.0), axis=1, keepdims=True)
-    plain = jnp.sum(jnp.where(lane == turbines, total, 0.0), axis=1, keepdims=True)
-    later = coefs(scales[0], plain + forced)
+    own, left, right = (coefs(scales[k], as_column(sums_row, turbines, k * turbines)) for k in range(3))
+    row, lane = iota((turbines, LANES), 0), iota((turbines, LANES), 1)
+    own_row = jnp.sum(jnp.where(row == lane % turbines, own, 0.0), axis=0, keepdims=True)
+    products = matrix * own_row
+    forced = jnp.zeros((turbines, LANES), F32)
+    for r in range(rows):
+        here = (row // per_row == r) & (lane // turbines == row % per_row)
+        forced = forced + jnp.where(here, products[r : r + 1, :], 0.0)
+    forced = jnp.sum(forced, axis=1, keepdims=True)
+    later = coefs(scales[0], as_column(sums_row, turbines, 3 * turbines) + forced)
 
     for s in range(0, slots, 16):
         first = jnp.zeros((16, levels), F32)
@@ -410,23 +446,23 @@
     there_x = (ix > 0, ix < lax.axis_size("gx") - 1)
     there_y = (iy > 0, iy < last_y)
     beside_y = (jnp.maximum(iy - 1, 0), jnp.minimum(iy + 1, last_y))
-    corner_rows = [jnp.where(there_y[k], got[beside_y[k], turbines : turbines + 8, :], 0.0) for k in range(2)]
+    corner_rows = [jnp.where(there_y[k], got[beside_y[k]].astype(F32), 0.0) for k in range(2)]
     row_x, row_y = iota((nx, LANES), 0), iota((ny, LANES), 0)
     for c in range(comps):
-        corner = [[corner_rows[y][c * 2 + x : c * 2 + x + 1, :] for y in range(2)] for x in range(2)]
+        at_corner = [[corner_rows[y][corner + c * 2 + x : corner + c * 2 + x + 1, :] for y in range(2)] for x in range(2)]
         for k, (a, b) in enumerate(((xo, xe), (xe, xo))):
             at = (c * 2 + 1 - k) * ny
             x = k * (nx + 1)
             push = rounded(rounded(picked(ev_x, a, b, at, at + ny)) * sums[k])
-            extra = jnp.where(row_y == 0, corner[k][0], 0.0) + jnp.where(row_y == ny - 1, corner[k][1], 0.0)
+            extra = jnp.where(row_y == 0, at_corner[k][0], 0.0) + jnp.where(row_y == ny - 1, at_corner[k][1], 0.0)
             value = update_ref[c, x, :, :] + SPREAD * extra + push
             field[c, x, OWN : OWN + ny, :] = jnp.where(there_x[k], value, 0.0)
         for k, (a, b) in enumerate(((yo, ye), (ye, yo))):
             at = (c * 2 + 1 - k) * nx
             y = OWN - 1 + k * (ny + 1)
             push = rounded(rounded(picked(ev_y, a, b, at, at + nx)) * sums[2 + k])
-            extra = jnp.where(row_x == 0, (SPREAD + CARRY) * corner[0][k], 0.0)
-            extra = extra + jnp.where(row_x == nx - 1, SPREAD * corner[1][k], 0.0)
+            extra = jnp.where(row_x == 0, (SPREAD + CARRY) * at_corner[0][k], 0.0)
+            extra = extra + jnp.where(row_x == nx - 1, SPREAD * at_corner[1][k], 0.0)
             value = strip_ref[c, k] + extra + push
             field[c, 1 : 1 + nx, y, :] = jnp.where(there_y[k], value, 0.0)
     copies = []
@@ -445,6 +481,7 @@
     slots = tile_cells.shape[2]
     tiles_y = lax.axis_size("gy")
     pieces = points // LANES
+    chunk_rows = packing(turbines)[3]
     rows_y = comps * 2 * nx + 8
     rows_x = comps * 2 * ny + 2 * pieces * turbines + 8
     args = (velocity, tile_cells, owner, point_slot, point_z, loading)
@@ -453,42 +490,38 @@
     def field(n, planes):
         return pltpu.VMEM((n, planes, PLANE, levels), F32)
 
-    v, tc, own, slot, height, load, y_even, y_odd = call(
-        stage,
-        "stage",
-        [(x.shape, x.dtype) for x in args] + [((rows_y, levels), F32)] * 2,
+    v, tc, slot, height, load, counts, line, y_even, y_odd, x_even, x_odd = call(
+        prepare,
+        "prepare",
+        [(x.shape, x.dtype) for x in (velocity, tile_cells, point_slot, point_z, loading)]
+        + [((turbines, slots, levels), BF16), ((8, LANES), F32)]
+        + [((rows_y, levels), F32)] * 2
+        + [((rows_x, levels), F32)] * 2,
         args,
-        [pltpu.SemaphoreType.DMA((len(args),))],
+        [
+            pltpu.VMEM(owner.shape, jnp.int32),
+            pltpu.VMEM((turbines, slots, levels), F32),
+            pltpu.VMEM((turbines, levels), F32),
+            pltpu.SemaphoreType.DMA((len(args),)),
+        ],
         space=pltpu.HBM,
+        **work,
     )
     yo, ye = swap(y_odd, "gy", 1), swap(y_even, "gy", 0)
-    counts, line, x_even, x_odd = call(
-        histogram,
-        "histogram",
-        [
-            ((turbines, slots, levels), BF16),
-            ((8, LANES), F32),
-            ((rows_x, levels), F32),
-            ((rows_x, levels), F32),
-        ],
-        (v, tc, own, slot, height, load),
-        [pltpu.VMEM((turbines, levels), F32)],
-        **work,
-    )
     xo, xe = swap(x_odd, "gx", 1), swap(x_even, "gx", 0)
     loads, matrix, edge_counts = call(
         pair_up,
         "pair_up",
-        [((turbines, slots, levels), F32), ((turbines, LANES), F32), ((turbines, 2 * ny, levels), F32)],
+        [((turbines, slots, levels), F32), ((8, LANES), F32), ((turbines, 2 * ny, levels), F32)],
         (v, tc, slot, height, load, counts),
         [pltpu.VMEM((turbines, slots, levels), BF16)],
         **work,
     )
-    (couple,) = call(
+    (part,) = call(
         beside,
         "beside",
-        [((turbines, LANES), F32)],
-        (v, tc, yo, ye, counts, matrix),
+        [((8, LANES), F32)],
+        (v, tc, yo, ye, counts),
         [field(1, nx + 2), pltpu.VMEM((turbines, levels), F32)],
         flops=work["flops"] // 4,
         nbytes=work["nbytes"],
@@ -500,9 +533,9 @@
     (chunk,) = call(
         reduce_of,
         "reduce_sums",
-        [((tiles_y, turbines + 8, LANES), F32)],
-        (yo, ye, xo, xe, edge_counts, line, couple),
-        [pltpu.VMEM((turbines, levels), F32), pltpu.VMEM((2, 8, LANES), F32)],
+        [((tiles_y, chunk_rows, LANES), BF16)],
+        (yo, ye, xo, xe, edge_counts, line, matrix, part),
+        [pltpu.VMEM((turbines, levels), F32), pltpu.VMEM((2, chunk_rows, LANES), F32)],
     )
     got = lax.all_to_all(chunk, "gy", 0, 0)
 

time: 25.7 us -> 25.2 us (0.981)
  Pallas kernels: 9.12 us -> 8.85 us
    all_to_all x1, waiting for transfers between devices: 4.97 us -> 4.57 us  [body(): got = lax.all_to_all(chunk, 'gy', 0, 0)]
    pallas_call x7 -> x6, Pallas kernels: 9.12 us -> 8.85 us  [call(): pl.pallas_call(kernel, out_shape=[jax.ShapeDtypeStruct(s, d) for s, d in...]
  transfers between devices with their start and end apart: 5 -> 5, of which waited for: 2 -> 2; matrix products, arithmetic and copies ran while one was open for 0% -> 0% of each run, Pallas kernels for 23% -> 18%
where the time goes in v8:
time: 25.2 us; the launch traced here: 25 us
  starting transfers between devices  10.9 us (43%)
  Pallas kernels  8.85 us (35%)
  waiting for transfers between devices  5.25 us (21%)
    pallas_call x6, Pallas kernels, call(): pl.pallas_call(kernel, out_shape=[jax.ShapeDtypeStruct(s, d) for s, d in...  8.85 us
    ppermute x4, starting transfers between devices, swap(): return lax.ppermute(x, ('gx', 'gy'), pairs + [(b, a) for a, b in pairs])  6.16 us
    all_to_all x1, starting transfers between devices, body(): got = lax.all_to_all(chunk, 'gy', 0, 0)  4.71 us
    all_to_all x1, waiting for transfers between devices, body(): got = lax.all_to_all(chunk, 'gy', 0, 0)  4.57 us
    ppermute x4, waiting for transfers between devices, swap(): return lax.ppermute(x, ('gx', 'gy'), pairs + [(b, a) for a, b in pairs])  0.68 us
  transfers between devices with their start and end apart: 5, of which 2 were waited for; matrix products, arithmetic and copies ran while one was open for 0% of the time, Pallas kernels for 18%

profile of v8, /device:TPU:0, one launch (start us, length us, event | category | flops | bytes accessed | tf_op | source)
XLA Modules:
  0.0 25.0 jit_solution(14047532950004924513)
XLA Ops:
  0.0 2.1 %prepare.1 = (f32[3,16,16,128]{3,2,1,0:T(8,128)S(1)}, s32[1,1,96]{2,1,0:T(1,128)S(1)}, s32[1,16,384]{2,1,0:T(8,128)S(1)}, s32[1,16,384]{2,1,0:T(8,128)S(1)}, f32...) custom-call(f32[3,16,16,128]{3,2,1,0:T(8,128)} %v_hbm.1, ...), custom_call_target="tpu_custom_call" | custom-call | flops 1962934272 | bytes 1048576 | tf_op jit(solution)/shard_map/prepare/pallas_call | solution.py:68
  2.1 0.5 %collective-permute-start = (f32[104,128]{1,0:T(8,128)S(1)}, f32[104,128]{1,0:T(8,128)S(1)}, u32[]{:S(2)}, u32[]{:S(2)}) collective-permute-start(f32[104,128]{1,0:T(8,128)S(1)} %get-tuple-element.24), channel_id=1, source_target_pairs={{1,2},{9,10},{17,18},{25,26},{3,4},{11,12},{19,20},{27,28},{5,6},{... | collective-permute-start | bytes 159752 | tf_op jit(solution)/shard_map/ppermute | solution.py:64
  2.6 4.0 %collective-permute-start.1 = (f32[104,128]{1,0:T(8,128)S(1)}, f32[104,128]{1,0:T(8,128)S(1)}, u32[]{:S(2)}, u32[]{:S(2)}) collective-permute-start(f32[104,128]{1,0:T(8,128)S(1)} %get-tuple-element.25), channel_id=1, source_target_pairs={{0,1},{8,9},{16,17},{24,25},{2,3},{10,11},{18,19},{26,27},{4,5},{1... | collective-permute-start | bytes 159752 | tf_op jit(solution)/shard_map/ppermute | solution.py:64
  6.7 0.0 collective-permute-start.2
  6.7 1.6 %collective-permute-start.3 = (f32[200,128]{1,0:T(8,128)S(1)}, f32[200,128]{1,0:T(8,128)S(1)}, u32[]{:S(2)}, u32[]{:S(2)}) collective-permute-start(f32[200,128]{1,0:T(8,128)S(1)} %get-tuple-element.27), channel_id=1, source_target_pairs={{0,8},{1,9},{2,10},{3,11},{4,12},{5,13},{6,14},{7,15},{16,24},{17,... | collective-permute-start | bytes 307208 | tf_op jit(solution)/shard_map/ppermute | solution.py:64
  8.3 1.9 %pair_up.1 = (f32[16,96,128]{2,1,0:T(8,128)S(1)}, f32[8,128]{1,0:T(8,128)S(1)}, f32[16,32,128]{2,1,0:T(8,128)S(1)}) custom-call(f32[3,16,16,128]{3,2,1,0:T(8,128)S(1)} %get-tuple-element.28.v.refs_0_.refs_1_, s32[1,1,96]{2,1,0:T(1,128)S(1)} %get-tuple-element.29.tc.refs_2_, s32[1,16,384]{2,1,0:T(8,128)S(1)} %get-tuple-element.30.slot.refs_1_, ...), custom_call_target="tpu_custom_call" | custom-call | flops 1962934272 | bytes 1048576 | tf_op jit(solution)/shard_map/pair_up/pallas_call | solution.py:68
  10.2 0.0 collective-permute-done.yo.refs_0_.refs_4_.refs_3_
  10.2 0.0 collective-permute-done.1.ye.refs_1_.refs_5_.refs_4_
  10.2 0.5 %beside.1.refs_7_ = f32[8,128]{1,0:T(8,128)S(1)} custom-call(f32[3,16,16,128]{3,2,1,0:T(8,128)S(1)} %get-tuple-element.28.v.refs_0_.refs_1_, s32[1,1,96]{2,1,0:T(1,128)S(1)} %get-tuple-element.29.tc.refs_2_, f32[104,128]{1,0:T(8,128)S(1)} %collective-permute-done.yo.refs_0_.refs_4_.refs_3_, f32[104,128]{1,0:T(8,128)S(1)} %collective-permute-done.1.ye.refs_1_.refs_5_.refs_4_, ...), custom_call_target="tpu_custom_call" | custom-call | flops 490733568 | bytes 1048576 | tf_op jit(solution)/shard_map/beside/pallas_call | solution.py:68
  10.7 0.7 %collective-permute-done.2.refs_2_.refs_6_.refs_5_ = f32[200,128]{1,0:T(8,128)S(1)} collective-permute-done((f32[200,128]{1,0:T(8,128)S(1)}, f32[200,128]{1,0:T(8,128)S(1)}, u32[]{:S(2)}, u32[]{:S(2)}) %collective-permute-start.2) | collective-permute-done | bytes 102432 | tf_op jit(solution)/shard_map/ppermute | solution.py:64
  11.3 0.0 collective-permute-done.3.refs_3_.refs_7_.refs_6_
  11.3 0.8 %reduce_sums.1 = bf16[8,16,128]{2,1,0:T(8,128)(2,1)} custom-call(f32[104,128]{1,0:T(8,128)S(1)} %collective-permute-done.yo.refs_0_.refs_4_.refs_3_, f32[104,128]{1,0:T(8,128)S(1)} %collective-permute-done.1.ye.refs_1_.refs_5_.refs_4_, f32[200,128]{1,0:T(8,128)S(1)} %collective-permute-done.2.refs_2_.refs_6_.refs_5_, ...), custom_call_target="tpu_custom_call" | custom-call | tf_op jit(solution)/shard_map/reduce_sums/pallas_call | solution.py:68
  12.1 4.7 %all-to-all-start = ((bf16[8,16,128]{2,1,0:T(8,128)(2,1)}), bf16[8,16,128]{2,1,0:T(8,128)(2,1)S(1)}, u32[]{:S(2)}, u32[]{:S(2)}) async-start(bf16[8,16,128]{2,1,0:T(8,128)(2,1)} %reduce_sums.1), calls=%async_computation | async-start | bytes 65536 | tf_op jit(solution)/shard_map/all_to_all | solution.py:540
  16.8 2.1 %edges.1 = (f32[2,16,16,128]{3,2,1,0:T(8,128)S(1)}, f32[2,16,16,128]{3,2,1,0:T(8,128)S(1)}, f32[3,18,16,128]{3,2,1,0:T(8,128)S(1)}, f32[3,2,16,128]{3,2,1,0:T(8,128)S(1)}, f32[3,16,128]{2,1,0:T(8,128)S(1)}) custom-call(f32[3,16,16,128]{3,2,1,0:T(8,128)S(1)} %get-tuple-element.28.v.refs_0_.refs_1_, s32[1,16,384]{2,1,0:T(8,128)S(1)} %get-tuple-element.30.slot.refs_1_, ...), custom_call_target="tpu_custom_call" | custom-call | flops 1962934272 | bytes 1048576 | tf_op jit(solution)/shard_map/edges/pallas_call | solution.py:68
  18.9 4.6 %all-to-all-done.refs_0_ = bf16[8,16,128]{2,1,0:T(8,128)(2,1)S(1)} async-done(((bf16[8,16,128]{2,1,0:T(8,128)(2,1)}), bf16[8,16,128]{2,1,0:T(8,128)(2,1)S(1)}, u32[]{:S(2)}, u32[]{:S(2)}) %all-to-all-start) | async-done | bytes 32800 | tf_op jit(solution)/shard_map/all_to_all | solution.py:540
  23.5 1.5 %advance.1 = f32[3,16,16,128]{3,2,1,0:T(8,128)} custom-call(bf16[8,16,128]{2,1,0:T(8,128)(2,1)S(1)} %all-to-all-done.refs_0_, f32[3,16,16,128]{3,2,1,0:T(8,128)S(1)} %get-tuple-element.28.v.refs_0_.refs_1_, s32[1,1,96]{2,1,0:T(1,128)S(1)} %get-tuple-element.29.tc.refs_2_, f32[104,128]{1,0:T(8,128)S(1)} %collective-permute-done.yo.refs_0_.refs_4_.refs_3_, ...), custom_call_target="tpu_custom_call" | custom-call | tf_op jit(solution)/shard_map/advance/pallas_call | solution.py:68
Async XLA Ops:
  2.1 8.1 %collective-permute-start = (f32[104,128]{1,0:T(8,128)S(1)}, f32[104,128]{1,0:T(8,128)S(1)}, u32[]{:S(2)}, u32[]{:S(2)}) collective-permute-start(f32[104,128]{1,0:T(8,128)S(1)} %get-tuple-element.24), channel_id=1, source_target_pairs={{1,2},{9,10},{17,18},{25,26},{3,4},{11,12},{19,20},{27,28},{5,6},{... | collective-permute-start | bytes 159752 | tf_op jit(solution)/shard_map/ppermute | solution.py:64
  2.6 7.6 %collective-permute-start.1 = (f32[104,128]{1,0:T(8,128)S(1)}, f32[104,128]{1,0:T(8,128)S(1)}, u32[]{:S(2)}, u32[]{:S(2)}) collective-permute-start(f32[104,128]{1,0:T(8,128)S(1)} %get-tuple-element.25), channel_id=1, source_target_pairs={{0,1},{8,9},{16,17},{24,25},{2,3},{10,11},{18,19},{26,27},{4,5},{1... | collective-permute-start | bytes 159752 | tf_op jit(solution)/shard_map/ppermute | solution.py:64
  6.7 4.7 %collective-permute-start.2 = (f32[200,128]{1,0:T(8,128)S(1)}, f32[200,128]{1,0:T(8,128)S(1)}, u32[]{:S(2)}, u32[]{:S(2)}) collective-permute-start(f32[200,128]{1,0:T(8,128)S(1)} %get-tuple-element.26), channel_id=1, source_target_pairs={{8,16},{9,17},{10,18},{11,19},{12,20},{13,21},{14,22},{15,23},{0,1... | collective-permute-start | bytes 307208 | tf_op jit(solution)/shard_map/ppermute | solution.py:64
  6.7 4.6 %collective-permute-start.3 = (f32[200,128]{1,0:T(8,128)S(1)}, f32[200,128]{1,0:T(8,128)S(1)}, u32[]{:S(2)}, u32[]{:S(2)}) collective-permute-start(f32[200,128]{1,0:T(8,128)S(1)} %get-tuple-element.27), channel_id=1, source_target_pairs={{0,8},{1,9},{2,10},{3,11},{4,12},{5,13},{6,14},{7,15},{16,24},{17,... | collective-permute-start | bytes 307208 | tf_op jit(solution)/shard_map/ppermute | solution.py:64
  12.1 11.4 %all-to-all-start = ((bf16[8,16,128]{2,1,0:T(8,128)(2,1)}), bf16[8,16,128]{2,1,0:T(8,128)(2,1)S(1)}, u32[]{:S(2)}, u32[]{:S(2)}) async-start(bf16[8,16,128]{2,1,0:T(8,128)(2,1)} %reduce_sums.1), calls=%async_computation | async-start | bytes 65536 | tf_op jit(solution)/shard_map/all_to_all | solution.py:540

commit v9 on v8

--- a/solution.py
+++ b/solution.py
@@ -244,7 +244,7 @@
     return [both[2 * k * n : (2 * k + 1) * n] + both[(2 * k + 1) * n : (2 * k + 2) * n] for k in range(len(places))]
 
 
-def pair_up(v, tc, slot, height, load, counts, loads, matrix, edge_counts, products):
+def pair_up(v, tc, slot, height, load, counts, loads, matrix, edge_counts, single, products):
     turbines, slots, levels = counts.shape
     _, nx, ny, _ = v.shape
     cells = nx * ny
@@ -265,18 +265,24 @@
         both = lax.dot_general(a, b, NT, preferred_element_type=F32)
         both = both[:, :levels] + both[:, levels:]
         loads[t] = both
-        products[t] = (rows * both).astype(BF16)
+        for k, piece in enumerate(in_parts(rows * both, 2)):
+            products[k, t] = piece.astype(BF16)
     for t in range(0, turbines, 2):
         pair = jnp.concatenate([counts[t], counts[t + 1]], axis=1)
         both = jnp.dot(select, pair, preferred_element_type=F32)
         edge_counts[t], edge_counts[t + 1] = both[:, :levels], both[:, levels:]
+    hits = counts[0].astype(F32)
+    for t in range(1, turbines):
+        hits = hits + counts[t].astype(F32)
+    single[...] = jnp.where(hits == 1.0, 1.0, 0.0).astype(BF16)
     block = 16
     wide = turbines * block
     gram = jnp.zeros((wide, wide), F32)
     for b in range(0, slots, block):
         left = counts[:, b : b + block, :].reshape(wide, levels)
-        right = products[:, b : b + block, :].reshape(wide, levels)
-        gram = gram + lax.dot_general(left, right, NT, preferred_element_type=F32)
+        for k in range(2):
+            right = products[k, :, b : b + block, :].reshape(wide, levels)
+            gram = gram + lax.dot_general(left, right, NT, preferred_element_type=F32)
     keep = (iota((wide, wide), 0) & (block - 1)) == (iota((wide, wide), 1) & (block - 1))
     gram = jnp.sum(jnp.where(keep, gram, 0.0).reshape(turbines, block, wide), axis=1)
     select = jnp.where(iota((wide, LANES), 0) // block == iota((wide, LANES), 1) % turbines, 1.0, 0.0).astype(BF16)
@@ -298,8 +304,10 @@
     field[0, 1 : 1 + nx, OWN + ny, :] = high_edge("gy", yo, ye, 0, nx)
     for x in (0, nx + 1):
         field[0, x, OWN : OWN + ny, :] = jnp.zeros((ny, levels), F32)
-    update = stencil(field, 0, 1, nx, ny).reshape(cells, levels).astype(BF16)
+    update = stencil(field, 0, 1, nx, ny).reshape(cells, levels)
+    update = jnp.concatenate(in_parts(update, 2), axis=1).astype(BF16)
     later = jnp.dot(pick_slots(tc, cells), update, preferred_element_type=F32)
+    later = later[:, :levels] + later[:, levels:]
     for t in range(turbines):
         sums[t : t + 1, :] = jnp.sum(counts[t].astype(F32) * later, axis=0, keepdims=True)
     row = as_row(jnp.sum(sums[...], axis=1, keepdims=True), LANES, 3 * turbines)
@@ -385,7 +393,7 @@
         edge_y[0, t], edge_y[1, t] = spread(places, height[0, t : t + 1, :], load[0, t : t + 1, :])
 
 
-def advance(points, got, v, tc, yo, ye, xo, xe, scales, loads, edge_x, edge_y, update_ref, strip_ref, out, field, parts, result, sems):
+def advance(points, got, v, tc, yo, ye, xo, xe, scales, loads, single, edge_x, edge_y, update_ref, strip_ref, out, field, parts, result, sems):
     comps, nx, ny, levels = v.shape
     turbines, slots, _ = loads.shape
     cells = nx * ny
@@ -425,15 +433,21 @@
                 rest = rest - piece.astype(F32)
                 at = (2 * i + k) * levels
                 parts[s : s + 16, at : at + levels] = piece
+    parts[:, 4 * levels :] = single[...]
     row = tc[0, :, :]
     put = jnp.where(iota((cells, slots), 0) == row, 1.0, 0.0).astype(BF16)
     spread_out = jnp.dot(put, parts[...], preferred_element_type=F32)
-    pieces = [spread_out[:, k * levels : (k + 1) * levels] for k in range(4)]
+    pieces = [spread_out[:, k * levels : (k + 1) * levels] for k in range(5)]
     first = (pieces[0] + pieces[1]).reshape(nx, ny, levels)
     second = (pieces[2] + pieces[3]).reshape(nx, ny, levels)
+    alone = pieces[4].reshape(nx, ny, levels) > 0.5
+
+    def force(values, weight):
+        push = rounded(values) * weight
+        return jnp.where(alone, rounded(push), push)
+
     for c in range(comps):
-        push = rounded(rounded(v[c, :, :, :]) * first)
-        field[c, 1 : 1 + nx, OWN : OWN + ny, :] = update_ref[c, 1 : 1 + nx, :, :] + push
+        field[c, 1 : 1 + nx, OWN : OWN + ny, :] = update_ref[c, 1 : 1 + nx, :, :] + force(v[c, :, :, :], first)
 
     sums = []
     for edge, coef in ((edge_x.at[0], left), (edge_x.at[1], right), (edge_y.at[0], own), (edge_y.at[1], own)):
@@ -468,7 +482,7 @@
     copies = []
     for c in range(comps):
         now = field[c, 1 : 1 + nx, OWN : OWN + ny, :]
-        result[c] = stencil(field, c, 1, nx, ny) + rounded(rounded(now) * second)
+        result[c] = stencil(field, c, 1, nx, ny) + force(now, second)
         copies.append(pltpu.make_async_copy(result.at[c], out.at[c], sems.at[c]))
         copies[c].start()
     for copy in copies:
@@ -509,12 +523,17 @@
     )
     yo, ye = swap(y_odd, "gy", 1), swap(y_even, "gy", 0)
     xo, xe = swap(x_odd, "gx", 1), swap(x_even, "gx", 0)
-    loads, matrix, edge_counts = call(
+    loads, matrix, edge_counts, single = call(
         pair_up,
         "pair_up",
-        [((turbines, slots, levels), F32), ((8, LANES), F32), ((turbines, 2 * ny, levels), F32)],
+        [
+            ((turbines, slots, levels), F32),
+            ((8, LANES), F32),
+            ((turbines, 2 * ny, levels), F32),
+            ((slots, levels), BF16),
+        ],
         (v, tc, slot, height, load, counts),
-        [pltpu.VMEM((turbines, slots, levels), BF16)],
+        [pltpu.VMEM((2, turbines, slots, levels), BF16)],
         **work,
     )
     (part,) = call(
@@ -564,10 +583,10 @@
         advance_by,
         "advance",
         [(velocity.shape, F32)],
-        (got, v, tc, yo, ye, xo, xe, scales, loads, edge_x, edge_y, update, strip),
+        (got, v, tc, yo, ye, xo, xe, scales, loads, single, edge_x, edge_y, update, strip),
         [
             field(comps, nx + 2),
-            pltpu.VMEM((slots, 4 * levels), BF16),
+            pltpu.VMEM((slots, 5 * levels), BF16),
             pltpu.VMEM(velocity.shape, F32),
             pltpu.SemaphoreType.DMA((comps,)),
         ],

time: 25.2 us -> 25.3 us (level)
  Pallas kernels: 8.85 us -> 9.51 us
  waiting for transfers between devices: 5.25 us -> 4.63 us
    pallas_call x6, Pallas kernels: 8.85 us -> 9.51 us  [call(): pl.pallas_call(kernel, out_shape=[jax.ShapeDtypeStruct(s, d) for s, d in...]
    ppermute x4, waiting for transfers between devices: 0.68 us -> 0.06 us  [swap(): return lax.ppermute(x, ('gx', 'gy'), pairs + [(b, a) for a, b in pairs])]
  transfers between devices with their start and end apart: 5 -> 5, of which waited for: 2 -> 1; matrix products, arithmetic and copies ran while one was open for 0% -> 0% of each run, Pallas kernels for 18% -> 20%
where the time goes in v9:
time: 25.3 us; the launch traced here: 25 us
  starting transfers between devices  10.9 us (43%)
  Pallas kernels  9.51 us (38%)
  waiting for transfers between devices  4.63 us (18%)
    pallas_call x6, Pallas kernels, call(): pl.pallas_call(kernel, out_shape=[jax.ShapeDtypeStruct(s, d) for s, d in...  9.51 us
    ppermute x4, starting transfers between devices, swap(): return lax.ppermute(x, ('gx', 'gy'), pairs + [(b, a) for a, b in pairs])  6.16 us
    all_to_all x1, starting transfers between devices, body(): got = lax.all_to_all(chunk, 'gy', 0, 0)  4.71 us
    all_to_all x1, waiting for transfers between devices, body(): got = lax.all_to_all(chunk, 'gy', 0, 0)  4.58 us
  transfers between devices with their start and end apart: 5, of which 1 were waited for; matrix products, arithmetic and copies ran while one was open for 0% of the time, Pallas kernels for 20%

profile of v9, /device:TPU:0, one launch (start us, length us, event | category | flops | bytes accessed | tf_op | source)
XLA Modules:
  0.0 25.0 jit_solution(11053039481201072946)
XLA Ops:
  0.0 2.1 %prepare.1 = (f32[3,16,16,128]{3,2,1,0:T(8,128)S(1)}, s32[1,1,96]{2,1,0:T(1,128)S(1)}, s32[1,16,384]{2,1,0:T(8,128)S(1)}, s32[1,16,384]{2,1,0:T(8,128)S(1)}, f32...) custom-call(f32[3,16,16,128]{3,2,1,0:T(8,128)} %v_hbm.1, ...), custom_call_target="tpu_custom_call" | custom-call | flops 1962934272 | bytes 1048576 | tf_op jit(solution)/shard_map/prepare/pallas_call | solution.py:68
  2.1 0.5 %collective-permute-start = (f32[104,128]{1,0:T(8,128)S(1)}, f32[104,128]{1,0:T(8,128)S(1)}, u32[]{:S(2)}, u32[]{:S(2)}) collective-permute-start(f32[104,128]{1,0:T(8,128)S(1)} %get-tuple-element.25), channel_id=1, source_target_pairs={{1,2},{9,10},{17,18},{25,26},{3,4},{11,12},{19,20},{27,28},{5,6},{... | collective-permute-start | bytes 159752 | tf_op jit(solution)/shard_map/ppermute | solution.py:64
  2.7 4.0 %collective-permute-start.1 = (f32[104,128]{1,0:T(8,128)S(1)}, f32[104,128]{1,0:T(8,128)S(1)}, u32[]{:S(2)}, u32[]{:S(2)}) collective-permute-start(f32[104,128]{1,0:T(8,128)S(1)} %get-tuple-element.26), channel_id=1, source_target_pairs={{0,1},{8,9},{16,17},{24,25},{2,3},{10,11},{18,19},{26,27},{4,5},{1... | collective-permute-start | bytes 159752 | tf_op jit(solution)/shard_map/ppermute | solution.py:64
  6.7 0.0 collective-permute-start.2
  6.7 1.6 %collective-permute-start.3 = (f32[200,128]{1,0:T(8,128)S(1)}, f32[200,128]{1,0:T(8,128)S(1)}, u32[]{:S(2)}, u32[]{:S(2)}) collective-permute-start(f32[200,128]{1,0:T(8,128)S(1)} %get-tuple-element.28), channel_id=1, source_target_pairs={{0,8},{1,9},{2,10},{3,11},{4,12},{5,13},{6,14},{7,15},{16,24},{17,... | collective-permute-start | bytes 307208 | tf_op jit(solution)/shard_map/ppermute | solution.py:64
  8.3 2.5 %pair_up.1 = (f32[16,96,128]{2,1,0:T(8,128)S(1)}, f32[8,128]{1,0:T(8,128)S(1)}, f32[16,32,128]{2,1,0:T(8,128)S(1)}, bf16[96,128]{1,0:T(8,128)(2,1)S(1)}) custom-call(f32[3,16,16,128]{3,2,1,0:T(8,128)S(1)} %get-tuple-element.29.v.refs_0_.refs_1_, s32[1,1,96]{2,1,0:T(1,128)S(1)} %get-tuple-element.30.tc.refs_2_, ...), custom_call_target="tpu_custom_call" | custom-call | flops 1962934272 | bytes 1048576 | tf_op jit(solution)/shard_map/pair_up/pallas_call | solution.py:68
  10.8 0.0 collective-permute-done.yo.refs_0_.refs_4_.refs_3_
  10.8 0.0 collective-permute-done.1.ye.refs_1_.refs_5_.refs_4_
  10.8 0.5 %beside.1.refs_7_ = f32[8,128]{1,0:T(8,128)S(1)} custom-call(f32[3,16,16,128]{3,2,1,0:T(8,128)S(1)} %get-tuple-element.29.v.refs_0_.refs_1_, s32[1,1,96]{2,1,0:T(1,128)S(1)} %get-tuple-element.30.tc.refs_2_, f32[104,128]{1,0:T(8,128)S(1)} %collective-permute-done.yo.refs_0_.refs_4_.refs_3_, f32[104,128]{1,0:T(8,128)S(1)} %collective-permute-done.1.ye.refs_1_.refs_5_.refs_4_, ...), custom_call_target="tpu_custom_call" | custom-call | flops 490733568 | bytes 1048576 | tf_op jit(solution)/shard_map/beside/pallas_call | solution.py:68
  11.3 0.0 collective-permute-done.2.refs_2_.refs_6_.refs_5_
  11.3 0.0 collective-permute-done.3.refs_3_.refs_7_.refs_6_
  11.3 0.8 %reduce_sums.1 = bf16[8,16,128]{2,1,0:T(8,128)(2,1)} custom-call(f32[104,128]{1,0:T(8,128)S(1)} %collective-permute-done.yo.refs_0_.refs_4_.refs_3_, f32[104,128]{1,0:T(8,128)S(1)} %collective-permute-done.1.ye.refs_1_.refs_5_.refs_4_, f32[200,128]{1,0:T(8,128)S(1)} %collective-permute-done.2.refs_2_.refs_6_.refs_5_, ...), custom_call_target="tpu_custom_call" | custom-call | tf_op jit(solution)/shard_map/reduce_sums/pallas_call | solution.py:68
  12.1 4.7 %all-to-all-start = ((bf16[8,16,128]{2,1,0:T(8,128)(2,1)}), bf16[8,16,128]{2,1,0:T(8,128)(2,1)S(1)}, u32[]{:S(2)}, u32[]{:S(2)}) async-start(bf16[8,16,128]{2,1,0:T(8,128)(2,1)} %reduce_sums.1), calls=%async_computation | async-start | bytes 65536 | tf_op jit(solution)/shard_map/all_to_all | solution.py:559
  16.8 2.1 %edges.1 = (f32[2,16,16,128]{3,2,1,0:T(8,128)S(1)}, f32[2,16,16,128]{3,2,1,0:T(8,128)S(1)}, f32[3,18,16,128]{3,2,1,0:T(8,128)S(1)}, f32[3,2,16,128]{3,2,1,0:T(8,128)S(1)}, f32[3,16,128]{2,1,0:T(8,128)S(1)}) custom-call(f32[3,16,16,128]{3,2,1,0:T(8,128)S(1)} %get-tuple-element.29.v.refs_0_.refs_1_, s32[1,16,384]{2,1,0:T(8,128)S(1)} %get-tuple-element.31.slot.refs_1_, ...), custom_call_target="tpu_custom_call" | custom-call | flops 1962934272 | bytes 1048576 | tf_op jit(solution)/shard_map/edges/pallas_call | solution.py:68
  18.9 4.6 %all-to-all-done.refs_0_ = bf16[8,16,128]{2,1,0:T(8,128)(2,1)S(1)} async-done(((bf16[8,16,128]{2,1,0:T(8,128)(2,1)}), bf16[8,16,128]{2,1,0:T(8,128)(2,1)S(1)}, u32[]{:S(2)}, u32[]{:S(2)}) %all-to-all-start) | async-done | bytes 32800 | tf_op jit(solution)/shard_map/all_to_all | solution.py:559
  23.5 1.5 %advance.1 = f32[3,16,16,128]{3,2,1,0:T(8,128)} custom-call(bf16[8,16,128]{2,1,0:T(8,128)(2,1)S(1)} %all-to-all-done.refs_0_, f32[3,16,16,128]{3,2,1,0:T(8,128)S(1)} %get-tuple-element.29.v.refs_0_.refs_1_, s32[1,1,96]{2,1,0:T(1,128)S(1)} %get-tuple-element.30.tc.refs_2_, f32[104,128]{1,0:T(8,128)S(1)} %collective-permute-done.yo.refs_0_.refs_4_.refs_3_, ...), custom_call_target="tpu_custom_call" | custom-call | tf_op jit(solution)/shard_map/advance/pallas_call | solution.py:68
Async XLA Ops:
  2.1 8.7 %collective-permute-start = (f32[104,128]{1,0:T(8,128)S(1)}, f32[104,128]{1,0:T(8,128)S(1)}, u32[]{:S(2)}, u32[]{:S(2)}) collective-permute-start(f32[104,128]{1,0:T(8,128)S(1)} %get-tuple-element.25), channel_id=1, source_target_pairs={{1,2},{9,10},{17,18},{25,26},{3,4},{11,12},{19,20},{27,28},{5,6},{... | collective-permute-start | bytes 159752 | tf_op jit(solution)/shard_map/ppermute | solution.py:64
  2.7 8.2 %collective-permute-start.1 = (f32[104,128]{1,0:T(8,128)S(1)}, f32[104,128]{1,0:T(8,128)S(1)}, u32[]{:S(2)}, u32[]{:S(2)}) collective-permute-start(f32[104,128]{1,0:T(8,128)S(1)} %get-tuple-element.26), channel_id=1, source_target_pairs={{0,1},{8,9},{16,17},{24,25},{2,3},{10,11},{18,19},{26,27},{4,5},{1... | collective-permute-start | bytes 159752 | tf_op jit(solution)/shard_map/ppermute | solution.py:64
  6.7 4.7 %collective-permute-start.2 = (f32[200,128]{1,0:T(8,128)S(1)}, f32[200,128]{1,0:T(8,128)S(1)}, u32[]{:S(2)}, u32[]{:S(2)}) collective-permute-start(f32[200,128]{1,0:T(8,128)S(1)} %get-tuple-element.27), channel_id=1, source_target_pairs={{8,16},{9,17},{10,18},{11,19},{12,20},{13,21},{14,22},{15,23},{0,1... | collective-permute-start | bytes 307208 | tf_op jit(solution)/shard_map/ppermute | solution.py:64
  6.7 4.6 %collective-permute-start.3 = (f32[200,128]{1,0:T(8,128)S(1)}, f32[200,128]{1,0:T(8,128)S(1)}, u32[]{:S(2)}, u32[]{:S(2)}) collective-permute-start(f32[200,128]{1,0:T(8,128)S(1)} %get-tuple-element.28), channel_id=1, source_target_pairs={{0,8},{1,9},{2,10},{3,11},{4,12},{5,13},{6,14},{7,15},{16,24},{17,... | collective-permute-start | bytes 307208 | tf_op jit(solution)/shard_map/ppermute | solution.py:64
  12.1 11.4 %all-to-all-start = ((bf16[8,16,128]{2,1,0:T(8,128)(2,1)}), bf16[8,16,128]{2,1,0:T(8,128)(2,1)S(1)}, u32[]{:S(2)}, u32[]{:S(2)}) async-start(bf16[8,16,128]{2,1,0:T(8,128)(2,1)} %reduce_sums.1), calls=%async_computation | async-start | bytes 65536 | tf_op jit(solution)/shard_map/all_to_all | solution.py:559

commit v10 on v9

--- a/solution.py
+++ b/solution.py
@@ -480,11 +480,16 @@
             value = strip_ref[c, k] + extra + push
             field[c, 1 : 1 + nx, y, :] = jnp.where(there_y[k], value, 0.0)
     copies = []
+    half = nx // 2
     for c in range(comps):
-        now = field[c, 1 : 1 + nx, OWN : OWN + ny, :]
-        result[c] = stencil(field, c, 1, nx, ny) + force(now, second)
-        copies.append(pltpu.make_async_copy(result.at[c], out.at[c], sems.at[c]))
-        copies[c].start()
+        for x in (0, half):
+            now = field[c, 1 + x : 1 + x + half, OWN : OWN + ny, :]
+            push = rounded(now) * second[x : x + half]
+            push = jnp.where(alone[x : x + half], rounded(push), push)
+            result[c, x : x + half] = stencil(field, c, 1 + x, half, ny) + push
+            part = (c, pl.ds(x, half))
+            copies.append(pltpu.make_async_copy(result.at[part], out.at[part], sems.at[len(copies)]))
+            copies[-1].start()
     for copy in copies:
         copy.wait()
 
@@ -588,7 +593,7 @@
             field(comps, nx + 2),
             pltpu.VMEM((slots, 5 * levels), BF16),
             pltpu.VMEM(velocity.shape, F32),
-            pltpu.SemaphoreType.DMA((comps,)),
+            pltpu.SemaphoreType.DMA((2 * comps,)),
         ],
         out_space=pltpu.HBM,
     )

time: 25.3 us -> 25.3 us (level)
  no operation moved by 1% of the time
where the time goes in v10:
time: 25.3 us; the launch traced here: 25 us
  starting transfers between devices  10.9 us (43%)
  Pallas kernels  9.51 us (38%)
  waiting for transfers between devices  4.63 us (18%)
    pallas_call x6, Pallas kernels, call(): pl.pallas_call(kernel, out_shape=[jax.ShapeDtypeStruct(s, d) for s, d in...  9.51 us
    ppermute x4, starting transfers between devices, swap(): return lax.ppermute(x, ('gx', 'gy'), pairs + [(b, a) for a, b in pairs])  6.16 us
    all_to_all x1, starting transfers between devices, body(): got = lax.all_to_all(chunk, 'gy', 0, 0)  4.71 us
    all_to_all x1, waiting for transfers between devices, body(): got = lax.all_to_all(chunk, 'gy', 0, 0)  4.58 us
  transfers between devices with their start and end apart: 5, of which 1 were waited for; matrix products, arithmetic and copies ran while one was open for 0% of the time, Pallas kernels for 20%

profile of v10, /device:TPU:0, one launch (start us, length us, event | category | flops | bytes accessed | tf_op | source)
XLA Modules:
  0.0 25.0 jit_solution(14172229595920687821)
XLA Ops:
  0.0 2.1 %prepare.1 = (f32[3,16,16,128]{3,2,1,0:T(8,128)S(1)}, s32[1,1,96]{2,1,0:T(1,128)S(1)}, s32[1,16,384]{2,1,0:T(8,128)S(1)}, s32[1,16,384]{2,1,0:T(8,128)S(1)}, f32...) custom-call(f32[3,16,16,128]{3,2,1,0:T(8,128)} %v_hbm.1, ...), custom_call_target="tpu_custom_call" | custom-call | flops 1962934272 | bytes 1048576 | tf_op jit(solution)/shard_map/prepare/pallas_call | solution.py:68
  2.1 0.5 %collective-permute-start = (f32[104,128]{1,0:T(8,128)S(1)}, f32[104,128]{1,0:T(8,128)S(1)}, u32[]{:S(2)}, u32[]{:S(2)}) collective-permute-start(f32[104,128]{1,0:T(8,128)S(1)} %get-tuple-element.25), channel_id=1, source_target_pairs={{1,2},{9,10},{17,18},{25,26},{3,4},{11,12},{19,20},{27,28},{5,6},{... | collective-permute-start | bytes 159752 | tf_op jit(solution)/shard_map/ppermute | solution.py:64
  2.7 4.0 %collective-permute-start.1 = (f32[104,128]{1,0:T(8,128)S(1)}, f32[104,128]{1,0:T(8,128)S(1)}, u32[]{:S(2)}, u32[]{:S(2)}) collective-permute-start(f32[104,128]{1,0:T(8,128)S(1)} %get-tuple-element.26), channel_id=1, source_target_pairs={{0,1},{8,9},{16,17},{24,25},{2,3},{10,11},{18,19},{26,27},{4,5},{1... | collective-permute-start | bytes 159752 | tf_op jit(solution)/shard_map/ppermute | solution.py:64
  6.7 0.0 collective-permute-start.2
  6.7 1.6 %collective-permute-start.3 = (f32[200,128]{1,0:T(8,128)S(1)}, f32[200,128]{1,0:T(8,128)S(1)}, u32[]{:S(2)}, u32[]{:S(2)}) collective-permute-start(f32[200,128]{1,0:T(8,128)S(1)} %get-tuple-element.28), channel_id=1, source_target_pairs={{0,8},{1,9},{2,10},{3,11},{4,12},{5,13},{6,14},{7,15},{16,24},{17,... | collective-permute-start | bytes 307208 | tf_op jit(solution)/shard_map/ppermute | solution.py:64
  8.3 2.5 %pair_up.1 = (f32[16,96,128]{2,1,0:T(8,128)S(1)}, f32[8,128]{1,0:T(8,128)S(1)}, f32[16,32,128]{2,1,0:T(8,128)S(1)}, bf16[96,128]{1,0:T(8,128)(2,1)S(1)}) custom-call(f32[3,16,16,128]{3,2,1,0:T(8,128)S(1)} %get-tuple-element.29.v.refs_0_.refs_1_, s32[1,1,96]{2,1,0:T(1,128)S(1)} %get-tuple-element.30.tc.refs_2_, ...), custom_call_target="tpu_custom_call" | custom-call | flops 1962934272 | bytes 1048576 | tf_op jit(solution)/shard_map/pair_up/pallas_call | solution.py:68
  10.8 0.0 collective-permute-done.yo.refs_0_.refs_4_.refs_3_
  10.8 0.0 collective-permute-done.1.ye.refs_1_.refs_5_.refs_4_
  10.8 0.5 %beside.1.refs_7_ = f32[8,128]{1,0:T(8,128)S(1)} custom-call(f32[3,16,16,128]{3,2,1,0:T(8,128)S(1)} %get-tuple-element.29.v.refs_0_.refs_1_, s32[1,1,96]{2,1,0:T(1,128)S(1)} %get-tuple-element.30.tc.refs_2_, f32[104,128]{1,0:T(8,128)S(1)} %collective-permute-done.yo.refs_0_.refs_4_.refs_3_, f32[104,128]{1,0:T(8,128)S(1)} %collective-permute-done.1.ye.refs_1_.refs_5_.refs_4_, ...), custom_call_target="tpu_custom_call" | custom-call | flops 490733568 | bytes 1048576 | tf_op jit(solution)/shard_map/beside/pallas_call | solution.py:68
  11.3 0.0 collective-permute-done.2.refs_2_.refs_6_.refs_5_
  11.3 0.0 collective-permute-done.3.refs_3_.refs_7_.refs_6_
  11.3 0.8 %reduce_sums.1 = bf16[8,16,128]{2,1,0:T(8,128)(2,1)} custom-call(f32[104,128]{1,0:T(8,128)S(1)} %collective-permute-done.yo.refs_0_.refs_4_.refs_3_, f32[104,128]{1,0:T(8,128)S(1)} %collective-permute-done.1.ye.refs_1_.refs_5_.refs_4_, f32[200,128]{1,0:T(8,128)S(1)} %collective-permute-done.2.refs_2_.refs_6_.refs_5_, ...), custom_call_target="tpu_custom_call" | custom-call | tf_op jit(solution)/shard_map/reduce_sums/pallas_call | solution.py:68
  12.1 4.7 %all-to-all-start = ((bf16[8,16,128]{2,1,0:T(8,128)(2,1)}), bf16[8,16,128]{2,1,0:T(8,128)(2,1)S(1)}, u32[]{:S(2)}, u32[]{:S(2)}) async-start(bf16[8,16,128]{2,1,0:T(8,128)(2,1)} %reduce_sums.1), calls=%async_computation | async-start | bytes 65536 | tf_op jit(solution)/shard_map/all_to_all | solution.py:564
  16.8 2.1 %edges.1 = (f32[2,16,16,128]{3,2,1,0:T(8,128)S(1)}, f32[2,16,16,128]{3,2,1,0:T(8,128)S(1)}, f32[3,18,16,128]{3,2,1,0:T(8,128)S(1)}, f32[3,2,16,128]{3,2,1,0:T(8,128)S(1)}, f32[3,16,128]{2,1,0:T(8,128)S(1)}) custom-call(f32[3,16,16,128]{3,2,1,0:T(8,128)S(1)} %get-tuple-element.29.v.refs_0_.refs_1_, s32[1,16,384]{2,1,0:T(8,128)S(1)} %get-tuple-element.31.slot.refs_1_, ...), custom_call_target="tpu_custom_call" | custom-call | flops 1962934272 | bytes 1048576 | tf_op jit(solution)/shard_map/edges/pallas_call | solution.py:68
  18.9 4.6 %all-to-all-done.refs_0_ = bf16[8,16,128]{2,1,0:T(8,128)(2,1)S(1)} async-done(((bf16[8,16,128]{2,1,0:T(8,128)(2,1)}), bf16[8,16,128]{2,1,0:T(8,128)(2,1)S(1)}, u32[]{:S(2)}, u32[]{:S(2)}) %all-to-all-start) | async-done | bytes 32800 | tf_op jit(solution)/shard_map/all_to_all | solution.py:564
  23.5 1.5 %advance.1 = f32[3,16,16,128]{3,2,1,0:T(8,128)} custom-call(bf16[8,16,128]{2,1,0:T(8,128)(2,1)S(1)} %all-to-all-done.refs_0_, f32[3,16,16,128]{3,2,1,0:T(8,128)S(1)} %get-tuple-element.29.v.refs_0_.refs_1_, s32[1,1,96]{2,1,0:T(1,128)S(1)} %get-tuple-element.30.tc.refs_2_, f32[104,128]{1,0:T(8,128)S(1)} %collective-permute-done.yo.refs_0_.refs_4_.refs_3_, ...), custom_call_target="tpu_custom_call" | custom-call | tf_op jit(solution)/shard_map/advance/pallas_call | solution.py:68
Async XLA Ops:
  2.1 8.7 %collective-permute-start = (f32[104,128]{1,0:T(8,128)S(1)}, f32[104,128]{1,0:T(8,128)S(1)}, u32[]{:S(2)}, u32[]{:S(2)}) collective-permute-start(f32[104,128]{1,0:T(8,128)S(1)} %get-tuple-element.25), channel_id=1, source_target_pairs={{1,2},{9,10},{17,18},{25,26},{3,4},{11,12},{19,20},{27,28},{5,6},{... | collective-permute-start | bytes 159752 | tf_op jit(solution)/shard_map/ppermute | solution.py:64
  2.7 8.2 %collective-permute-start.1 = (f32[104,128]{1,0:T(8,128)S(1)}, f32[104,128]{1,0:T(8,128)S(1)}, u32[]{:S(2)}, u32[]{:S(2)}) collective-permute-start(f32[104,128]{1,0:T(8,128)S(1)} %get-tuple-element.26), channel_id=1, source_target_pairs={{0,1},{8,9},{16,17},{24,25},{2,3},{10,11},{18,19},{26,27},{4,5},{1... | collective-permute-start | bytes 159752 | tf_op jit(solution)/shard_map/ppermute | solution.py:64
  6.7 4.7 %collective-permute-start.2 = (f32[200,128]{1,0:T(8,128)S(1)}, f32[200,128]{1,0:T(8,128)S(1)}, u32[]{:S(2)}, u32[]{:S(2)}) collective-permute-start(f32[200,128]{1,0:T(8,128)S(1)} %get-tuple-element.27), channel_id=1, source_target_pairs={{8,16},{9,17},{10,18},{11,19},{12,20},{13,21},{14,22},{15,23},{0,1... | collective-permute-start | bytes 307208 | tf_op jit(solution)/shard_map/ppermute | solution.py:64
  6.7 4.6 %collective-permute-start.3 = (f32[200,128]{1,0:T(8,128)S(1)}, f32[200,128]{1,0:T(8,128)S(1)}, u32[]{:S(2)}, u32[]{:S(2)}) collective-permute-start(f32[200,128]{1,0:T(8,128)S(1)} %get-tuple-element.28), channel_id=1, source_target_pairs={{0,8},{1,9},{2,10},{3,11},{4,12},{5,13},{6,14},{7,15},{16,24},{17,... | collective-permute-start | bytes 307208 | tf_op jit(solution)/shard_map/ppermute | solution.py:64
  12.1 11.4 %all-to-all-start = ((bf16[8,16,128]{2,1,0:T(8,128)(2,1)}), bf16[8,16,128]{2,1,0:T(8,128)(2,1)S(1)}, u32[]{:S(2)}, u32[]{:S(2)}) async-start(bf16[8,16,128]{2,1,0:T(8,128)(2,1)} %reduce_sums.1), calls=%async_computation | async-start | bytes 65536 | tf_op jit(solution)/shard_map/all_to_all | solution.py:564
